TPU v7x, 256 devices: a whole 4x4x8 slice. The times are simulated.
256 devices in a mesh: seq: 64 (over z, x, core), head: 4 (over y).
Axes of the slice: x: 4, y: 4, z: 8, core: 2. Of those that a mesh axis runs over, the one named last changes fastest.
Arguments:
- queries: bfloat16 [65536, 2048], P('seq', 'head'), may hold values from -14 to 14, as said below
- key_vectors: bfloat16 [65536, 2048], P('seq', 'head'), may hold values from -6 to 6
- value_vectors: bfloat16 [65536, 2048], P('seq', 'head'), may hold values from -20 to 20, as said below
- cotangent: bfloat16 [65536, 2048], P('seq', 'head'), may hold values from -6 to 6
- norm_gain: float32 [2048], P('head'), may hold values from 0.5 to 2
Outputs:
- mixed: bfloat16 [65536, 2048], P('seq', 'head')
- grad_queries: bfloat16 [65536, 2048], P('seq', 'head')
- grad_keys: bfloat16 [65536, 2048], P('seq', 'head')
- grad_values: bfloat16 [65536, 2048], P('seq', 'head')
Inputs may be any that keep to these rules, and one draw needn't show every extreme that they name: `queries`: real values. `value_vectors`: real values.
All inputs are finite; a program needn't handle non-finite values.
Results may differ from a plain program's by a relative error of at most 0.013.
Values may be sent and summed in bfloat16 or wider, within the bound.
No kernel may reach another device: no remote copies, remote signals or barrier semaphores. Data moves between devices by JAX's collectives and lax.ppermute only.
A program may use at most 128 MiB of HBM per device.

v0:
```python
import jax
import jax.numpy as jnp
from jax import lax
from jax.sharding import PartitionSpec as P

HEAD_DIM = 128
WIDTH = 2048


epsilon = 1e-06


def shards(queries, key_vectors, value_vectors, cotangent, norm_gain):
    tokens_here = queries.shape[0]
    columns = queries.shape[1]
    heads_here = columns // HEAD_DIM
    shaped_q = queries.reshape(tokens_here, heads_here, HEAD_DIM)
    shaped_k = key_vectors.reshape(tokens_here, heads_here, HEAD_DIM)
    shaped_v = value_vectors.reshape(tokens_here, heads_here, HEAD_DIM)
    block_state = jnp.einsum(
        "thd,the->hde", shaped_k, shaped_v, preferred_element_type=jnp.float32
    ).astype(jnp.bfloat16)
    position = lax.axis_index("seq")
    piece = lax.all_gather(block_state[None], "seq", axis=0, tiled=True)
    owners = jnp.arange(piece.shape[0], dtype=jnp.int32)
    select = (owners < position).astype(jnp.bfloat16)
    prefix = jnp.einsum("n,nhde->hde", select, piece, preferred_element_type=jnp.float32)
    prefix_bf = prefix.astype(jnp.bfloat16)
    causal = jnp.arange(tokens_here)[:, None] >= jnp.arange(tokens_here)[None, :]
    head_outputs = []
    head_weights = []
    for head_number in range(heads_here):
        lower = head_number * HEAD_DIM
        query_head = queries[:, lower : lower + HEAD_DIM]
        key_head = key_vectors[:, lower : lower + HEAD_DIM]
        value_head = value_vectors[:, lower : lower + HEAD_DIM]
        scores = jnp.dot(query_head, key_head.T, preferred_element_type=jnp.float32)
        weights = jnp.where(causal, scores, 0.0).astype(jnp.bfloat16)
        output = jnp.dot(weights, value_head, preferred_element_type=jnp.float32)
        output = output + jnp.dot(
            query_head, prefix_bf[head_number], preferred_element_type=jnp.float32
        )
        head_outputs.append(output)
        head_weights.append(weights)
    attn = jnp.concatenate(head_outputs, axis=1)
    upstream = cotangent.astype(jnp.float32) * norm_gain
    squares = jnp.sum(attn * attn, axis=1)
    local_dots = jnp.sum(upstream * attn, axis=1)
    square_total = lax.psum(squares, "head")
    inv = lax.rsqrt(square_total / WIDTH + epsilon)
    mixed = (attn * inv[:, None] * norm_gain).astype(jnp.bfloat16)
    dot_total = lax.psum(local_dots, "head")
    grad_attn = (
        inv[:, None] * (upstream - attn * (inv * inv * dot_total / WIDTH)[:, None])
    ).astype(jnp.bfloat16)
    grad_shaped = grad_attn.reshape(tokens_here, heads_here, HEAD_DIM)
    query_term = jnp.einsum(
        "thd,the->hde", shaped_q, grad_shaped, preferred_element_type=jnp.float32
    ).astype(jnp.bfloat16)
    piece = lax.all_gather(query_term[None], "seq", axis=0, tiled=True)
    owners = jnp.arange(piece.shape[0], dtype=jnp.int32)
    select = (owners > position).astype(jnp.bfloat16)
    suffix = jnp.einsum("n,nhde->hde", select, piece, preferred_element_type=jnp.float32)
    suffix_bf = suffix.astype(jnp.bfloat16)
    grads_q = []
    grads_k = []
    grads_v = []
    for head_number in range(heads_here):
        lower = head_number * HEAD_DIM
        query_head = queries[:, lower : lower + HEAD_DIM]
        key_head = key_vectors[:, lower : lower + HEAD_DIM]
        value_head = value_vectors[:, lower : lower + HEAD_DIM]
        grad_head = grad_attn[:, lower : lower + HEAD_DIM]
        dscores = jnp.dot(grad_head, value_head.T, preferred_element_type=jnp.float32)
        dweights = jnp.where(causal, dscores, 0.0).astype(jnp.bfloat16)
        grad_q = jnp.dot(dweights, key_head, preferred_element_type=jnp.float32)
        grad_q = grad_q + jnp.dot(
            grad_head, prefix_bf[head_number].T, preferred_element_type=jnp.float32
        )
        grad_k = jnp.dot(dweights.T, query_head, preferred_element_type=jnp.float32)
        grad_k = grad_k + jnp.dot(
            value_head, suffix_bf[head_number].T, preferred_element_type=jnp.float32
        )
        grad_v = jnp.dot(head_weights[head_number].T, grad_head, preferred_element_type=jnp.float32)
        grad_v = grad_v + jnp.dot(
            key_head, suffix_bf[head_number], preferred_element_type=jnp.float32
        )
        grads_q.append(grad_q.astype(jnp.bfloat16))
        grads_k.append(grad_k.astype(jnp.bfloat16))
        grads_v.append(grad_v.astype(jnp.bfloat16))
    return (
        mixed,
        jnp.concatenate(grads_q, axis=1),
        jnp.concatenate(grads_k, axis=1),
        jnp.concatenate(grads_v, axis=1),
    )


def solution(mesh):
    return jax.shard_map(
        shards,
        mesh=mesh,
        in_specs=(
            P("seq", "head"),
            P("seq", "head"),
            P("seq", "head"),
            P("seq", "head"),
            P("head"),
        ),
        out_specs=(P("seq", "head"), P("seq", "head"), P("seq", "head"), P("seq", "head")),
        check_vma=False,
    )
```

profile of v0, /device:TPU:57, one launch (start us, length us, event | category | flops | bytes accessed | tf_op | source)
XLA Modules:
  0.0 221.7 jit_solution(6410495051114955417)
XLA Ops:
  7.2 2.3 %copy.32 = bf16[1024,512]{0,1:T(8,128)(2,1)} copy(bf16[1024,512]{1,0:T(8,128)(2,1)} %param.6) | data formatting | bytes 2097152 | tf_op jit(solution)/shard_map/reshape | solution.py:18
  9.6 2.5 %convolution_convert_fusion.1 = bf16[4,128,128]{2,1,0:T(8,128)(2,1)} fusion(bf16[1024,4,128]{0,2,1:T(8,128)(2,1)} %bitcast.153, bf16[1024,512]{1,0:T(8,128)(2,1)S(1)} %copy-done.23), kind=kOutput, calls=%fused_computation.60 | convolution fusion | flops 134283264 | bytes 2228224 | tf_op jit(solution)/shard_map/thd,the->hde/dot_general | solution.py:20
  12.1 1.5 copy.19
  13.6 0.7 select_convert_fusion.5
  14.4 0.8 select_convert_fusion.6
  15.2 0.8 select_convert_fusion.7
  15.9 0.8 select_convert_fusion.4
  16.7 1.1 copy-done.24
  17.9 0.8 fusion.63
  18.7 1.6 fusion.75
  20.3 0.8 fusion.87
  21.2 0.8 fusion.51
  22.0 75.6 %all-gather.5.cloned.1.call-done = bf16[256,128,128]{2,1,0:T(8,128)(2,1)} async-done(((bf16[4,128,128]{2,1,0:T(8,128)(2,1)}), bf16[256,128,128]{2,1,0:T(8,128)(2,1)}) %all-gather.5.cloned.1.call-update) | async-done | bytes 8388624 | tf_op jit(solution)/shard_map/all_gather | solution.py:24
  97.6 8.1 %fusion.2 = f32[1,4,128,128]{3,0,2,1:T(1,128)S(1)} fusion(bf16[64,4,128,128]{3,2,1,0:T(8,128)(2,1)} %bitcast.150, s32[]{:T(128)S(6)} %axis_index.15), kind=kOutput, calls=%fused_computation.2 | convolution fusion | flops 8388672 | bytes 8650756 | tf_op jit(solution)/shard_map/n,nhde->hde/dot_general | solution.py:27
  105.9 0.8 copy-done.34
  108.3 5.8 %all-reduce = (f32[1024]{0:T(1024)S(1)}, f32[1024]{0:T(1024)S(1)}) all-reduce(f32[1024]{0:T(1024)S(1)} %get-tuple-element.13, f32[1024]{0:T(1024)S(1)} %get-tuple-element.12), channel_id=1, replica_groups=mesh['seq'=64,'head'=4] {'head'}, use_global_device_ids=true, to_apply=%region_1.2 | all-reduce | flops 2048 | bytes 16384 | tf_op jit(solution)/shard_map/psum | solution.py:49
  114.1 2.9 %multiply_convert_fusion = (bf16[1024,512]{0,1:T(8,128)(2,1)S(1)}, bf16[1024,512]{0,1:T(8,128)(2,1)}) fusion(bf16[1024,512]{0,1:T(8,128)(2,1)S(1)} %copy.19, f32[1024]{0:T(1024)S(1)} %get-tuple-element.18, f32[512]{0:T(512)S(1)} %copy-done.35, f32[1024]{0:T(1024)S(1)} %get-tuple-element.19, f32[1024,128]{0,1:T(8,128)} %copy-done.17, ...), kind=kLoop, calls=%fused_computation.14 | loop fusion | flops 6291456 | bytes 5253120 | tf_op jit(solution)/shard_map/convert_element_type | solution.py:55
  117.5 0.8 copy.21
  118.2 1.3 copy.22
  119.6 1.8 select_convert_fusion
  121.4 0.8 fusion.54
  122.6 0.8 select_convert_fusion.1
  123.5 0.8 fusion.66
  124.5 0.8 select_convert_fusion.2
  125.3 0.8 fusion.78
  126.4 0.8 select_convert_fusion.3
  127.2 0.8 fusion.90
  128.1 0.5 copy-done.4
  128.7 1.0 pad_maximum_fusion.1
  129.8 2.3 %copy.23 = bf16[1024,512]{1,0:T(8,128)(2,1)} copy(bf16[1024,512]{0,1:T(8,128)(2,1)} %pad_maximum_fusion.1) | data formatting | bytes 2097152
  132.1 3.0 %fusion.46 = f32[1024,128]{0,1:T(8,128)} fusion(bf16[1024,1024]{1,0:T(8,128)(2,1)} %copy-done.15, bf16[1024,512]{0,1:T(8,128)(2,1)S(1)} %get-tuple-element.16), kind=kOutput, calls=%fused_computation.82 | convolution fusion | flops 268435456 | bytes 2883584 | tf_op jit(solution)/shard_map/dot_general | solution.py:84
  135.1 1.3 fusion.42
  136.3 0.5 copy-done.10
  136.9 1.2 fusion.38
  138.1 0.6 copy-done.12
  138.6 1.2 fusion.34
  139.9 1.3 fusion.57
  141.2 0.5 copy-done.1
  141.7 0.5 fusion.69
  142.2 1.1 copy-done.3
  143.3 1.3 fusion.81
  145.1 1.3 fusion.93
  146.3 54.4 %all-gather.7.cloned.1.call-done = bf16[256,128,128]{2,1,0:T(8,128)(2,1)} async-done(((bf16[4,128,128]{2,1,0:T(8,128)(2,1)}), bf16[256,128,128]{2,1,0:T(8,128)(2,1)}) %all-gather.7.cloned.1.call-update) | async-done | bytes 8388624 | tf_op jit(solution)/shard_map/all_gather | solution.py:60
  200.8 8.1 %fusion = f32[1,4,128,128]{3,0,2,1:T(1,128)S(1)} fusion(bf16[64,4,128,128]{3,2,1,0:T(8,128)(2,1)} %bitcast.149, s32[]{:T(128)S(6)} %axis_index.15), kind=kOutput, calls=%fused_computation | convolution fusion | flops 8388672 | bytes 8650756 | tf_op jit(solution)/shard_map/n,nhde->hde/dot_general | solution.py:63
  209.4 0.5 copy-done.31
  210.5 1.3 copy.25
  212.4 0.6 copy-done.28
  213.5 1.3 copy.24
  (90 shorter events, 6.1 us)
Async XLA Ops:
  7.2 2.4 %copy-start.23 = (bf16[1024,512]{1,0:T(8,128)(2,1)S(1)}, bf16[1024,512]{1,0:T(8,128)(2,1)}, u32[]{:S(2)}) copy-start(bf16[1024,512]{1,0:T(8,128)(2,1)} %param.7) | copy-start | bytes 3145732
  7.2 90.4 %all-gather.5.cloned.1.call-start = ((), (), s32[]{:S(2)}) async-start(), calls=%async_computation | async-start | bytes 8519680 | tf_op jit(solution)/shard_map/all_gather | solution.py:24
  9.6 4.0 %copy-start.6 = (bf16[1024,512]{1,0:T(8,128)(2,1)S(1)}, bf16[1024,512]{1,0:T(8,128)(2,1)}, u32[]{:S(2)}) copy-start(bf16[1024,512]{1,0:T(8,128)(2,1)} %param.6) | copy-start | bytes 3145732
  9.6 4.0 %copy-start.19 = (bf16[1024,512]{1,0:T(8,128)(2,1)S(1)}, bf16[1024,512]{1,0:T(8,128)(2,1)}, u32[]{:S(2)}) copy-start(bf16[1024,512]{1,0:T(8,128)(2,1)} %param.5) | copy-start | bytes 3145732
  12.1 188.7 %all-gather.7.cloned.1.call-start = ((), (), s32[]{:S(2)}) async-start(), calls=%async_computation.1 | async-start | bytes 8519680 | tf_op jit(solution)/shard_map/all_gather | solution.py:60
  14.4 2.3 %copy-start.9 = (bf16[1024,1024]{1,0:T(8,128)(2,1)}, bf16[1024,1024]{1,0:T(8,128)(2,1)S(1)}, u32[]{:S(2)}) copy-start(bf16[1024,1024]{1,0:T(8,128)(2,1)S(1)} %select_convert_fusion.5) | copy-start | bytes 6291460
  15.2 3.5 %copy-start.13 = (bf16[1024,1024]{1,0:T(8,128)(2,1)}, bf16[1024,1024]{1,0:T(8,128)(2,1)S(1)}, u32[]{:S(2)}) copy-start(bf16[1024,1024]{1,0:T(8,128)(2,1)S(1)} %select_convert_fusion.6) | copy-start | bytes 6291460
  15.9 4.4 %copy-start.15 = (bf16[1024,1024]{1,0:T(8,128)(2,1)}, bf16[1024,1024]{1,0:T(8,128)(2,1)S(1)}, u32[]{:S(2)}) copy-start(bf16[1024,1024]{1,0:T(8,128)(2,1)S(1)} %select_convert_fusion.7) | copy-start | bytes 6291460
  15.9 1.9 copy-start.24
  17.9 3.3 %copy-start.11 = (bf16[1024,1024]{1,0:T(8,128)(2,1)}, bf16[1024,1024]{1,0:T(8,128)(2,1)S(1)}, u32[]{:S(2)}) copy-start(bf16[1024,1024]{1,0:T(8,128)(2,1)S(1)} %select_convert_fusion.4) | copy-start | bytes 6291460
  97.6 8.1 %copy-start.20 = (bf16[1024,512]{1,0:T(8,128)(2,1)S(1)}, bf16[1024,512]{1,0:T(8,128)(2,1)}, u32[]{:S(2)}) copy-start(bf16[1024,512]{1,0:T(8,128)(2,1)} %param.5) | copy-start | bytes 3145732
  105.6 1.0 copy-start.34
  106.7 0.8 copy-start.35
  107.2 0.8 copy-start.16
  107.5 0.8 copy-start.17
  114.1 2.9 %copy-start.21 = (bf16[1024,512]{1,0:T(8,128)(2,1)S(1)}, bf16[1024,512]{1,0:T(8,128)(2,1)}, u32[]{:S(2)}) copy-start(bf16[1024,512]{1,0:T(8,128)(2,1)} %param.5) | copy-start | bytes 3145732
  117.0 1.2 copy-start.18
  119.6 1.8 copy-start.7
  121.4 1.2 copy-start.25
  123.5 1.9 copy-start
  125.3 1.9 copy-start.2
  127.2 1.3 copy-start.4
  132.1 3.0 %copy-start.14 = (bf16[1024,1024]{1,0:T(8,128)(2,1)S(1)}, bf16[1024,1024]{1,0:T(8,128)(2,1)}, u32[]{:S(2)}) copy-start(bf16[1024,1024]{1,0:T(8,128)(2,1)} %copy-done.13) | copy-start | bytes 6291460
  135.1 1.8 copy-start.10
  136.9 1.8 copy-start.12
  138.6 1.2 copy-start.22
  139.9 1.8 copy-start.1
  141.7 1.6 copy-start.3
  143.3 1.8 copy-start.5
  200.8 8.2 %copy-start.8 = (bf16[1024,512]{1,0:T(8,128)(2,1)S(1)}, bf16[1024,512]{1,0:T(8,128)(2,1)}, u32[]{:S(2)}) copy-start(bf16[1024,512]{1,0:T(8,128)(2,1)} %param.6) | copy-start | bytes 3145732
  200.8 8.2 %copy-start.33 = (f32[1024,128]{0,1:T(8,128)S(1)}, f32[1024,128]{0,1:T(8,128)}, u32[]{:S(2)}) copy-start(f32[1024,128]{0,1:T(8,128)} %fusion.34) | copy-start | bytes 1572868
  200.8 8.4 %copy-start.32 = (f32[1024,128]{0,1:T(8,128)S(1)}, f32[1024,128]{0,1:T(8,128)}, u32[]{:S(2)}) copy-start(f32[1024,128]{0,1:T(8,128)} %fusion.38) | copy-start | bytes 1572868
  208.9 1.0 copy-start.31
  208.9 1.3 copy-start.30
  210.4 1.4 copy-start.26
  210.5 1.5 copy-start.27
  211.9 1.0 copy-start.28
  211.9 1.3 copy-start.29
Sparse Core Ops, SparseCore 0:
  12.2 85.3 all-gather.4
  118.4 82.3 all-gather.6
where the time goes:
time: 224 us; the launch traced here: 222 us
  waiting for transfers between devices  130 us (58%)
  matrix products  48.6 us (22%)
  local copies, waits for them, and re-layouts  18.1 us (8%)
  between operations  14.6 us (7%)
  blocking collectives  5.83 us (3%)
  other arithmetic  4.56 us (2%)
    all_gather x1, waiting for transfers between devices, shards(): piece = lax.all_gather(block_state[None], 'seq', axis=0, tiled=True)  75.6 us
    all_gather x1, waiting for transfers between devices, shards(): piece = lax.all_gather(query_term[None], 'seq', axis=0, tiled=True)  54.4 us
    dot_general x2, matrix products, shards(): jnp.einsum('n,nhde->hde', select, piece, preferred_element_type=jnp.float32)  16.2 us
    unnamed x77, local copies, waits for them, and re-layouts  14.9 us
    dot_general x4, matrix products, shards(): jnp.dot(head_weights[head_number].T, grad_head, preferred_element_type=jn...  6.73 us
    psum x1, blocking collectives, shards(): square_total = lax.psum(squares, 'head')  5.83 us
  transfers between devices with their start and end apart: 2, of which 2 were waited for; matrix products, arithmetic and copies ran while one was open for 15% of the time, Pallas kernels for 0%

commit v1 on v0

v1 whole, which is shorter than its diff:
```python
import jax
import jax.numpy as jnp
from jax import lax
from jax.experimental import pallas as pl
from jax.experimental.pallas import tpu as pltpu
from jax.sharding import PartitionSpec as P

HEAD_DIM = 128
WIDTH = 2048
epsilon = 1e-06
ROWS = 256

f32 = jnp.float32
bf16 = jnp.bfloat16


def nn(a, b):
    return lax.dot_general(a, b, (((1,), (0,)), ((), ())), preferred_element_type=f32)


def nt(a, b):
    return lax.dot_general(a, b, (((1,), (1,)), ((), ())), preferred_element_type=f32)


def tn(a, b):
    return lax.dot_general(a, b, (((0,), (0,)), ((), ())), preferred_element_type=f32)


def params(mib=24):
    return pltpu.CompilerParams(vmem_limit_bytes=mib << 20)


def cost(flops, nbytes):
    return pl.CostEstimate(flops=flops, bytes_accessed=nbytes, transcendentals=0)


def outer_kernel(a_ref, b_ref, s_ref, acc_ref):
    step = pl.program_id(0)

    @pl.when(step == 0)
    def _():
        acc_ref[...] = jnp.zeros_like(acc_ref)

    pairs = acc_ref.shape[0]
    for p in range(pairs):
        cols = slice(p * 256, p * 256 + 256)
        acc_ref[p] += tn(a_ref[:, cols], b_ref[:, cols])

    @pl.when(step == pl.num_programs(0) - 1)
    def _():
        for p in range(pairs):
            s_ref[2 * p] = acc_ref[p, :128, :128].astype(bf16)
            s_ref[2 * p + 1] = acc_ref[p, 128:, 128:].astype(bf16)


def block_state(a, b):
    t, c = a.shape
    heads = c // HEAD_DIM
    spec = pl.BlockSpec((ROWS, c), lambda i: (i, 0))
    return pl.pallas_call(
        outer_kernel,
        grid=(t // ROWS,),
        in_specs=[spec, spec],
        out_specs=pl.BlockSpec((heads, 128, 128), lambda i: (0, 0, 0)),
        out_shape=jax.ShapeDtypeStruct((heads, 128, 128), bf16),
        scratch_shapes=[pltpu.VMEM((heads // 2, 256, 256), f32)],
        compiler_params=params(8),
        cost_estimate=cost(2 * t * c * 256, 2 * t * c * 2),
        name="block_state",
    )(a, b)


def masked(x, r, c0, upper=False):
    row = lax.broadcasted_iota(jnp.int32, x.shape, 0) + r
    col = lax.broadcasted_iota(jnp.int32, x.shape, 1) + c0
    keep = (row <= col) if upper else (row >= col)
    return jnp.where(keep, x, 0.0).astype(bf16)


def local_kernel(q_ref, k_ref, v_ref, o_ref):
    t, c = q_ref.shape
    for h in range(c // HEAD_DIM):
        cols = slice(h * HEAD_DIM, (h + 1) * HEAD_DIM)
        for r in range(0, t, ROWS):
            q = q_ref[r : r + ROWS, cols]
            w = masked(nt(q, k_ref[r : r + ROWS, cols]), 0, 0)
            o = nn(w, v_ref[r : r + ROWS, cols])
            if r:
                w = nt(q, k_ref[:r, cols]).astype(bf16)
                o = o + nn(w, v_ref[:r, cols])
            o_ref[r : r + ROWS, cols] = o


def local_attn(q, k, v, part, parts):
    t, c = q.shape
    w = c // parts
    spec = pl.BlockSpec((t, w), lambda i: (0, part))
    return pl.pallas_call(
        local_kernel,
        grid=(1,),
        in_specs=[spec] * 3,
        out_specs=pl.BlockSpec((t, w), lambda i: (0, 0)),
        out_shape=jax.ShapeDtypeStruct((t, w), f32),
        compiler_params=params(24),
        cost_estimate=cost(2 * 2 * t * t * w * 5 // 8, t * w * 10),
        name="local_attn",
    )(q, k, v)


def row_sums(x):
    acc = x[:, :128]
    for g in range(1, x.shape[1] // 128):
        acc = acc + x[:, g * 128 : (g + 1) * 128]
    return jnp.sum(acc.T, axis=0, keepdims=True)


def column(row):
    return jnp.broadcast_to(row, (128, row.shape[1])).T


def attn_kernel(*refs):
    n = len(refs) - 6
    o_refs = refs[:n]
    q_ref, p_ref, y_ref, g_ref, attn_ref, stat_ref = refs[n:]
    w = o_refs[0].shape[1]
    for h in range(q_ref.shape[1] // HEAD_DIM):
        cols = slice(h * HEAD_DIM, (h + 1) * HEAD_DIM)
        at = h * HEAD_DIM
        own = o_refs[at // w][:, at % w : at % w + HEAD_DIM]
        attn_ref[:, cols] = own + nn(q_ref[:, cols], p_ref[h])
    attn = attn_ref[...]
    up = y_ref[...].astype(f32) * g_ref[...]
    stat_ref[0:1, :] = row_sums(attn * attn)
    stat_ref[1:2, :] = row_sums(up * attn)


def attn_stats(locals_, q, prefix, y, gain):
    t, c = q.shape
    w = locals_[0].shape[1]
    wide = pl.BlockSpec((ROWS, c), lambda i: (i, 0))
    return pl.pallas_call(
        attn_kernel,
        grid=(t // ROWS,),
        in_specs=[pl.BlockSpec((ROWS, w), lambda i: (i, 0))] * len(locals_)
        + [
            wide,
            pl.BlockSpec(prefix.shape, lambda i: (0, 0, 0)),
            wide,
            pl.BlockSpec((1, c), lambda i: (0, 0)),
        ],
        out_specs=(wide, pl.BlockSpec((2, ROWS), lambda i: (0, i))),
        out_shape=(jax.ShapeDtypeStruct((t, c), f32), jax.ShapeDtypeStruct((2, t), f32)),
        compiler_params=params(12),
        cost_estimate=cost(2 * t * c * 128, t * c * 12),
        name="attn_stats",
    )(*locals_, q, prefix, y, gain)


def grad_kernel(attn_ref, y_ref, q_ref, stat_ref, g_ref, mixed_ref, d_ref, term_ref, acc_ref):
    step = pl.program_id(0)

    @pl.when(step == 0)
    def _():
        acc_ref[...] = jnp.zeros_like(acc_ref)

    inv_row = lax.rsqrt(stat_ref[0:1, :] / WIDTH + epsilon)
    scale_row = inv_row * inv_row * stat_ref[1:2, :] / WIDTH
    inv = column(inv_row)
    scale = column(scale_row)
    for h in range(q_ref.shape[1] // HEAD_DIM):
        cols = slice(h * HEAD_DIM, (h + 1) * HEAD_DIM)
        attn = attn_ref[:, cols]
        gain = g_ref[:, cols]
        mixed_ref[:, cols] = (attn * inv * gain).astype(bf16)
        up = y_ref[:, cols].astype(f32) * gain
        d_ref[:, cols] = (inv * (up - attn * scale)).astype(bf16)
    pairs = acc_ref.shape[0]
    for p in range(pairs):
        cols = slice(p * 256, p * 256 + 256)
        acc_ref[p] += tn(q_ref[:, cols], d_ref[:, cols])

    @pl.when(step == pl.num_programs(0) - 1)
    def _():
        for p in range(pairs):
            term_ref[2 * p] = acc_ref[p, :128, :128].astype(bf16)
            term_ref[2 * p + 1] = acc_ref[p, 128:, 128:].astype(bf16)


def grads_of_norm(attn, y, q, stats, gain):
    t, c = q.shape
    heads = c // HEAD_DIM
    wide = pl.BlockSpec((ROWS, c), lambda i: (i, 0))
    return pl.pallas_call(
        grad_kernel,
        grid=(t // ROWS,),
        in_specs=[
            wide,
            wide,
            wide,
            pl.BlockSpec((2, ROWS), lambda i: (0, i)),
            pl.BlockSpec((1, c), lambda i: (0, 0)),
        ],
        out_specs=(wide, wide, pl.BlockSpec((heads, 128, 128), lambda i: (0, 0, 0))),
        out_shape=(
            jax.ShapeDtypeStruct((t, c), bf16),
            jax.ShapeDtypeStruct((t, c), bf16),
            jax.ShapeDtypeStruct((heads, 128, 128), bf16),
        ),
        scratch_shapes=[pltpu.VMEM((heads // 2, 256, 256), f32)],
        compiler_params=params(12),
        cost_estimate=cost(2 * t * c * 256, t * c * 12),
        name="grads_of_norm",
    )(attn, y, q, stats, gain)


def back_kernel(q_ref, k_ref, v_ref, d_ref, p_ref, dq_ref, dk_ref, dv_ref):
    t, c = q_ref.shape
    for h in range(c // HEAD_DIM):
        cols = slice(h * HEAD_DIM, (h + 1) * HEAD_DIM)
        for r in range(0, t, ROWS):
            here = slice(r, r + ROWS)
            q, k, v, d = q_ref[here, cols], k_ref[here, cols], v_ref[here, cols], d_ref[here, cols]
            dq = nt(d, p_ref[h]) + nn(masked(nt(d, v), 0, 0), k)
            if r:
                dq = dq + nn(nt(d, v_ref[:r, cols]).astype(bf16), k_ref[:r, cols])
            dq_ref[here, cols] = dq.astype(bf16)
            dk = nn(masked(nt(v, d), 0, 0, True), q)
            dv = nn(masked(nt(k, q), 0, 0, True), d)
            e = r + ROWS
            if e < t:
                dk = dk + nn(nt(v, d_ref[e:, cols]).astype(bf16), q_ref[e:, cols])
                dv = dv + nn(nt(k, q_ref[e:, cols]).astype(bf16), d_ref[e:, cols])
            dk_ref[here, cols] = dk
            dv_ref[here, cols] = dv


def local_back(q, k, v, d, prefix, part, parts):
    t, c = q.shape
    w = c // parts
    spec = pl.BlockSpec((t, w), lambda i: (0, part))
    out = pl.BlockSpec((t, w), lambda i: (0, 0))
    return pl.pallas_call(
        back_kernel,
        grid=(1,),
        in_specs=[spec] * 4 + [pl.BlockSpec((w // 128, 128, 128), lambda i: (part, 0, 0))],
        out_specs=(out,) * 3,
        out_shape=(
            jax.ShapeDtypeStruct((t, w), bf16),
            jax.ShapeDtypeStruct((t, w), f32),
            jax.ShapeDtypeStruct((t, w), f32),
        ),
        compiler_params=params(24),
        cost_estimate=cost(6 * 2 * t * t * w * 5 // 8, t * w * 18),
        name="local_back",
    )(q, k, v, d, prefix)


def final_kernel(*refs):
    n = (len(refs) - 5) // 2
    dk_refs, dv_refs = refs[:n], refs[n : 2 * n]
    k_ref, v_ref, s_ref, ok_ref, ov_ref = refs[2 * n :]
    w = dk_refs[0].shape[1]
    for h in range(k_ref.shape[1] // HEAD_DIM):
        cols = slice(h * HEAD_DIM, (h + 1) * HEAD_DIM)
        at = h * HEAD_DIM
        part = slice(at % w, at % w + HEAD_DIM)
        ok_ref[:, cols] = (dk_refs[at // w][:, part] + nt(v_ref[:, cols], s_ref[h])).astype(bf16)
        ov_ref[:, cols] = (dv_refs[at // w][:, part] + nn(k_ref[:, cols], s_ref[h])).astype(bf16)


def finish(dks, dvs, k, v, suffix):
    t, c = k.shape
    w = dks[0].shape[1]
    wide = pl.BlockSpec((ROWS, c), lambda i: (i, 0))
    return pl.pallas_call(
        final_kernel,
        grid=(t // ROWS,),
        in_specs=[pl.BlockSpec((ROWS, w), lambda i: (i, 0))] * (2 * len(dks))
        + [wide, wide, pl.BlockSpec(suffix.shape, lambda i: (0, 0, 0))],
        out_specs=(wide, wide),
        out_shape=(jax.ShapeDtypeStruct((t, c), bf16),) * 2,
        compiler_params=params(16),
        cost_estimate=cost(4 * t * c * 128, t * c * 16),
        name="finish",
    )(*dks, *dvs, k, v, suffix)


NZ, NX = 8, 4


def step_pairs(reverse, dz=0, dx=0, swap=False):
    pairs = []
    for i in range(NZ * NX * 2):
        z, x, c = i // 8, (i // 2) % 4, i % 2
        z2 = z + dz
        if not 0 <= z2 < NZ:
            continue
        j = (z2 * NX + (x + dx) % NX) * 2 + (1 - c if swap else c)
        pairs.append((63 - i, 63 - j) if reverse else (i, j))
    return pairs


def exclusive_sum(own, reverse):
    def send(a, **step):
        return lax.ppermute(a, "seq", step_pairs(reverse, **step))

    index = lax.axis_index("seq")
    index = 63 - index if reverse else index
    x, c = (index // 2) % 4, index % 2
    first = c == 0
    n = own.shape[0] // 2
    mine = jnp.where(first, own[:n], own[n:])
    other = jnp.where(first, own[n:], own[:n])
    got = send(other, swap=True)
    chip = (mine.astype(f32) + got.astype(f32)).astype(bf16)
    row = chip.astype(f32)
    before = jnp.zeros_like(row)
    for k in (2, 1, 3):
        r = send(chip, dx=k).astype(f32)
        row = row + r
        before = before + jnp.where(x >= k, r, 0.0)
    plane = row.astype(bf16)
    near = send(plane, dz=2).astype(f32) + send(plane, dz=1).astype(f32)
    three = (row + near).astype(bf16)
    far = send(three, dz=3).astype(f32) + send(three, dz=6).astype(f32)
    e0 = before + near + far
    e1 = e0 + jnp.where(first, mine, got).astype(f32)
    e0, e1 = e0.astype(bf16), e1.astype(bf16)
    keep = jnp.where(first, e0, e1)
    back = send(jnp.where(first, e1, e0), swap=True)
    return jnp.where(first, jnp.concatenate([keep, back]), jnp.concatenate([back, keep]))


def head_sum(a):
    r = [lax.ppermute(a, "head", [(i, (i + k) % 4) for i in range(4)]) for k in (2, 1, 3)]
    return a + r[0] + r[1] + r[2]


FWD, BWD = 2, 4


def shards(q, k, v, y, gain):
    gain = gain[None, :]
    prefix = exclusive_sum(block_state(k, v), False)
    locals_ = [local_attn(q, k, v, i, FWD) for i in range(FWD)]
    attn, stats = attn_stats(locals_, q, prefix, y, gain)
    stats = head_sum(stats)
    mixed, d, term = grads_of_norm(attn, y, q, stats, gain)
    suffix = exclusive_sum(term, True)
    parts = [local_back(q, k, v, d, prefix, i, BWD) for i in range(BWD)]
    dk, dv = finish([p[1] for p in parts], [p[2] for p in parts], k, v, suffix)
    return mixed, jnp.concatenate([p[0] for p in parts], axis=1), dk, dv


def solution(mesh):
    wide = P("seq", "head")
    return jax.shard_map(
        shards,
        mesh=mesh,
        in_specs=(wide, wide, wide, wide, P("head")),
        out_specs=(wide, wide, wide, wide),
        check_vma=False,
    )
```

time: 224 us -> 101 us (0.45)
  waiting for transfers between devices: 130 us -> 17.1 us
  matrix products: 48.6 us -> 0 us
  starting transfers between devices: 0.08 us -> 47.6 us
  Pallas kernels: 0 us -> 25 us
  between operations: 14.6 us -> 0.95 us
  local copies, waits for them, and re-layouts: 18.1 us -> 6.63 us
  blocking collectives: 5.83 us -> 0 us
    all_gather x2 -> x0, waiting for transfers between devices: 130 us -> none  [the longest x1 75.6 us: shards(): piece = lax.all_gather(block_state[None], 'seq', axis=0, tiled=True)]
    dot_general x44 -> x0, matrix products: 48.6 us -> none  [the longest x2 16.2 us: shards(): jnp.einsum('n,nhde->hde', select, piece, preferred_element_type=jnp.float32)]
    ppermute x0 -> x21, starting transfers between devices: none -> 47.6 us  [the longest x18 44.9 us: send(): return lax.ppermute(a, 'seq', step_pairs(reverse, **step))]
    pallas_call x0 -> x10, Pallas kernels: none -> 25 us  [the longest x4 12.9 us: local_back(): pl.pallas_call(back_kernel, grid=(1,), in_specs=[spec] * 4 + [pl.BlockSpe...]
    ppermute x0 -> x21, waiting for transfers between devices: none -> 17.1 us  [the longest x18 13.1 us: send(): return lax.ppermute(a, 'seq', step_pairs(reverse, **step))]
    unnamed x77 -> x24, local copies, waits for them, and re-layouts: 14.9 us -> 6.63 us
    psum x1 -> x0, blocking collectives: 5.83 us -> none  [shards(): square_total = lax.psum(squares, 'head')]
    reshape x1 -> x0, local copies, waits for them, and re-layouts: 2.35 us -> none  [shards(): shaped_k = key_vectors.reshape(tokens_here, heads_here, HEAD_DIM)]
  transfers between devices with their start and end apart: 2 -> 21, of which waited for: 2 -> 11; matrix products, arithmetic and copies ran while one was open for 15% -> 1% of each run, Pallas kernels for 0% -> 17%
where the time goes in v1:
time: 101 us; the launch traced here: 100 us
  starting transfers between devices  47.6 us (47%)
  Pallas kernels  25 us (25%)
  waiting for transfers between devices  17.1 us (17%)
  local copies, waits for them, and re-layouts  6.63 us (7%)
  other arithmetic  3.26 us (3%)
    ppermute x18, starting transfers between devices, send(): return lax.ppermute(a, 'seq', step_pairs(reverse, **step))  44.9 us
    ppermute x18, waiting for transfers between devices, send(): return lax.ppermute(a, 'seq', step_pairs(reverse, **step))  13.1 us
    pallas_call x4, Pallas kernels, local_back(): pl.pallas_call(back_kernel, grid=(1,), in_specs=[spec] * 4 + [pl.BlockSpe...  12.9 us
    unnamed x24, local copies, waits for them, and re-layouts  6.63 us
    pallas_call x2, Pallas kernels, local_attn(): pl.pallas_call(local_kernel, grid=(1,), in_specs=[spec] * 3, out_specs=pl...  4.08 us
    ppermute x3, waiting for transfers between devices, head_sum(): lax.ppermute(a, 'head', [(i, (i + k) % 4) for i in range(4)])  4 us
    pallas_call x1, Pallas kernels, grads_of_norm(): pl.pallas_call(grad_kernel, grid=(t // ROWS,), in_specs=[wide, wide, wide...  2.84 us
    ppermute x3, starting transfers between devices, head_sum(): lax.ppermute(a, 'head', [(i, (i + k) % 4) for i in range(4)])  2.68 us
  transfers between devices with their start and end apart: 21, of which 11 were waited for; matrix products, arithmetic and copies ran while one was open for 1% of the time, Pallas kernels for 17%

profile of v1, /device:TPU:57, one launch (start us, length us, event | category | flops | bytes accessed | tf_op | source)
XLA Modules:
  0.0 100.5 jit_solution(6177774430681590613)
XLA Ops:
  0.7 1.2 %copy-done = bf16[1024,512]{1,0:T(8,128)(2,1)S(1)} copy-done((bf16[1024,512]{1,0:T(8,128)(2,1)S(1)}, bf16[1024,512]{1,0:T(8,128)(2,1)}, u32[]{:S(2)}) %copy-start) | copy-done | bytes 1048600
  1.9 1.2 %copy-done.2 = bf16[1024,512]{1,0:T(8,128)(2,1)S(1)} copy-done((bf16[1024,512]{1,0:T(8,128)(2,1)S(1)}, bf16[1024,512]{1,0:T(8,128)(2,1)}, u32[]{:S(2)}) %copy-start.2) | copy-done | bytes 1048600
  3.1 1.2 %block_state.1 = bf16[4,128,128]{2,1,0:T(8,128)(2,1)S(1)} custom-call(bf16[1024,512]{1,0:T(8,128)(2,1)S(1)} %copy-done, bf16[1024,512]{1,0:T(8,128)(2,1)S(1)} %copy-done.2), custom_call_target="tpu_custom_call" | custom-call | flops 268435456 | bytes 2097152 | tf_op jit(solution)/shard_map/block_state/pallas_call | solution.py:60
  4.3 0.8 collective-permute-start
  5.1 0.9 collective-permute-done
  6.0 2.6 %collective-permute-start.3 = (bf16[2,128,128]{2,1,0:T(8,128)(2,1)S(1)}, bf16[2,128,128]{2,1,0:T(8,128)(2,1)S(1)}, u32[]{:S(2)}, u32[]{:S(2)}) collective-permute-start(bf16[2,128,128]{2,1,0:T(8,128)(2,1)S(1)} %add_convert_fusion.5), channel_id=1, source_target_pairs={{0,24},{4,28},{8,0},{12,4},{16,8},{20,12},{24,16},{28,20},{32,56},... | collective-permute-start | bytes 196616 | tf_op jit(solution)/shard_map/ppermute | solution.py:305
  8.5 1.7 %collective-permute-start.1 = (bf16[2,128,128]{2,1,0:T(8,128)(2,1)S(1)}, bf16[2,128,128]{2,1,0:T(8,128)(2,1)S(1)}, u32[]{:S(2)}, u32[]{:S(2)}) collective-permute-start(bf16[2,128,128]{2,1,0:T(8,128)(2,1)S(1)} %add_convert_fusion.5), channel_id=1, source_target_pairs={{0,16},{4,20},{8,24},{12,28},{16,0},{20,4},{24,8},{28,12},{32,48},... | collective-permute-start | bytes 196616 | tf_op jit(solution)/shard_map/ppermute | solution.py:305
  10.3 3.0 %collective-permute-done.2 = bf16[2,128,128]{2,1,0:T(8,128)(2,1)S(1)} collective-permute-done((bf16[2,128,128]{2,1,0:T(8,128)(2,1)S(1)}, bf16[2,128,128]{2,1,0:T(8,128)(2,1)S(1)}, u32[]{:S(2)}, u32[]{:S(2)}) %collective-permute-start.2) | collective-permute-done | bytes 65568 | tf_op jit(solution)/shard_map/ppermute | solution.py:305
  13.3 0.9 collective-permute-done.1
  14.2 3.5 %collective-permute-start.5 = (bf16[2,128,128]{2,1,0:T(8,128)(2,1)S(1)}, bf16[2,128,128]{2,1,0:T(8,128)(2,1)S(1)}, u32[]{:S(2)}, u32[]{:S(2)}) collective-permute-start(bf16[2,128,128]{2,1,0:T(8,128)(2,1)S(1)} %fusion.8), channel_id=1, source_target_pairs={{0,32},{4,36},{8,40},{12,44},{16,48},{20,52},{24,56},{28,60},{32,6... | collective-permute-start | bytes 196616 | tf_op jit(solution)/shard_map/ppermute | solution.py:305
  17.8 6.1 %collective-permute-start.4 = (bf16[2,128,128]{2,1,0:T(8,128)(2,1)S(1)}, bf16[2,128,128]{2,1,0:T(8,128)(2,1)S(1)}, u32[]{:S(2)}, u32[]{:S(2)}) collective-permute-start(bf16[2,128,128]{2,1,0:T(8,128)(2,1)S(1)} %fusion.8), channel_id=1, source_target_pairs={{0,64},{4,68},{8,72},{12,76},{16,80},{20,84},{24,88},{28,92},{32,9... | collective-permute-start | bytes 196616 | tf_op jit(solution)/shard_map/ppermute | solution.py:305
  23.9 1.3 %collective-permute-done.4 = bf16[2,128,128]{2,1,0:T(8,128)(2,1)S(1)} collective-permute-done((bf16[2,128,128]{2,1,0:T(8,128)(2,1)S(1)}, bf16[2,128,128]{2,1,0:T(8,128)(2,1)S(1)}, u32[]{:S(2)}, u32[]{:S(2)}) %collective-permute-start.4) | collective-permute-done | bytes 65568 | tf_op jit(solution)/shard_map/ppermute | solution.py:305
  25.2 0.7 add_convert_fusion.4
  25.9 4.7 %collective-permute-start.7 = (bf16[2,128,128]{2,1,0:T(8,128)(2,1)}, bf16[2,128,128]{2,1,0:T(8,128)(2,1)}, u32[]{:S(2)}, u32[]{:S(2)}) collective-permute-start(bf16[2,128,128]{2,1,0:T(8,128)(2,1)} %add_convert_fusion.4), channel_id=1, source_target_pairs={{0,192},{4,196},{8,200},{12,204},{16,208},{20,212},{24,216},{28,22... | collective-permute-start | bytes 196616 | tf_op jit(solution)/shard_map/ppermute | solution.py:305
  30.6 4.1 %collective-permute-start.6 = (bf16[2,128,128]{2,1,0:T(8,128)(2,1)}, bf16[2,128,128]{2,1,0:T(8,128)(2,1)}, u32[]{:S(2)}, u32[]{:S(2)}) collective-permute-start(bf16[2,128,128]{2,1,0:T(8,128)(2,1)} %add_convert_fusion.4), channel_id=1, source_target_pairs={{0,96},{4,100},{8,104},{12,108},{16,112},{20,116},{24,120},{28,124... | collective-permute-start | bytes 196616 | tf_op jit(solution)/shard_map/ppermute | solution.py:305
  34.7 1.0 %collective-permute-done.6 = bf16[2,128,128]{2,1,0:T(8,128)(2,1)} collective-permute-done((bf16[2,128,128]{2,1,0:T(8,128)(2,1)}, bf16[2,128,128]{2,1,0:T(8,128)(2,1)}, u32[]{:S(2)}, u32[]{:S(2)}) %collective-permute-start.6) | collective-permute-done | bytes 65568 | tf_op jit(solution)/shard_map/ppermute | solution.py:305
  35.7 1.0 %broadcast_select_fusion.5 = (bf16[2,128,128]{2,1,0:T(8,128)(2,1)S(1)}, f32[2,128,128]{2,1,0:T(8,128)S(1)}) fusion(pred[]{:T(512)S(6)} %eq.11, bf16[2,128,128]{2,1,0:T(8,128)(2,1)S(1)} %collective-permute-done, bf16[4,128,128]{2,1,0:T(8,128)(2,1)S(1)} %block_state.1, bf16[2,128,128]{2,1,0:T(8,128)(2,1)} %collective-permute-done.7, ...), kind=kLoop, calls=%fused_computation.36 | loop fusion | flops 753664 | bytes 851972 | tf_op jit(solution)/shard_map/jit(_where)/select_n | solution.py:329
  36.8 3.9 %collective-permute-start.8 = (bf16[2,128,128]{2,1,0:T(8,128)(2,1)S(1)}, bf16[2,128,128]{2,1,0:T(8,128)(2,1)S(1)}, u32[]{:S(2)}, u32[]{:S(2)}) collective-permute-start(bf16[2,128,128]{2,1,0:T(8,128)(2,1)S(1)} %broadcast_select_fusion.4), channel_id=1, source_target_pairs={{0,4},{4,0},{8,12},{12,8},{16,20},{20,16},{24,28},{28,24},{32,36},... | collective-permute-start | bytes 196616 | tf_op jit(solution)/shard_map/ppermute | solution.py:305
  40.7 2.0 %local_attn.2.refs_0_ = f32[1024,256]{1,0:T(8,128)S(1)} custom-call(bf16[1024,512]{1,0:T(8,128)(2,1)S(1)} %copy-done.4, bf16[1024,512]{1,0:T(8,128)(2,1)S(1)} %copy-done.1, bf16[1024,512]{1,0:T(8,128)(2,1)S(1)} %copy-done.3), custom_call_target="tpu_custom_call" | custom-call | flops 671088640 | bytes 2621440 | tf_op jit(solution)/shard_map/local_attn/pallas_call | solution.py:98
  42.8 2.0 %local_attn.3.refs_1_ = f32[1024,256]{1,0:T(8,128)S(1)} custom-call(bf16[1024,512]{1,0:T(8,128)(2,1)S(1)} %copy-done.4, bf16[1024,512]{1,0:T(8,128)(2,1)S(1)} %copy-done.1, bf16[1024,512]{1,0:T(8,128)(2,1)S(1)} %copy-done.3), custom_call_target="tpu_custom_call" | custom-call | flops 671088640 | bytes 2621440 | tf_op jit(solution)/shard_map/local_attn/pallas_call | solution.py:98
  44.9 1.5 %attn_stats.1 = (f32[1024,512]{1,0:T(8,128)S(1)}, f32[2,1024]{1,0:T(2,128)S(1)}) custom-call(f32[1024,256]{1,0:T(8,128)S(1)} %local_attn.2.refs_0_, f32[1024,256]{1,0:T(8,128)S(1)} %local_attn.3.refs_1_, bf16[1024,512]{1,0:T(8,128)(2,1)S(1)} %copy-done.4, bf16[4,128,128]{2,1,0:T(8,128)(2,1)S(1)} %maximum_select_fusion.refs_3_.p_ref, ...), custom_call_target="tpu_custom_call" | custom-call | flops 134217728 | bytes 6291456 | tf_op jit(solution)/shard_map/attn_stats/pallas_call | solution.py:141
  46.4 1.3 %copy-done.7 = f32[1024,512]{1,0:T(8,128)} copy-done((f32[1024,512]{1,0:T(8,128)}, f32[1024,512]{1,0:T(8,128)S(1)}, u32[]{:S(2)}) %copy-start.7) | copy-done | bytes 2097176
  47.7 0.5 collective-permute-start.11
  48.2 2.2 %collective-permute-start.10 = (f32[2,1024]{1,0:T(2,128)S(1)}, f32[2,1024]{1,0:T(2,128)S(1)}, u32[]{:S(2)}, u32[]{:S(2)}) collective-permute-start(f32[2,1024]{1,0:T(2,128)S(1)} %get-tuple-element.24), channel_id=1, source_target_pairs={{0,1},{1,2},{2,3},{3,0},{4,5},{5,6},{6,7},{7,4},{8,9},{9,10},{10,1... | collective-permute-start | bytes 24584 | tf_op jit(solution)/shard_map/ppermute | solution.py:335
  50.4 1.0 %collective-permute-done.11 = f32[2,1024]{1,0:T(2,128)S(1)} collective-permute-done((f32[2,1024]{1,0:T(2,128)S(1)}, f32[2,1024]{1,0:T(2,128)S(1)}, u32[]{:S(2)}, u32[]{:S(2)}) %collective-permute-start.11) | collective-permute-done | bytes 8224 | tf_op jit(solution)/shard_map/ppermute | solution.py:335
  51.5 3.0 %collective-permute-done.9 = f32[2,1024]{1,0:T(2,128)S(1)} collective-permute-done((f32[2,1024]{1,0:T(2,128)S(1)}, f32[2,1024]{1,0:T(2,128)S(1)}, u32[]{:S(2)}, u32[]{:S(2)}) %collective-permute-start.9) | collective-permute-done | bytes 8224 | tf_op jit(solution)/shard_map/ppermute | solution.py:335
  54.4 1.2 %copy-done.6 = bf16[1024,512]{1,0:T(8,128)(2,1)S(1)} copy-done((bf16[1024,512]{1,0:T(8,128)(2,1)S(1)}, bf16[1024,512]{1,0:T(8,128)(2,1)}, u32[]{:S(2)}) %copy-start.6) | copy-done | bytes 1048600
  55.7 1.6 %copy-done.8 = f32[1024,512]{1,0:T(8,128)S(1)} copy-done((f32[1024,512]{1,0:T(8,128)S(1)}, f32[1024,512]{1,0:T(8,128)}, u32[]{:S(2)}) %copy-start.8) | copy-done | bytes 2097176
  57.3 2.8 %grads_of_norm.1 = (bf16[1024,512]{1,0:T(8,128)(2,1)}, bf16[1024,512]{1,0:T(8,128)(2,1)S(1)}, bf16[4,128,128]{2,1,0:T(8,128)(2,1)S(1)}) custom-call(f32[1024,512]{1,0:T(8,128)S(1)} %copy-done.8, bf16[1024,512]{1,0:T(8,128)(2,1)S(1)} %copy-done.6, bf16[1024,512]{1,0:T(8,128)(2,1)S(1)} %copy-done.4, f32[2,1024]{1,0:T(2,128)S(1)} %add_add_fusion.stat_ref, ...), custom_call_target="tpu_custom_call" | custom-call | flops 268435456 | bytes 6291456 | tf_op jit(solution)/shard_map/grads_of_norm/pallas_call | solution.py:193
  60.1 2.0 %collective-permute-start.12 = (bf16[2,128,128]{2,1,0:T(8,128)(2,1)S(1)}, bf16[2,128,128]{2,1,0:T(8,128)(2,1)S(1)}, u32[]{:S(2)}, u32[]{:S(2)}) collective-permute-start(bf16[2,128,128]{2,1,0:T(8,128)(2,1)S(1)} %broadcast_select_fusion.2), channel_id=1, source_target_pairs={{252,248},{248,252},{244,240},{240,244},{236,232},{232,236},{228,2... | collective-permute-start | bytes 196616 | tf_op jit(solution)/shard_map/ppermute | solution.py:305
  62.1 3.2 %local_back.7 = (bf16[1024,128]{1,0:T(8,128)(2,1)S(1)}, f32[1024,128]{1,0:T(8,128)S(1)}, f32[1024,128]{1,0:T(8,128)S(1)}) custom-call(bf16[1024,512]{1,0:T(8,128)(2,1)S(1)} %copy-done.4, bf16[1024,512]{1,0:T(8,128)(2,1)S(1)} %copy-done.1, bf16[1024,512]{1,0:T(8,128)(2,1)S(1)} %copy-done.3, bf16[1024,512]{1,0:T(8,128)(2,1)S(1)} %get-tuple-element.26.d_ref, ...), custom_call_target="tpu_custom_call" | custom-call | flops 1006632960 | bytes 2359296 | tf_op jit(solution)/shard_map/local_back/pallas_call | solution.py:242
  65.5 2.7 %collective-permute-start.14 = (bf16[2,128,128]{2,1,0:T(8,128)(2,1)S(1)}, bf16[2,128,128]{2,1,0:T(8,128)(2,1)S(1)}, u32[]{:S(2)}, u32[]{:S(2)}) collective-permute-start(bf16[2,128,128]{2,1,0:T(8,128)(2,1)S(1)} %add_convert_fusion.2), channel_id=1, source_target_pairs={{252,244},{248,240},{244,236},{240,232},{236,228},{232,224},{228,2... | collective-permute-start | bytes 196616 | tf_op jit(solution)/shard_map/ppermute | solution.py:305
  68.2 0.7 collective-permute-start.13
  68.9 3.2 %local_back.6 = (bf16[1024,128]{1,0:T(8,128)(2,1)S(1)}, f32[1024,128]{1,0:T(8,128)S(1)}, f32[1024,128]{1,0:T(8,128)S(1)}) custom-call(bf16[1024,512]{1,0:T(8,128)(2,1)S(1)} %copy-done.4, bf16[1024,512]{1,0:T(8,128)(2,1)S(1)} %copy-done.1, bf16[1024,512]{1,0:T(8,128)(2,1)S(1)} %copy-done.3, bf16[1024,512]{1,0:T(8,128)(2,1)S(1)} %get-tuple-element.26.d_ref, ...), custom_call_target="tpu_custom_call" | custom-call | flops 1006632960 | bytes 2359296 | tf_op jit(solution)/shard_map/local_back/pallas_call | solution.py:242
  72.2 0.6 collective-permute-done.13
  72.8 1.9 %collective-permute-start.17 = (bf16[2,128,128]{2,1,0:T(8,128)(2,1)S(1)}, bf16[2,128,128]{2,1,0:T(8,128)(2,1)S(1)}, u32[]{:S(2)}, u32[]{:S(2)}) collective-permute-start(bf16[2,128,128]{2,1,0:T(8,128)(2,1)S(1)} %fusion.9), channel_id=1, source_target_pairs={{252,220},{248,216},{244,212},{240,208},{236,204},{232,200},{228,1... | collective-permute-start | bytes 196616 | tf_op jit(solution)/shard_map/ppermute | solution.py:305
  74.8 1.3 %collective-permute-start.16 = (bf16[2,128,128]{2,1,0:T(8,128)(2,1)S(1)}, bf16[2,128,128]{2,1,0:T(8,128)(2,1)S(1)}, u32[]{:S(2)}, u32[]{:S(2)}) collective-permute-start(bf16[2,128,128]{2,1,0:T(8,128)(2,1)S(1)} %fusion.9), channel_id=1, source_target_pairs={{252,188},{248,184},{244,180},{240,176},{236,172},{232,168},{228,1... | collective-permute-start | bytes 196616 | tf_op jit(solution)/shard_map/ppermute | solution.py:305
  76.1 3.2 %local_back.5 = (bf16[1024,128]{1,0:T(8,128)(2,1)S(1)}, f32[1024,128]{1,0:T(8,128)S(1)}, f32[1024,128]{1,0:T(8,128)S(1)}) custom-call(bf16[1024,512]{1,0:T(8,128)(2,1)S(1)} %copy-done.4, bf16[1024,512]{1,0:T(8,128)(2,1)S(1)} %copy-done.1, bf16[1024,512]{1,0:T(8,128)(2,1)S(1)} %copy-done.3, bf16[1024,512]{1,0:T(8,128)(2,1)S(1)} %get-tuple-element.26.d_ref, ...), custom_call_target="tpu_custom_call" | custom-call | flops 1006632960 | bytes 2359296 | tf_op jit(solution)/shard_map/local_back/pallas_call | solution.py:242
  79.3 2.0 %collective-permute-done.16 = bf16[2,128,128]{2,1,0:T(8,128)(2,1)S(1)} collective-permute-done((bf16[2,128,128]{2,1,0:T(8,128)(2,1)S(1)}, bf16[2,128,128]{2,1,0:T(8,128)(2,1)S(1)}, u32[]{:S(2)}, u32[]{:S(2)}) %collective-permute-start.16) | collective-permute-done | bytes 65568 | tf_op jit(solution)/shard_map/ppermute | solution.py:305
  81.4 1.3 %collective-permute-start.19 = (bf16[2,128,128]{2,1,0:T(8,128)(2,1)S(1)}, bf16[2,128,128]{2,1,0:T(8,128)(2,1)S(1)}, u32[]{:S(2)}, u32[]{:S(2)}) collective-permute-start(bf16[2,128,128]{2,1,0:T(8,128)(2,1)S(1)} %add_convert_fusion.1), channel_id=1, source_target_pairs={{252,60},{248,56},{244,52},{240,48},{236,44},{232,40},{228,36},{22... | collective-permute-start | bytes 196616 | tf_op jit(solution)/shard_map/ppermute | solution.py:305
  82.7 1.5 %collective-permute-start.18 = (bf16[2,128,128]{2,1,0:T(8,128)(2,1)S(1)}, bf16[2,128,128]{2,1,0:T(8,128)(2,1)S(1)}, u32[]{:S(2)}, u32[]{:S(2)}) collective-permute-start(bf16[2,128,128]{2,1,0:T(8,128)(2,1)S(1)} %add_convert_fusion.1), channel_id=1, source_target_pairs={{252,156},{248,152},{244,148},{240,144},{236,140},{232,136},{228,1... | collective-permute-start | bytes 196616 | tf_op jit(solution)/shard_map/ppermute | solution.py:305
  84.2 3.2 %local_back.4 = (bf16[1024,128]{1,0:T(8,128)(2,1)S(1)}, f32[1024,128]{1,0:T(8,128)S(1)}, f32[1024,128]{1,0:T(8,128)S(1)}) custom-call(bf16[1024,512]{1,0:T(8,128)(2,1)S(1)} %copy-done.4, bf16[1024,512]{1,0:T(8,128)(2,1)S(1)} %copy-done.1, bf16[1024,512]{1,0:T(8,128)(2,1)S(1)} %copy-done.3, bf16[1024,512]{1,0:T(8,128)(2,1)S(1)} %get-tuple-element.26.d_ref, ...), custom_call_target="tpu_custom_call" | custom-call | flops 1006632960 | bytes 2359296 | tf_op jit(solution)/shard_map/local_back/pallas_call | solution.py:242
  87.4 2.5 %collective-permute-done.19 = bf16[2,128,128]{2,1,0:T(8,128)(2,1)S(1)} collective-permute-done((bf16[2,128,128]{2,1,0:T(8,128)(2,1)S(1)}, bf16[2,128,128]{2,1,0:T(8,128)(2,1)S(1)}, u32[]{:S(2)}, u32[]{:S(2)}) %collective-permute-start.19) | collective-permute-done | bytes 65568 | tf_op jit(solution)/shard_map/ppermute | solution.py:305
  89.9 0.9 collective-permute-done.18
  90.8 0.1 broadcast_select_fusion.1
  91.0 6.0 %collective-permute-start.20 = (bf16[2,128,128]{2,1,0:T(8,128)(2,1)S(1)}, bf16[2,128,128]{2,1,0:T(8,128)(2,1)S(1)}, u32[]{:S(2)}, u32[]{:S(2)}) collective-permute-start(bf16[2,128,128]{2,1,0:T(8,128)(2,1)S(1)} %broadcast_select_fusion), channel_id=1, source_target_pairs={{252,248},{248,252},{244,240},{240,244},{236,232},{232,236},{228,2... | collective-permute-start | bytes 196616 | tf_op jit(solution)/shard_map/ppermute | solution.py:305
  96.9 1.1 %pad_maximum_fusion = bf16[1024,512]{1,0:T(8,128)(2,1)} fusion(bf16[1024,128]{1,0:T(8,128)(2,1)S(1)} %get-tuple-element.30, bf16[1024,128]{1,0:T(8,128)(2,1)S(1)} %get-tuple-element.29, bf16[1024,128]{1,0:T(8,128)(2,1)S(1)} %get-tuple-element.28, bf16[1024,128]{1,0:T(8,128)(2,1)S(1)} %get-tuple-element.27), kind=kLoop, calls=%fused_computation | loop fusion | flops 4194304 | bytes 2097152 | tf_op jit(solution)/shard_map/concatenate | solution.py:352
  98.0 2.5 %finish.1 = (bf16[1024,512]{1,0:T(8,128)(2,1)}, bf16[1024,512]{1,0:T(8,128)(2,1)}) custom-call(f32[1024,128]{1,0:T(8,128)S(1)} %get-tuple-element.31.refs_0_, f32[1024,128]{1,0:T(8,128)S(1)} %get-tuple-element.32.refs_1_, f32[1024,128]{1,0:T(8,128)S(1)} %get-tuple-element.33.refs_2_, f32[1024,128]{1,0:T(8,128)S(1)} %get-tuple-element.34.refs_3_, ...), custom_call_target="tpu_custom_call" | custom-call | flops 268435456 | bytes 8388608 | tf_op jit(solution)/shard_map/finish/pallas_call | solution.py:275
  (44 shorter events, 0.5 us)
Async XLA Ops:
  0.6 1.2 %copy-start = (bf16[1024,512]{1,0:T(8,128)(2,1)S(1)}, bf16[1024,512]{1,0:T(8,128)(2,1)}, u32[]{:S(2)}) copy-start(bf16[1024,512]{1,0:T(8,128)(2,1)} %refs_8_.1) | copy-start | bytes 3145732
  1.9 1.2 %copy-start.2 = (bf16[1024,512]{1,0:T(8,128)(2,1)S(1)}, bf16[1024,512]{1,0:T(8,128)(2,1)}, u32[]{:S(2)}) copy-start(bf16[1024,512]{1,0:T(8,128)(2,1)} %refs_9_.1) | copy-start | bytes 3145732
  3.1 37.6 %copy-start.1 = (bf16[1024,512]{1,0:T(8,128)(2,1)S(1)}, bf16[1024,512]{1,0:T(8,128)(2,1)}, u32[]{:S(2)}) copy-start(bf16[1024,512]{1,0:T(8,128)(2,1)} %refs_8_.1) | copy-start | bytes 3145732
  3.1 37.6 %copy-start.3 = (bf16[1024,512]{1,0:T(8,128)(2,1)S(1)}, bf16[1024,512]{1,0:T(8,128)(2,1)}, u32[]{:S(2)}) copy-start(bf16[1024,512]{1,0:T(8,128)(2,1)} %refs_9_.1) | copy-start | bytes 3145732
  3.1 37.6 %copy-start.4 = (bf16[1024,512]{1,0:T(8,128)(2,1)S(1)}, bf16[1024,512]{1,0:T(8,128)(2,1)}, u32[]{:S(2)}) copy-start(bf16[1024,512]{1,0:T(8,128)(2,1)} %q_ref.13) | copy-start | bytes 3145732
  4.3 1.7 %collective-permute-start = (bf16[2,128,128]{2,1,0:T(8,128)(2,1)S(1)}, bf16[2,128,128]{2,1,0:T(8,128)(2,1)S(1)}, u32[]{:S(2)}, u32[]{:S(2)}) collective-permute-start(bf16[2,128,128]{2,1,0:T(8,128)(2,1)S(1)} %broadcast_select_fusion.6), channel_id=1, source_target_pairs={{0,4},{4,0},{8,12},{12,8},{16,20},{20,16},{24,28},{28,24},{32,36},... | collective-permute-start | bytes 196616 | tf_op jit(solution)/shard_map/ppermute | solution.py:305
  6.0 4.3 %collective-permute-start.3 = (bf16[2,128,128]{2,1,0:T(8,128)(2,1)S(1)}, bf16[2,128,128]{2,1,0:T(8,128)(2,1)S(1)}, u32[]{:S(2)}, u32[]{:S(2)}) collective-permute-start(bf16[2,128,128]{2,1,0:T(8,128)(2,1)S(1)} %add_convert_fusion.5), channel_id=1, source_target_pairs={{0,24},{4,28},{8,0},{12,4},{16,8},{20,12},{24,16},{28,20},{32,56},... | collective-permute-start | bytes 196616 | tf_op jit(solution)/shard_map/ppermute | solution.py:305
  8.5 4.7 %collective-permute-start.2 = (bf16[2,128,128]{2,1,0:T(8,128)(2,1)S(1)}, bf16[2,128,128]{2,1,0:T(8,128)(2,1)S(1)}, u32[]{:S(2)}, u32[]{:S(2)}) collective-permute-start(bf16[2,128,128]{2,1,0:T(8,128)(2,1)S(1)} %add_convert_fusion.5), channel_id=1, source_target_pairs={{0,8},{4,12},{8,16},{12,20},{16,24},{20,28},{24,0},{28,4},{32,40},... | collective-permute-start | bytes 196616 | tf_op jit(solution)/shard_map/ppermute | solution.py:305
  8.5 5.6 %collective-permute-start.1 = (bf16[2,128,128]{2,1,0:T(8,128)(2,1)S(1)}, bf16[2,128,128]{2,1,0:T(8,128)(2,1)S(1)}, u32[]{:S(2)}, u32[]{:S(2)}) collective-permute-start(bf16[2,128,128]{2,1,0:T(8,128)(2,1)S(1)} %add_convert_fusion.5), channel_id=1, source_target_pairs={{0,16},{4,20},{8,24},{12,28},{16,0},{20,4},{24,8},{28,12},{32,48},... | collective-permute-start | bytes 196616 | tf_op jit(solution)/shard_map/ppermute | solution.py:305
  14.2 9.7 %collective-permute-start.5 = (bf16[2,128,128]{2,1,0:T(8,128)(2,1)S(1)}, bf16[2,128,128]{2,1,0:T(8,128)(2,1)S(1)}, u32[]{:S(2)}, u32[]{:S(2)}) collective-permute-start(bf16[2,128,128]{2,1,0:T(8,128)(2,1)S(1)} %fusion.8), channel_id=1, source_target_pairs={{0,32},{4,36},{8,40},{12,44},{16,48},{20,52},{24,56},{28,60},{32,6... | collective-permute-start | bytes 196616 | tf_op jit(solution)/shard_map/ppermute | solution.py:305
  17.8 7.4 %collective-permute-start.4 = (bf16[2,128,128]{2,1,0:T(8,128)(2,1)S(1)}, bf16[2,128,128]{2,1,0:T(8,128)(2,1)S(1)}, u32[]{:S(2)}, u32[]{:S(2)}) collective-permute-start(bf16[2,128,128]{2,1,0:T(8,128)(2,1)S(1)} %fusion.8), channel_id=1, source_target_pairs={{0,64},{4,68},{8,72},{12,76},{16,80},{20,84},{24,88},{28,92},{32,9... | collective-permute-start | bytes 196616 | tf_op jit(solution)/shard_map/ppermute | solution.py:305
  23.9 2.0 %copy-start.10 = (bf16[2,128,128]{2,1,0:T(8,128)(2,1)}, bf16[2,128,128]{2,1,0:T(8,128)(2,1)S(1)}, u32[]{:S(2)}) copy-start(bf16[2,128,128]{2,1,0:T(8,128)(2,1)S(1)} %collective-permute-done.5) | copy-start | bytes 196612
  25.2 5.4 %copy-start.11 = (bf16[2,128,128]{2,1,0:T(8,128)(2,1)}, bf16[2,128,128]{2,1,0:T(8,128)(2,1)S(1)}, u32[]{:S(2)}) copy-start(bf16[2,128,128]{2,1,0:T(8,128)(2,1)S(1)} %collective-permute-done.4) | copy-start | bytes 196612
  25.9 8.8 %collective-permute-start.7 = (bf16[2,128,128]{2,1,0:T(8,128)(2,1)}, bf16[2,128,128]{2,1,0:T(8,128)(2,1)}, u32[]{:S(2)}, u32[]{:S(2)}) collective-permute-start(bf16[2,128,128]{2,1,0:T(8,128)(2,1)} %add_convert_fusion.4), channel_id=1, source_target_pairs={{0,192},{4,196},{8,200},{12,204},{16,208},{20,212},{24,216},{28,22... | collective-permute-start | bytes 196616 | tf_op jit(solution)/shard_map/ppermute | solution.py:305
  30.6 5.1 %collective-permute-start.6 = (bf16[2,128,128]{2,1,0:T(8,128)(2,1)}, bf16[2,128,128]{2,1,0:T(8,128)(2,1)}, u32[]{:S(2)}, u32[]{:S(2)}) collective-permute-start(bf16[2,128,128]{2,1,0:T(8,128)(2,1)} %add_convert_fusion.4), channel_id=1, source_target_pairs={{0,96},{4,100},{8,104},{12,108},{16,112},{20,116},{24,120},{28,124... | collective-permute-start | bytes 196616 | tf_op jit(solution)/shard_map/ppermute | solution.py:305
  36.8 8.0 %collective-permute-start.8 = (bf16[2,128,128]{2,1,0:T(8,128)(2,1)S(1)}, bf16[2,128,128]{2,1,0:T(8,128)(2,1)S(1)}, u32[]{:S(2)}, u32[]{:S(2)}) collective-permute-start(bf16[2,128,128]{2,1,0:T(8,128)(2,1)S(1)} %broadcast_select_fusion.4), channel_id=1, source_target_pairs={{0,4},{4,0},{8,12},{12,8},{16,20},{20,16},{24,28},{28,24},{32,36},... | collective-permute-start | bytes 196616 | tf_op jit(solution)/shard_map/ppermute | solution.py:305
  42.8 2.1 %copy-start.5 = (bf16[1024,512]{1,0:T(8,128)(2,1)S(1)}, bf16[1024,512]{1,0:T(8,128)(2,1)}, u32[]{:S(2)}) copy-start(bf16[1024,512]{1,0:T(8,128)(2,1)} %y_ref.1) | copy-start | bytes 3145732
  42.8 2.1 %copy-start.9 = (f32[512]{0:T(512)S(1)}, f32[512]{0:T(512)}, u32[]{:S(2)}) copy-start(f32[512]{0:T(512)} %param.9) | copy-start | bytes 6148
  46.4 1.4 %copy-start.7 = (f32[1024,512]{1,0:T(8,128)}, f32[1024,512]{1,0:T(8,128)S(1)}, u32[]{:S(2)}) copy-start(f32[1024,512]{1,0:T(8,128)S(1)} %get-tuple-element.23.attn_ref) | copy-start | bytes 6291460
  47.7 3.7 %collective-permute-start.11 = (f32[2,1024]{1,0:T(2,128)S(1)}, f32[2,1024]{1,0:T(2,128)S(1)}, u32[]{:S(2)}, u32[]{:S(2)}) collective-permute-start(f32[2,1024]{1,0:T(2,128)S(1)} %get-tuple-element.24), channel_id=1, source_target_pairs={{0,3},{1,0},{2,1},{3,2},{4,7},{5,4},{6,5},{7,6},{8,11},{9,8},{10,9... | collective-permute-start | bytes 24584 | tf_op jit(solution)/shard_map/ppermute | solution.py:335
  48.2 3.3 %collective-permute-start.10 = (f32[2,1024]{1,0:T(2,128)S(1)}, f32[2,1024]{1,0:T(2,128)S(1)}, u32[]{:S(2)}, u32[]{:S(2)}) collective-permute-start(f32[2,1024]{1,0:T(2,128)S(1)} %get-tuple-element.24), channel_id=1, source_target_pairs={{0,1},{1,2},{2,3},{3,0},{4,5},{5,6},{6,7},{7,4},{8,9},{9,10},{10,1... | collective-permute-start | bytes 24584 | tf_op jit(solution)/shard_map/ppermute | solution.py:335
  50.4 4.0 %collective-permute-start.9 = (f32[2,1024]{1,0:T(2,128)S(1)}, f32[2,1024]{1,0:T(2,128)S(1)}, u32[]{:S(2)}, u32[]{:S(2)}) collective-permute-start(f32[2,1024]{1,0:T(2,128)S(1)} %get-tuple-element.24), channel_id=1, source_target_pairs={{0,2},{1,3},{2,0},{3,1},{4,6},{5,7},{6,4},{7,5},{8,10},{9,11},{10,... | collective-permute-start | bytes 24584 | tf_op jit(solution)/shard_map/ppermute | solution.py:335
  54.4 1.2 %copy-start.6 = (bf16[1024,512]{1,0:T(8,128)(2,1)S(1)}, bf16[1024,512]{1,0:T(8,128)(2,1)}, u32[]{:S(2)}) copy-start(bf16[1024,512]{1,0:T(8,128)(2,1)} %y_ref.1) | copy-start | bytes 3145732
  55.7 1.6 %copy-start.8 = (f32[1024,512]{1,0:T(8,128)S(1)}, f32[1024,512]{1,0:T(8,128)}, u32[]{:S(2)}) copy-start(f32[1024,512]{1,0:T(8,128)} %copy-done.7) | copy-start | bytes 6291460
  60.1 5.3 %collective-permute-start.12 = (bf16[2,128,128]{2,1,0:T(8,128)(2,1)S(1)}, bf16[2,128,128]{2,1,0:T(8,128)(2,1)S(1)}, u32[]{:S(2)}, u32[]{:S(2)}) collective-permute-start(bf16[2,128,128]{2,1,0:T(8,128)(2,1)S(1)} %broadcast_select_fusion.2), channel_id=1, source_target_pairs={{252,248},{248,252},{244,240},{240,244},{236,232},{232,236},{228,2... | collective-permute-start | bytes 196616 | tf_op jit(solution)/shard_map/ppermute | solution.py:305
  65.4 6.7 %collective-permute-start.15 = (bf16[2,128,128]{2,1,0:T(8,128)(2,1)S(1)}, bf16[2,128,128]{2,1,0:T(8,128)(2,1)S(1)}, u32[]{:S(2)}, u32[]{:S(2)}) collective-permute-start(bf16[2,128,128]{2,1,0:T(8,128)(2,1)S(1)} %add_convert_fusion.2), channel_id=1, source_target_pairs={{252,228},{248,224},{244,252},{240,248},{236,244},{232,240},{228,2... | collective-permute-start | bytes 196616 | tf_op jit(solution)/shard_map/ppermute | solution.py:305
  65.5 6.7 %collective-permute-start.14 = (bf16[2,128,128]{2,1,0:T(8,128)(2,1)S(1)}, bf16[2,128,128]{2,1,0:T(8,128)(2,1)S(1)}, u32[]{:S(2)}, u32[]{:S(2)}) collective-permute-start(bf16[2,128,128]{2,1,0:T(8,128)(2,1)S(1)} %add_convert_fusion.2), channel_id=1, source_target_pairs={{252,244},{248,240},{244,236},{240,232},{236,228},{232,224},{228,2... | collective-permute-start | bytes 196616 | tf_op jit(solution)/shard_map/ppermute | solution.py:305
  68.2 4.6 %collective-permute-start.13 = (bf16[2,128,128]{2,1,0:T(8,128)(2,1)S(1)}, bf16[2,128,128]{2,1,0:T(8,128)(2,1)S(1)}, u32[]{:S(2)}, u32[]{:S(2)}) collective-permute-start(bf16[2,128,128]{2,1,0:T(8,128)(2,1)S(1)} %add_convert_fusion.2), channel_id=1, source_target_pairs={{252,236},{248,232},{244,228},{240,224},{236,252},{232,248},{228,2... | collective-permute-start | bytes 196616 | tf_op jit(solution)/shard_map/ppermute | solution.py:305
  72.8 6.5 %collective-permute-start.17 = (bf16[2,128,128]{2,1,0:T(8,128)(2,1)S(1)}, bf16[2,128,128]{2,1,0:T(8,128)(2,1)S(1)}, u32[]{:S(2)}, u32[]{:S(2)}) collective-permute-start(bf16[2,128,128]{2,1,0:T(8,128)(2,1)S(1)} %fusion.9), channel_id=1, source_target_pairs={{252,220},{248,216},{244,212},{240,208},{236,204},{232,200},{228,1... | collective-permute-start | bytes 196616 | tf_op jit(solution)/shard_map/ppermute | solution.py:305
  74.8 6.6 %collective-permute-start.16 = (bf16[2,128,128]{2,1,0:T(8,128)(2,1)S(1)}, bf16[2,128,128]{2,1,0:T(8,128)(2,1)S(1)}, u32[]{:S(2)}, u32[]{:S(2)}) collective-permute-start(bf16[2,128,128]{2,1,0:T(8,128)(2,1)S(1)} %fusion.9), channel_id=1, source_target_pairs={{252,188},{248,184},{244,180},{240,176},{236,172},{232,168},{228,1... | collective-permute-start | bytes 196616 | tf_op jit(solution)/shard_map/ppermute | solution.py:305
  81.4 8.5 %collective-permute-start.19 = (bf16[2,128,128]{2,1,0:T(8,128)(2,1)S(1)}, bf16[2,128,128]{2,1,0:T(8,128)(2,1)S(1)}, u32[]{:S(2)}, u32[]{:S(2)}) collective-permute-start(bf16[2,128,128]{2,1,0:T(8,128)(2,1)S(1)} %add_convert_fusion.1), channel_id=1, source_target_pairs={{252,60},{248,56},{244,52},{240,48},{236,44},{232,40},{228,36},{22... | collective-permute-start | bytes 196616 | tf_op jit(solution)/shard_map/ppermute | solution.py:305
  82.7 8.1 %collective-permute-start.18 = (bf16[2,128,128]{2,1,0:T(8,128)(2,1)S(1)}, bf16[2,128,128]{2,1,0:T(8,128)(2,1)S(1)}, u32[]{:S(2)}, u32[]{:S(2)}) collective-permute-start(bf16[2,128,128]{2,1,0:T(8,128)(2,1)S(1)} %add_convert_fusion.1), channel_id=1, source_target_pairs={{252,156},{248,152},{244,148},{240,144},{236,140},{232,136},{228,1... | collective-permute-start | bytes 196616 | tf_op jit(solution)/shard_map/ppermute | solution.py:305
  91.0 7.0 %collective-permute-start.20 = (bf16[2,128,128]{2,1,0:T(8,128)(2,1)S(1)}, bf16[2,128,128]{2,1,0:T(8,128)(2,1)S(1)}, u32[]{:S(2)}, u32[]{:S(2)}) collective-permute-start(bf16[2,128,128]{2,1,0:T(8,128)(2,1)S(1)} %broadcast_select_fusion), channel_id=1, source_target_pairs={{252,248},{248,252},{244,240},{240,244},{236,232},{232,236},{228,2... | collective-permute-start | bytes 196616 | tf_op jit(solution)/shard_map/ppermute | solution.py:305

commit v2 on v1

--- a/solution.py
+++ b/solution.py
@@ -4,6 +4,7 @@
 from jax.experimental import pallas as pl
 from jax.experimental.pallas import tpu as pltpu
 from jax.sharding import PartitionSpec as P
+
 
 HEAD_DIM = 128
 WIDTH = 2048
@@ -156,15 +157,16 @@
     )(*locals_, q, prefix, y, gain)
 
 
-def grad_kernel(attn_ref, y_ref, q_ref, stat_ref, g_ref, mixed_ref, d_ref, term_ref, acc_ref):
+def grad_kernel(attn_ref, y_ref, q_ref, s0, s1, s2, s3, g_ref, mixed_ref, d_ref, term_ref, acc_ref):
     step = pl.program_id(0)
 
     @pl.when(step == 0)
     def _():
         acc_ref[...] = jnp.zeros_like(acc_ref)
 
-    inv_row = lax.rsqrt(stat_ref[0:1, :] / WIDTH + epsilon)
-    scale_row = inv_row * inv_row * stat_ref[1:2, :] / WIDTH
+    stat = (s0[...] + s1[...]) + (s2[...] + s3[...])
+    inv_row = lax.rsqrt(stat[0:1, :] / WIDTH + epsilon)
+    scale_row = inv_row * inv_row * stat[1:2, :] / WIDTH
     inv = column(inv_row)
     scale = column(scale_row)
     for h in range(q_ref.shape[1] // HEAD_DIM):
@@ -197,7 +199,7 @@
             wide,
             wide,
             wide,
-            pl.BlockSpec((2, ROWS), lambda i: (0, i)),
+            *[pl.BlockSpec((2, ROWS), lambda i: (0, i))] * 4,
             pl.BlockSpec((1, c), lambda i: (0, 0)),
         ],
         out_specs=(wide, wide, pl.BlockSpec((heads, 128, 128), lambda i: (0, 0, 0))),
@@ -210,10 +212,11 @@
         compiler_params=params(12),
         cost_estimate=cost(2 * t * c * 256, t * c * 12),
         name="grads_of_norm",
-    )(attn, y, q, stats, gain)
-
-
-def back_kernel(q_ref, k_ref, v_ref, d_ref, p_ref, dq_ref, dk_ref, dv_ref):
+    )(attn, y, q, *stats, gain)
+
+
+def back_kernel(q_ref, k_ref, v_ref, d_ref, p_ref, *refs):
+    dq_ref, dk_ref, dv_ref = refs[-3:]
     t, c = q_ref.shape
     for h in range(c // HEAD_DIM):
         cols = slice(h * HEAD_DIM, (h + 1) * HEAD_DIM)
@@ -234,25 +237,29 @@
             dv_ref[here, cols] = dv
 
 
-def local_back(q, k, v, d, prefix, part, parts):
+def local_back(q, k, v, d, prefix, dq, part, parts):
     t, c = q.shape
     w = c // parts
     spec = pl.BlockSpec((t, w), lambda i: (0, part))
     out = pl.BlockSpec((t, w), lambda i: (0, 0))
+    held = [] if dq is None else [dq]
     return pl.pallas_call(
         back_kernel,
         grid=(1,),
-        in_specs=[spec] * 4 + [pl.BlockSpec((w // 128, 128, 128), lambda i: (part, 0, 0))],
-        out_specs=(out,) * 3,
+        in_specs=[spec] * 4
+        + [pl.BlockSpec((w // 128, 128, 128), lambda i: (part, 0, 0))]
+        + [pl.BlockSpec(memory_space=pl.ANY)] * len(held),
+        out_specs=(spec, out, out),
+        input_output_aliases={5: 0} if held else {},
         out_shape=(
-            jax.ShapeDtypeStruct((t, w), bf16),
+            jax.ShapeDtypeStruct((t, c), bf16),
             jax.ShapeDtypeStruct((t, w), f32),
             jax.ShapeDtypeStruct((t, w), f32),
         ),
         compiler_params=params(24),
         cost_estimate=cost(6 * 2 * t * t * w * 5 // 8, t * w * 18),
         name="local_back",
-    )(q, k, v, d, prefix)
+    )(q, k, v, d, prefix, *held)
 
 
 def final_kernel(*refs):
@@ -292,22 +299,32 @@
     pairs = []
     for i in range(NZ * NX * 2):
         z, x, c = i // 8, (i // 2) % 4, i % 2
-        z2 = z + dz
-        if not 0 <= z2 < NZ:
-            continue
-        j = (z2 * NX + (x + dx) % NX) * 2 + (1 - c if swap else c)
+        j = ((z + dz) % NZ * NX + (x + dx) % NX) * 2 + (1 - c if swap else c)
         pairs.append((63 - i, 63 - j) if reverse else (i, j))
     return pairs
 
 
-def exclusive_sum(own, reverse):
+def places(reverse):
+    index = lax.axis_index("seq")
+    index = 63 - index if reverse else index
+    z, x, c = index >> 3, (index >> 1) & 3, index & 1
+    low, high = (z + 7) & 7, (z + 1) & 7
+    up, down = (z + 3) & 7, (z + 5) & 7
+    return (
+        c == 0,
+        tuple(x >= k for k in (1, 2, 3)),
+        z >= 1,
+        z == 7,
+        (low < up, z < up, high < up),
+        (low < down, z < down),
+    )
+
+
+def exclusive_sum(own, reverse, masks):
     def send(a, **step):
         return lax.ppermute(a, "seq", step_pairs(reverse, **step))
 
-    index = lax.axis_index("seq")
-    index = 63 - index if reverse else index
-    x, c = (index // 2) % 4, index % 2
-    first = c == 0
+    first, west, south, north, up, down = masks
     n = own.shape[0] // 2
     mine = jnp.where(first, own[:n], own[n:])
     other = jnp.where(first, own[n:], own[:n])
@@ -315,14 +332,20 @@
     chip = (mine.astype(f32) + got.astype(f32)).astype(bf16)
     row = chip.astype(f32)
     before = jnp.zeros_like(row)
-    for k in (2, 1, 3):
+    for k in (1, 3, 2):
         r = send(chip, dx=k).astype(f32)
         row = row + r
-        before = before + jnp.where(x >= k, r, 0.0)
+        before = before + jnp.where(west[k - 1], r, 0.0)
     plane = row.astype(bf16)
-    near = send(plane, dz=2).astype(f32) + send(plane, dz=1).astype(f32)
-    three = (row + near).astype(bf16)
-    far = send(three, dz=3).astype(f32) + send(three, dz=6).astype(f32)
+    below = send(plane, dz=1).astype(f32)
+    above = send(plane, dz=-1).astype(f32)
+    near = jnp.where(south, below, 0.0) + jnp.where(north, above, 0.0)
+
+    def lacking(flags):
+        return sum(jnp.where(m, p, 0.0) for m, p in zip(flags, (below, row, above))).astype(bf16)
+
+    far = send(lacking(up), dz=3).astype(f32)
+    far = far + send(lacking(down), dz=-3).astype(f32)
     e0 = before + near + far
     e1 = e0 + jnp.where(first, mine, got).astype(f32)
     e0, e1 = e0.astype(bf16), e1.astype(bf16)
@@ -331,25 +354,34 @@
     return jnp.where(first, jnp.concatenate([keep, back]), jnp.concatenate([back, keep]))
 
 
-def head_sum(a):
-    r = [lax.ppermute(a, "head", [(i, (i + k) % 4) for i in range(4)]) for k in (2, 1, 3)]
-    return a + r[0] + r[1] + r[2]
-
-
-FWD, BWD = 2, 4
+def head_parts(a):
+    return [a] + [
+        lax.ppermute(a, "head", [(i, (i + k) % 4) for i in range(4)]) for k in (1, 3, 2)
+    ]
+
+
+PARTS = 4
 
 
 def shards(q, k, v, y, gain):
     gain = gain[None, :]
-    prefix = exclusive_sum(block_state(k, v), False)
-    locals_ = [local_attn(q, k, v, i, FWD) for i in range(FWD)]
+    first, last = places(False), places(True)
+    first, last, k, v = lax.optimization_barrier((first, last, k, v))
+    in_hbm = [pltpu.with_memory_space_constraint(a, pltpu.HBM) for a in (k, v)]
+    prefix = exclusive_sum(block_state(*in_hbm), False, first)
+    locals_ = []
+    for i in range(PARTS):
+        locals_.append(local_attn(q, k, v, i, PARTS))
     attn, stats = attn_stats(locals_, q, prefix, y, gain)
-    stats = head_sum(stats)
-    mixed, d, term = grads_of_norm(attn, y, q, stats, gain)
-    suffix = exclusive_sum(term, True)
-    parts = [local_back(q, k, v, d, prefix, i, BWD) for i in range(BWD)]
-    dk, dv = finish([p[1] for p in parts], [p[2] for p in parts], k, v, suffix)
-    return mixed, jnp.concatenate([p[0] for p in parts], axis=1), dk, dv
+    mixed, d, term = grads_of_norm(attn, y, q, head_parts(stats), gain)
+    suffix = exclusive_sum(term, True, last)
+    dq, dks, dvs = None, [], []
+    for i in range(PARTS):
+        dq, dk, dv = local_back(q, k, v, d, prefix, dq, i, PARTS)
+        dks.append(dk)
+        dvs.append(dv)
+    dk, dv = finish(dks, dvs, k, v, suffix)
+    return mixed, dq, dk, dv
 
 
 def solution(mesh):

time: 101 us -> 87.4 us (0.87)
  the two profiles are of different devices: /device:TPU:57 before, /device:TPU:1 now
where the time goes in v2:
time: 87.4 us; the launch traced here: 87.3 us
  starting transfers between devices  38.8 us (44%)
  Pallas kernels  29.4 us (34%)
  waiting for transfers between devices  17.5 us (20%)
  between operations  0.88 us (1%)
    ppermute x18, starting transfers between devices, send(): return lax.ppermute(a, 'seq', step_pairs(reverse, **step))  34.3 us
    pallas_call x4, Pallas kernels, local_back(): pl.pallas_call(back_kernel, grid=(1,), in_specs=[spec] * 4 + [pl.BlockSpe...  15 us
    ppermute x18, waiting for transfers between devices, send(): return lax.ppermute(a, 'seq', step_pairs(reverse, **step))  14.5 us
    ppermute x3, starting transfers between devices, head_parts(): lax.ppermute(a, 'head', [(i, (i + k) % 4) for i in range(4)])  4.46 us
    pallas_call x4, Pallas kernels, local_attn(): pl.pallas_call(local_kernel, grid=(1,), in_specs=[spec] * 3, out_specs=pl...  4.41 us
    pallas_call x1, Pallas kernels, block_state(): pl.pallas_call(outer_kernel, grid=(t // ROWS,), in_specs=[spec, spec], ou...  3.15 us
    ppermute x3, waiting for transfers between devices, head_parts(): lax.ppermute(a, 'head', [(i, (i + k) % 4) for i in range(4)])  3.02 us
    pallas_call x1, Pallas kernels, grads_of_norm(): pl.pallas_call(grad_kernel, grid=(t // ROWS,), in_specs=[wide, wide, wide...  2.89 us
  transfers between devices with their start and end apart: 21, of which 11 were waited for; matrix products, arithmetic and copies ran while one was open for 0% of the time, Pallas kernels for 22%

profile of v2, /device:TPU:1, one launch (start us, length us, event | category | flops | bytes accessed | tf_op | source)
XLA Modules:
  0.0 87.3 jit_solution(124801412049177117)
XLA Ops:
  0.7 3.1 %block_state.1 = bf16[4,128,128]{2,1,0:T(8,128)(2,1)S(1)} custom-call(bf16[1024,512]{1,0:T(8,128)(2,1)} %refs_8_, bf16[1024,512]{1,0:T(8,128)(2,1)} %refs_9_), custom_call_target="tpu_custom_call" | custom-call | flops 268435456 | bytes 2097152 | tf_op jit(solution)/shard_map/block_state/pallas_call | solution.py:61
  3.9 3.3 %collective-permute-start = (bf16[2,128,128]{2,1,0:T(8,128)(2,1)S(1)}, bf16[2,128,128]{2,1,0:T(8,128)(2,1)S(1)}, u32[]{:S(2)}, u32[]{:S(2)}) collective-permute-start(bf16[2,128,128]{2,1,0:T(8,128)(2,1)S(1)} %broadcast_select_fusion.6), channel_id=1, source_target_pairs={{0,4},{4,0},{8,12},{12,8},{16,20},{20,16},{24,28},{28,24},{32,36},... | collective-permute-start | bytes 196616 | tf_op jit(solution)/shard_map/ppermute | solution.py:325
  7.2 0.9 %collective-permute-done = bf16[2,128,128]{2,1,0:T(8,128)(2,1)S(1)} collective-permute-done((bf16[2,128,128]{2,1,0:T(8,128)(2,1)S(1)}, bf16[2,128,128]{2,1,0:T(8,128)(2,1)S(1)}, u32[]{:S(2)}, u32[]{:S(2)}) %collective-permute-start) | collective-permute-done | bytes 65568 | tf_op jit(solution)/shard_map/ppermute | solution.py:325
  8.1 1.1 %collective-permute-start.3 = (bf16[2,128,128]{2,1,0:T(8,128)(2,1)S(1)}, bf16[2,128,128]{2,1,0:T(8,128)(2,1)S(1)}, u32[]{:S(2)}, u32[]{:S(2)}) collective-permute-start(bf16[2,128,128]{2,1,0:T(8,128)(2,1)S(1)} %add_convert_fusion.3), channel_id=1, source_target_pairs={{0,16},{4,20},{8,24},{12,28},{16,0},{20,4},{24,8},{28,12},{32,48},... | collective-permute-start | bytes 196616 | tf_op jit(solution)/shard_map/ppermute | solution.py:325
  9.2 0.9 collective-permute-start.2
  10.1 0.6 collective-permute-start.1
  10.7 2.1 %collective-permute-done.3 = bf16[2,128,128]{2,1,0:T(8,128)(2,1)S(1)} collective-permute-done((bf16[2,128,128]{2,1,0:T(8,128)(2,1)S(1)}, bf16[2,128,128]{2,1,0:T(8,128)(2,1)S(1)}, u32[]{:S(2)}, u32[]{:S(2)}) %collective-permute-start.3) | collective-permute-done | bytes 65568 | tf_op jit(solution)/shard_map/ppermute | solution.py:325
  12.8 0.2 collective-permute-done.2
  13.0 1.4 %collective-permute-done.1 = bf16[2,128,128]{2,1,0:T(8,128)(2,1)S(1)} collective-permute-done((bf16[2,128,128]{2,1,0:T(8,128)(2,1)S(1)}, bf16[2,128,128]{2,1,0:T(8,128)(2,1)S(1)}, u32[]{:S(2)}, u32[]{:S(2)}) %collective-permute-start.1) | collective-permute-done | bytes 65568 | tf_op jit(solution)/shard_map/ppermute | solution.py:325
  14.5 5.7 %collective-permute-start.5 = (bf16[2,128,128]{2,1,0:T(8,128)(2,1)S(1)}, bf16[2,128,128]{2,1,0:T(8,128)(2,1)S(1)}, u32[]{:S(2)}, u32[]{:S(2)}) collective-permute-start(bf16[2,128,128]{2,1,0:T(8,128)(2,1)S(1)} %fusion.20), channel_id=1, source_target_pairs={{0,224},{4,228},{8,232},{12,236},{16,240},{20,244},{24,248},{28,25... | collective-permute-start | bytes 196616 | tf_op jit(solution)/shard_map/ppermute | solution.py:325
  20.1 1.3 %collective-permute-done.5 = bf16[2,128,128]{2,1,0:T(8,128)(2,1)S(1)} collective-permute-done((bf16[2,128,128]{2,1,0:T(8,128)(2,1)S(1)}, bf16[2,128,128]{2,1,0:T(8,128)(2,1)S(1)}, u32[]{:S(2)}, u32[]{:S(2)}) %collective-permute-start.5) | collective-permute-done | bytes 65568 | tf_op jit(solution)/shard_map/ppermute | solution.py:325
  21.5 3.0 %collective-permute-done.4 = bf16[2,128,128]{2,1,0:T(8,128)(2,1)S(1)} collective-permute-done((bf16[2,128,128]{2,1,0:T(8,128)(2,1)S(1)}, bf16[2,128,128]{2,1,0:T(8,128)(2,1)S(1)}, u32[]{:S(2)}, u32[]{:S(2)}) %collective-permute-start.4) | collective-permute-done | bytes 65568 | tf_op jit(solution)/shard_map/ppermute | solution.py:325
  24.5 0.1 fusion.6
  24.5 0.1 collective-permute-start.6
  24.6 4.5 %collective-permute-start.7 = (bf16[2,128,128]{2,1,0:T(8,128)(2,1)S(1)}, bf16[2,128,128]{2,1,0:T(8,128)(2,1)S(1)}, u32[]{:S(2)}, u32[]{:S(2)}) collective-permute-start(bf16[2,128,128]{2,1,0:T(8,128)(2,1)S(1)} %get-tuple-element.97), channel_id=1, source_target_pairs={{0,160},{4,164},{8,168},{12,172},{16,176},{20,180},{24,184},{28,18... | collective-permute-start | bytes 196616 | tf_op jit(solution)/shard_map/ppermute | solution.py:325
  29.1 1.1 %local_attn.7.refs_3_ = f32[1024,128]{1,0:T(8,128)S(1)} custom-call(bf16[1024,512]{1,0:T(8,128)(2,1)S(1)} %copy-done.2, bf16[1024,512]{1,0:T(8,128)(2,1)S(1)} %copy-done, bf16[1024,512]{1,0:T(8,128)(2,1)S(1)} %copy-done.1), custom_call_target="tpu_custom_call" | custom-call | flops 335544320 | bytes 1310720 | tf_op jit(solution)/shard_map/local_attn/pallas_call | solution.py:99
  30.2 0.8 collective-permute-done.6
  31.0 0.1 broadcast_select_fusion.5
  31.1 4.9 %collective-permute-start.8 = (bf16[2,128,128]{2,1,0:T(8,128)(2,1)S(1)}, bf16[2,128,128]{2,1,0:T(8,128)(2,1)S(1)}, u32[]{:S(2)}, u32[]{:S(2)}) collective-permute-start(bf16[2,128,128]{2,1,0:T(8,128)(2,1)S(1)} %broadcast_select_fusion.4), channel_id=1, source_target_pairs={{0,4},{4,0},{8,12},{12,8},{16,20},{20,16},{24,28},{28,24},{32,36},... | collective-permute-start | bytes 196616 | tf_op jit(solution)/shard_map/ppermute | solution.py:325
  36.0 1.1 %local_attn.6.refs_2_ = f32[1024,128]{1,0:T(8,128)S(1)} custom-call(bf16[1024,512]{1,0:T(8,128)(2,1)S(1)} %copy-done.2, bf16[1024,512]{1,0:T(8,128)(2,1)S(1)} %copy-done, bf16[1024,512]{1,0:T(8,128)(2,1)S(1)} %copy-done.1), custom_call_target="tpu_custom_call" | custom-call | flops 335544320 | bytes 1310720 | tf_op jit(solution)/shard_map/local_attn/pallas_call | solution.py:99
  37.1 1.1 %local_attn.5.refs_1_ = f32[1024,128]{1,0:T(8,128)S(1)} custom-call(bf16[1024,512]{1,0:T(8,128)(2,1)S(1)} %copy-done.2, bf16[1024,512]{1,0:T(8,128)(2,1)S(1)} %copy-done, bf16[1024,512]{1,0:T(8,128)(2,1)S(1)} %copy-done.1), custom_call_target="tpu_custom_call" | custom-call | flops 335544320 | bytes 1310720 | tf_op jit(solution)/shard_map/local_attn/pallas_call | solution.py:99
  38.3 1.1 %local_attn.4.refs_0_ = f32[1024,128]{1,0:T(8,128)S(1)} custom-call(bf16[1024,512]{1,0:T(8,128)(2,1)S(1)} %copy-done.2, bf16[1024,512]{1,0:T(8,128)(2,1)S(1)} %copy-done, bf16[1024,512]{1,0:T(8,128)(2,1)S(1)} %copy-done.1), custom_call_target="tpu_custom_call" | custom-call | flops 335544320 | bytes 1310720 | tf_op jit(solution)/shard_map/local_attn/pallas_call | solution.py:99
  39.4 0.1 copy-done.3
  39.5 1.5 %attn_stats.1 = (f32[1024,512]{1,0:T(8,128)S(1)}, f32[2,1024]{1,0:T(2,128)S(1)}) custom-call(f32[1024,128]{1,0:T(8,128)S(1)} %local_attn.4.refs_0_, f32[1024,128]{1,0:T(8,128)S(1)} %local_attn.5.refs_1_, f32[1024,128]{1,0:T(8,128)S(1)} %local_attn.6.refs_2_, f32[1024,128]{1,0:T(8,128)S(1)} %local_attn.7.refs_3_, bf16[1024,512]{1,0:T(8,128)(2,1)S(1)} %copy-done.2, ...), custom_call_target="tpu_custom_call" | custom-call | flops 134217728 | bytes 6291456 | tf_op jit(solution)/shard_map/attn_stats/pallas_call | solution.py:142
  41.0 3.0 %collective-permute-start.11 = (f32[2,1024]{1,0:T(2,128)S(1)}, f32[2,1024]{1,0:T(2,128)S(1)}, u32[]{:S(2)}, u32[]{:S(2)}) collective-permute-start(f32[2,1024]{1,0:T(2,128)S(1)} %get-tuple-element.61.s0), channel_id=1, source_target_pairs={{0,2},{1,3},{2,0},{3,1},{4,6},{5,7},{6,4},{7,5},{8,10},{9,11},{10,... | collective-permute-start | bytes 24584 | tf_op jit(solution)/shard_map/ppermute | solution.py:359
  44.0 0.8 collective-permute-start.10
  44.8 0.7 collective-permute-start.9
  45.5 1.0 %collective-permute-done.10.s2 = f32[2,1024]{1,0:T(2,128)S(1)} collective-permute-done((f32[2,1024]{1,0:T(2,128)S(1)}, f32[2,1024]{1,0:T(2,128)S(1)}, u32[]{:S(2)}, u32[]{:S(2)}) %collective-permute-start.10) | collective-permute-done | bytes 8224 | tf_op jit(solution)/shard_map/ppermute | solution.py:359
  46.5 2.0 %collective-permute-done.9.s1 = f32[2,1024]{1,0:T(2,128)S(1)} collective-permute-done((f32[2,1024]{1,0:T(2,128)S(1)}, f32[2,1024]{1,0:T(2,128)S(1)}, u32[]{:S(2)}, u32[]{:S(2)}) %collective-permute-start.9) | collective-permute-done | bytes 8224 | tf_op jit(solution)/shard_map/ppermute | solution.py:359
  48.5 2.9 %grads_of_norm.1 = (bf16[1024,512]{1,0:T(8,128)(2,1)}, bf16[1024,512]{1,0:T(8,128)(2,1)S(1)}, bf16[4,128,128]{2,1,0:T(8,128)(2,1)S(1)}) custom-call(f32[1024,512]{1,0:T(8,128)S(1)} %get-tuple-element.60.attn_ref, bf16[1024,512]{1,0:T(8,128)(2,1)S(1)} %copy-done.3, bf16[1024,512]{1,0:T(8,128)(2,1)S(1)} %copy-done.2, f32[2,1024]{1,0:T(2,128)S(1)} %get-tuple-element.61.s0, ...), custom_call_target="tpu_custom_call" | custom-call | flops 268435456 | bytes 6291456 | tf_op jit(solution)/shard_map/grads_of_norm/pallas_call | solution.py:195
  51.4 1.8 %collective-permute-start.12 = (bf16[2,128,128]{2,1,0:T(8,128)(2,1)S(1)}, bf16[2,128,128]{2,1,0:T(8,128)(2,1)S(1)}, u32[]{:S(2)}, u32[]{:S(2)}) collective-permute-start(bf16[2,128,128]{2,1,0:T(8,128)(2,1)S(1)} %broadcast_select_fusion.2), channel_id=1, source_target_pairs={{252,248},{248,252},{244,240},{240,244},{236,232},{232,236},{228,2... | collective-permute-start | bytes 196616 | tf_op jit(solution)/shard_map/ppermute | solution.py:325
  53.2 0.9 %collective-permute-done.12 = bf16[2,128,128]{2,1,0:T(8,128)(2,1)S(1)} collective-permute-done((bf16[2,128,128]{2,1,0:T(8,128)(2,1)S(1)}, bf16[2,128,128]{2,1,0:T(8,128)(2,1)S(1)}, u32[]{:S(2)}, u32[]{:S(2)}) %collective-permute-start.12) | collective-permute-done | bytes 65568 | tf_op jit(solution)/shard_map/ppermute | solution.py:325
  54.1 0.8 collective-permute-start.15
  54.9 0.4 collective-permute-start.14
  55.3 2.2 %collective-permute-start.13 = (bf16[2,128,128]{2,1,0:T(8,128)(2,1)S(1)}, bf16[2,128,128]{2,1,0:T(8,128)(2,1)S(1)}, u32[]{:S(2)}, u32[]{:S(2)}) collective-permute-start(bf16[2,128,128]{2,1,0:T(8,128)(2,1)S(1)} %add_convert_fusion.1), channel_id=1, source_target_pairs={{252,244},{248,240},{244,236},{240,232},{236,228},{232,224},{228,2... | collective-permute-start | bytes 196616 | tf_op jit(solution)/shard_map/ppermute | solution.py:325
  57.6 3.7 %local_back.4 = (bf16[1024,512]{1,0:T(8,128)(2,1)}, f32[1024,128]{1,0:T(8,128)S(1)}, f32[1024,128]{1,0:T(8,128)S(1)}) custom-call(bf16[1024,512]{1,0:T(8,128)(2,1)S(1)} %copy-done.2, bf16[1024,512]{1,0:T(8,128)(2,1)S(1)} %copy-done, bf16[1024,512]{1,0:T(8,128)(2,1)S(1)} %copy-done.1, bf16[1024,512]{1,0:T(8,128)(2,1)S(1)} %get-tuple-element.63.d_ref, ...), custom_call_target="tpu_custom_call" | custom-call | flops 1006632960 | bytes 2359296 | tf_op jit(solution)/shard_map/local_back/pallas_call | solution.py:246
  61.4 1.7 %collective-permute-start.17 = (bf16[2,128,128]{2,1,0:T(8,128)(2,1)S(1)}, bf16[2,128,128]{2,1,0:T(8,128)(2,1)S(1)}, u32[]{:S(2)}, u32[]{:S(2)}) collective-permute-start(bf16[2,128,128]{2,1,0:T(8,128)(2,1)S(1)} %fusion.21), channel_id=1, source_target_pairs={{252,28},{248,24},{244,20},{240,16},{236,12},{232,8},{228,4},{224,... | collective-permute-start | bytes 196616 | tf_op jit(solution)/shard_map/ppermute | solution.py:325
  63.1 1.0 %collective-permute-start.16 = (bf16[2,128,128]{2,1,0:T(8,128)(2,1)S(1)}, bf16[2,128,128]{2,1,0:T(8,128)(2,1)S(1)}, u32[]{:S(2)}, u32[]{:S(2)}) collective-permute-start(bf16[2,128,128]{2,1,0:T(8,128)(2,1)S(1)} %fusion.21), channel_id=1, source_target_pairs={{252,220},{248,216},{244,212},{240,208},{236,204},{232,200},{228,1... | collective-permute-start | bytes 196616 | tf_op jit(solution)/shard_map/ppermute | solution.py:325
  64.1 3.7 %local_back.5 = (bf16[1024,512]{1,0:T(8,128)(2,1)}, f32[1024,128]{1,0:T(8,128)S(1)}, f32[1024,128]{1,0:T(8,128)S(1)}) custom-call(bf16[1024,512]{1,0:T(8,128)(2,1)S(1)} %copy-done.2, bf16[1024,512]{1,0:T(8,128)(2,1)S(1)} %copy-done, bf16[1024,512]{1,0:T(8,128)(2,1)S(1)} %copy-done.1, ...), custom_call_target="tpu_custom_call", output_to_operand_aliasing={{0}: (5, {})} | custom-call | flops 1006632960 | bytes 2359296 | tf_op jit(solution)/shard_map/local_back/pallas_call | solution.py:246
  67.9 0.1 fusion.13
  68.0 3.5 %collective-permute-start.18 = (bf16[2,128,128]{2,1,0:T(8,128)(2,1)S(1)}, bf16[2,128,128]{2,1,0:T(8,128)(2,1)S(1)}, u32[]{:S(2)}, u32[]{:S(2)}) collective-permute-start(bf16[2,128,128]{2,1,0:T(8,128)(2,1)S(1)} %get-tuple-element.94), channel_id=1, source_target_pairs={{252,156},{248,152},{244,148},{240,144},{236,140},{232,136},{228,1... | collective-permute-start | bytes 196616 | tf_op jit(solution)/shard_map/ppermute | solution.py:325
  71.5 0.0 collective-permute-start.19
  71.5 3.7 %local_back.6 = (bf16[1024,512]{1,0:T(8,128)(2,1)}, f32[1024,128]{1,0:T(8,128)S(1)}, f32[1024,128]{1,0:T(8,128)S(1)}) custom-call(bf16[1024,512]{1,0:T(8,128)(2,1)S(1)} %copy-done.2, bf16[1024,512]{1,0:T(8,128)(2,1)S(1)} %copy-done, bf16[1024,512]{1,0:T(8,128)(2,1)S(1)} %copy-done.1, ...), custom_call_target="tpu_custom_call", output_to_operand_aliasing={{0}: (5, {})} | custom-call | flops 1006632960 | bytes 2359296 | tf_op jit(solution)/shard_map/local_back/pallas_call | solution.py:246
  75.3 3.8 %collective-permute-done.19 = bf16[2,128,128]{2,1,0:T(8,128)(2,1)S(1)} collective-permute-done((bf16[2,128,128]{2,1,0:T(8,128)(2,1)S(1)}, bf16[2,128,128]{2,1,0:T(8,128)(2,1)S(1)}, u32[]{:S(2)}, u32[]{:S(2)}) %collective-permute-start.19) | collective-permute-done | bytes 65568 | tf_op jit(solution)/shard_map/ppermute | solution.py:325
  79.1 0.1 broadcast_select_fusion.1
  79.3 1.8 %collective-permute-start.20 = (bf16[2,128,128]{2,1,0:T(8,128)(2,1)S(1)}, bf16[2,128,128]{2,1,0:T(8,128)(2,1)S(1)}, u32[]{:S(2)}, u32[]{:S(2)}) collective-permute-start(bf16[2,128,128]{2,1,0:T(8,128)(2,1)S(1)} %broadcast_select_fusion), channel_id=1, source_target_pairs={{252,248},{248,252},{244,240},{240,244},{236,232},{232,236},{228,2... | collective-permute-start | bytes 196616 | tf_op jit(solution)/shard_map/ppermute | solution.py:325
  81.1 3.7 %local_back.7 = (bf16[1024,512]{1,0:T(8,128)(2,1)}, f32[1024,128]{1,0:T(8,128)S(1)}, f32[1024,128]{1,0:T(8,128)S(1)}) custom-call(bf16[1024,512]{1,0:T(8,128)(2,1)S(1)} %copy-done.2, bf16[1024,512]{1,0:T(8,128)(2,1)S(1)} %copy-done, bf16[1024,512]{1,0:T(8,128)(2,1)S(1)} %copy-done.1, ...), custom_call_target="tpu_custom_call", output_to_operand_aliasing={{0}: (5, {})} | custom-call | flops 1006632960 | bytes 2359296 | tf_op jit(solution)/shard_map/local_back/pallas_call | solution.py:246
  84.8 2.5 %finish.1 = (bf16[1024,512]{1,0:T(8,128)(2,1)}, bf16[1024,512]{1,0:T(8,128)(2,1)}) custom-call(f32[1024,128]{1,0:T(8,128)S(1)} %get-tuple-element.68.refs_0_, f32[1024,128]{1,0:T(8,128)S(1)} %get-tuple-element.69.refs_1_, f32[1024,128]{1,0:T(8,128)S(1)} %get-tuple-element.70.refs_2_, f32[1024,128]{1,0:T(8,128)S(1)} %get-tuple-element.71.refs_3_, ...), custom_call_target="tpu_custom_call" | custom-call | flops 268435456 | bytes 8388608 | tf_op jit(solution)/shard_map/finish/pallas_call | solution.py:282
  (30 shorter events, 0.3 us)
Async XLA Ops:
  0.6 28.5 %copy-start.1 = (bf16[1024,512]{1,0:T(8,128)(2,1)S(1)}, bf16[1024,512]{1,0:T(8,128)(2,1)}, u32[]{:S(2)}) copy-start(bf16[1024,512]{1,0:T(8,128)(2,1)} %refs_9_) | copy-start | bytes 3145732
  0.6 28.5 %copy-start = (bf16[1024,512]{1,0:T(8,128)(2,1)S(1)}, bf16[1024,512]{1,0:T(8,128)(2,1)}, u32[]{:S(2)}) copy-start(bf16[1024,512]{1,0:T(8,128)(2,1)} %refs_8_) | copy-start | bytes 3145732
  0.7 28.5 %copy-start.2 = (bf16[1024,512]{1,0:T(8,128)(2,1)S(1)}, bf16[1024,512]{1,0:T(8,128)(2,1)}, u32[]{:S(2)}) copy-start(bf16[1024,512]{1,0:T(8,128)(2,1)} %q_ref.17) | copy-start | bytes 3145732
  3.9 4.2 %collective-permute-start = (bf16[2,128,128]{2,1,0:T(8,128)(2,1)S(1)}, bf16[2,128,128]{2,1,0:T(8,128)(2,1)S(1)}, u32[]{:S(2)}, u32[]{:S(2)}) collective-permute-start(bf16[2,128,128]{2,1,0:T(8,128)(2,1)S(1)} %broadcast_select_fusion.6), channel_id=1, source_target_pairs={{0,4},{4,0},{8,12},{12,8},{16,20},{20,16},{24,28},{28,24},{32,36},... | collective-permute-start | bytes 196616 | tf_op jit(solution)/shard_map/ppermute | solution.py:325
  8.1 4.7 %collective-permute-start.3 = (bf16[2,128,128]{2,1,0:T(8,128)(2,1)S(1)}, bf16[2,128,128]{2,1,0:T(8,128)(2,1)S(1)}, u32[]{:S(2)}, u32[]{:S(2)}) collective-permute-start(bf16[2,128,128]{2,1,0:T(8,128)(2,1)S(1)} %add_convert_fusion.3), channel_id=1, source_target_pairs={{0,16},{4,20},{8,24},{12,28},{16,0},{20,4},{24,8},{28,12},{32,48},... | collective-permute-start | bytes 196616 | tf_op jit(solution)/shard_map/ppermute | solution.py:325
  9.2 3.8 %collective-permute-start.2 = (bf16[2,128,128]{2,1,0:T(8,128)(2,1)S(1)}, bf16[2,128,128]{2,1,0:T(8,128)(2,1)S(1)}, u32[]{:S(2)}, u32[]{:S(2)}) collective-permute-start(bf16[2,128,128]{2,1,0:T(8,128)(2,1)S(1)} %add_convert_fusion.3), channel_id=1, source_target_pairs={{0,24},{4,28},{8,0},{12,4},{16,8},{20,12},{24,16},{28,20},{32,56},... | collective-permute-start | bytes 196616 | tf_op jit(solution)/shard_map/ppermute | solution.py:325
  10.1 4.3 %collective-permute-start.1 = (bf16[2,128,128]{2,1,0:T(8,128)(2,1)S(1)}, bf16[2,128,128]{2,1,0:T(8,128)(2,1)S(1)}, u32[]{:S(2)}, u32[]{:S(2)}) collective-permute-start(bf16[2,128,128]{2,1,0:T(8,128)(2,1)S(1)} %add_convert_fusion.3), channel_id=1, source_target_pairs={{0,8},{4,12},{8,16},{12,20},{16,24},{20,28},{24,0},{28,4},{32,40},... | collective-permute-start | bytes 196616 | tf_op jit(solution)/shard_map/ppermute | solution.py:325
  14.5 7.0 %collective-permute-start.5 = (bf16[2,128,128]{2,1,0:T(8,128)(2,1)S(1)}, bf16[2,128,128]{2,1,0:T(8,128)(2,1)S(1)}, u32[]{:S(2)}, u32[]{:S(2)}) collective-permute-start(bf16[2,128,128]{2,1,0:T(8,128)(2,1)S(1)} %fusion.20), channel_id=1, source_target_pairs={{0,224},{4,228},{8,232},{12,236},{16,240},{20,244},{24,248},{28,25... | collective-permute-start | bytes 196616 | tf_op jit(solution)/shard_map/ppermute | solution.py:325
  20.1 4.3 %collective-permute-start.4 = (bf16[2,128,128]{2,1,0:T(8,128)(2,1)S(1)}, bf16[2,128,128]{2,1,0:T(8,128)(2,1)S(1)}, u32[]{:S(2)}, u32[]{:S(2)}) collective-permute-start(bf16[2,128,128]{2,1,0:T(8,128)(2,1)S(1)} %fusion.20), channel_id=1, source_target_pairs={{0,32},{4,36},{8,40},{12,44},{16,48},{20,52},{24,56},{28,60},{32,6... | collective-permute-start | bytes 196616 | tf_op jit(solution)/shard_map/ppermute | solution.py:325
  24.5 6.4 %collective-permute-start.6 = (bf16[2,128,128]{2,1,0:T(8,128)(2,1)S(1)}, bf16[2,128,128]{2,1,0:T(8,128)(2,1)S(1)}, u32[]{:S(2)}, u32[]{:S(2)}) collective-permute-start(bf16[2,128,128]{2,1,0:T(8,128)(2,1)S(1)} %get-tuple-element.96), channel_id=1, source_target_pairs={{0,96},{4,100},{8,104},{12,108},{16,112},{20,116},{24,120},{28,124... | collective-permute-start | bytes 196616 | tf_op jit(solution)/shard_map/ppermute | solution.py:325
  24.6 6.3 %collective-permute-start.7 = (bf16[2,128,128]{2,1,0:T(8,128)(2,1)S(1)}, bf16[2,128,128]{2,1,0:T(8,128)(2,1)S(1)}, u32[]{:S(2)}, u32[]{:S(2)}) collective-permute-start(bf16[2,128,128]{2,1,0:T(8,128)(2,1)S(1)} %get-tuple-element.97), channel_id=1, source_target_pairs={{0,160},{4,164},{8,168},{12,172},{16,176},{20,180},{24,184},{28,18... | collective-permute-start | bytes 196616 | tf_op jit(solution)/shard_map/ppermute | solution.py:325
  31.1 8.2 %collective-permute-start.8 = (bf16[2,128,128]{2,1,0:T(8,128)(2,1)S(1)}, bf16[2,128,128]{2,1,0:T(8,128)(2,1)S(1)}, u32[]{:S(2)}, u32[]{:S(2)}) collective-permute-start(bf16[2,128,128]{2,1,0:T(8,128)(2,1)S(1)} %broadcast_select_fusion.4), channel_id=1, source_target_pairs={{0,4},{4,0},{8,12},{12,8},{16,20},{20,16},{24,28},{28,24},{32,36},... | collective-permute-start | bytes 196616 | tf_op jit(solution)/shard_map/ppermute | solution.py:325
  38.2 1.2 %copy-start.3 = (bf16[1024,512]{1,0:T(8,128)(2,1)S(1)}, bf16[1024,512]{1,0:T(8,128)(2,1)}, u32[]{:S(2)}) copy-start(bf16[1024,512]{1,0:T(8,128)(2,1)} %y_ref.1) | copy-start | bytes 3145732
  38.3 1.2 %copy-start.4 = (f32[512]{0:T(512)S(1)}, f32[512]{0:T(512)}, u32[]{:S(2)}) copy-start(f32[512]{0:T(512)} %param.9) | copy-start | bytes 6148
  41.0 4.5 %collective-permute-start.11 = (f32[2,1024]{1,0:T(2,128)S(1)}, f32[2,1024]{1,0:T(2,128)S(1)}, u32[]{:S(2)}, u32[]{:S(2)}) collective-permute-start(f32[2,1024]{1,0:T(2,128)S(1)} %get-tuple-element.61.s0), channel_id=1, source_target_pairs={{0,2},{1,3},{2,0},{3,1},{4,6},{5,7},{6,4},{7,5},{8,10},{9,11},{10,... | collective-permute-start | bytes 24584 | tf_op jit(solution)/shard_map/ppermute | solution.py:359
  44.0 2.5 %collective-permute-start.10 = (f32[2,1024]{1,0:T(2,128)S(1)}, f32[2,1024]{1,0:T(2,128)S(1)}, u32[]{:S(2)}, u32[]{:S(2)}) collective-permute-start(f32[2,1024]{1,0:T(2,128)S(1)} %get-tuple-element.61.s0), channel_id=1, source_target_pairs={{0,3},{1,0},{2,1},{3,2},{4,7},{5,4},{6,5},{7,6},{8,11},{9,8},{10,9... | collective-permute-start | bytes 24584 | tf_op jit(solution)/shard_map/ppermute | solution.py:359
  44.8 3.7 %collective-permute-start.9 = (f32[2,1024]{1,0:T(2,128)S(1)}, f32[2,1024]{1,0:T(2,128)S(1)}, u32[]{:S(2)}, u32[]{:S(2)}) collective-permute-start(f32[2,1024]{1,0:T(2,128)S(1)} %get-tuple-element.61.s0), channel_id=1, source_target_pairs={{0,1},{1,2},{2,3},{3,0},{4,5},{5,6},{6,7},{7,4},{8,9},{9,10},{10,1... | collective-permute-start | bytes 24584 | tf_op jit(solution)/shard_map/ppermute | solution.py:359
  51.4 2.7 %collective-permute-start.12 = (bf16[2,128,128]{2,1,0:T(8,128)(2,1)S(1)}, bf16[2,128,128]{2,1,0:T(8,128)(2,1)S(1)}, u32[]{:S(2)}, u32[]{:S(2)}) collective-permute-start(bf16[2,128,128]{2,1,0:T(8,128)(2,1)S(1)} %broadcast_select_fusion.2), channel_id=1, source_target_pairs={{252,248},{248,252},{244,240},{240,244},{236,232},{232,236},{228,2... | collective-permute-start | bytes 196616 | tf_op jit(solution)/shard_map/ppermute | solution.py:325
  54.1 7.2 %collective-permute-start.15 = (bf16[2,128,128]{2,1,0:T(8,128)(2,1)S(1)}, bf16[2,128,128]{2,1,0:T(8,128)(2,1)S(1)}, u32[]{:S(2)}, u32[]{:S(2)}) collective-permute-start(bf16[2,128,128]{2,1,0:T(8,128)(2,1)S(1)} %add_convert_fusion.1), channel_id=1, source_target_pairs={{252,236},{248,232},{244,228},{240,224},{236,252},{232,248},{228,2... | collective-permute-start | bytes 196616 | tf_op jit(solution)/shard_map/ppermute | solution.py:325
  54.9 6.4 %collective-permute-start.14 = (bf16[2,128,128]{2,1,0:T(8,128)(2,1)S(1)}, bf16[2,128,128]{2,1,0:T(8,128)(2,1)S(1)}, u32[]{:S(2)}, u32[]{:S(2)}) collective-permute-start(bf16[2,128,128]{2,1,0:T(8,128)(2,1)S(1)} %add_convert_fusion.1), channel_id=1, source_target_pairs={{252,228},{248,224},{244,252},{240,248},{236,244},{232,240},{228,2... | collective-permute-start | bytes 196616 | tf_op jit(solution)/shard_map/ppermute | solution.py:325
  55.3 6.0 %collective-permute-start.13 = (bf16[2,128,128]{2,1,0:T(8,128)(2,1)S(1)}, bf16[2,128,128]{2,1,0:T(8,128)(2,1)S(1)}, u32[]{:S(2)}, u32[]{:S(2)}) collective-permute-start(bf16[2,128,128]{2,1,0:T(8,128)(2,1)S(1)} %add_convert_fusion.1), channel_id=1, source_target_pairs={{252,244},{248,240},{244,236},{240,232},{236,228},{232,224},{228,2... | collective-permute-start | bytes 196616 | tf_op jit(solution)/shard_map/ppermute | solution.py:325
  61.4 6.5 %collective-permute-start.17 = (bf16[2,128,128]{2,1,0:T(8,128)(2,1)S(1)}, bf16[2,128,128]{2,1,0:T(8,128)(2,1)S(1)}, u32[]{:S(2)}, u32[]{:S(2)}) collective-permute-start(bf16[2,128,128]{2,1,0:T(8,128)(2,1)S(1)} %fusion.21), channel_id=1, source_target_pairs={{252,28},{248,24},{244,20},{240,16},{236,12},{232,8},{228,4},{224,... | collective-permute-start | bytes 196616 | tf_op jit(solution)/shard_map/ppermute | solution.py:325
  63.1 4.8 %collective-permute-start.16 = (bf16[2,128,128]{2,1,0:T(8,128)(2,1)S(1)}, bf16[2,128,128]{2,1,0:T(8,128)(2,1)S(1)}, u32[]{:S(2)}, u32[]{:S(2)}) collective-permute-start(bf16[2,128,128]{2,1,0:T(8,128)(2,1)S(1)} %fusion.21), channel_id=1, source_target_pairs={{252,220},{248,216},{244,212},{240,208},{236,204},{232,200},{228,1... | collective-permute-start | bytes 196616 | tf_op jit(solution)/shard_map/ppermute | solution.py:325
  68.0 7.3 %collective-permute-start.18 = (bf16[2,128,128]{2,1,0:T(8,128)(2,1)S(1)}, bf16[2,128,128]{2,1,0:T(8,128)(2,1)S(1)}, u32[]{:S(2)}, u32[]{:S(2)}) collective-permute-start(bf16[2,128,128]{2,1,0:T(8,128)(2,1)S(1)} %get-tuple-element.94), channel_id=1, source_target_pairs={{252,156},{248,152},{244,148},{240,144},{236,140},{232,136},{228,1... | collective-permute-start | bytes 196616 | tf_op jit(solution)/shard_map/ppermute | solution.py:325
  71.5 7.6 %collective-permute-start.19 = (bf16[2,128,128]{2,1,0:T(8,128)(2,1)S(1)}, bf16[2,128,128]{2,1,0:T(8,128)(2,1)S(1)}, u32[]{:S(2)}, u32[]{:S(2)}) collective-permute-start(bf16[2,128,128]{2,1,0:T(8,128)(2,1)S(1)} %get-tuple-element.95), channel_id=1, source_target_pairs={{252,92},{248,88},{244,84},{240,80},{236,76},{232,72},{228,68},{22... | collective-permute-start | bytes 196616 | tf_op jit(solution)/shard_map/ppermute | solution.py:325
  79.3 5.5 %collective-permute-start.20 = (bf16[2,128,128]{2,1,0:T(8,128)(2,1)S(1)}, bf16[2,128,128]{2,1,0:T(8,128)(2,1)S(1)}, u32[]{:S(2)}, u32[]{:S(2)}) collective-permute-start(bf16[2,128,128]{2,1,0:T(8,128)(2,1)S(1)} %broadcast_select_fusion), channel_id=1, source_target_pairs={{252,248},{248,252},{244,240},{240,244},{236,232},{232,236},{228,2... | collective-permute-start | bytes 196616 | tf_op jit(solution)/shard_map/ppermute | solution.py:325

commit v3 on v2

v3 whole, which is shorter than its diff:
```python
import functools

import jax
import jax.numpy as jnp
from jax import lax
from jax.experimental import pallas as pl
from jax.experimental.pallas import tpu as pltpu
from jax.sharding import PartitionSpec as P


HEAD_DIM = 128
WIDTH = 2048
epsilon = 1e-06
ROWS = 256

f32 = jnp.float32
bf16 = jnp.bfloat16


def nn(a, b):
    return lax.dot_general(a, b, (((1,), (0,)), ((), ())), preferred_element_type=f32)


def nt(a, b):
    return lax.dot_general(a, b, (((1,), (1,)), ((), ())), preferred_element_type=f32)


def tn(a, b):
    return lax.dot_general(a, b, (((0,), (0,)), ((), ())), preferred_element_type=f32)


def params(mib=24):
    return pltpu.CompilerParams(vmem_limit_bytes=mib << 20)


def cost(flops, nbytes):
    return pl.CostEstimate(flops=flops, bytes_accessed=nbytes, transcendentals=0)


VMEM = pl.BlockSpec(memory_space=pltpu.VMEM)
ANY = pl.BlockSpec(memory_space=pl.ANY)


def chunk(i):
    return slice(i * ROWS, (i + 1) * ROWS)


def outer_kernel(a_hbm, b_hbm, s_ref, a_ref, b_ref, sems):
    t, c = a_ref.shape
    n = t // ROWS
    copies = []
    for i in range(n):
        for hbm, ref in ((a_hbm, a_ref), (b_hbm, b_ref)):
            rows = pl.ds(i * ROWS, ROWS)
            copy = pltpu.make_async_copy(hbm.at[rows], ref.at[rows], sems.at[len(copies)])
            copy.start()
            copies.append(copy)
    total = [None] * (c // 256)
    for i in range(n):
        copies[2 * i].wait()
        copies[2 * i + 1].wait()
        for p in range(c // 256):
            cols = slice(p * 256, p * 256 + 256)
            x = tn(a_ref[chunk(i), cols], b_ref[chunk(i), cols])
            total[p] = x if i == 0 else total[p] + x
    for p in range(c // 256):
        s_ref[2 * p] = total[p][:128, :128].astype(bf16)
        s_ref[2 * p + 1] = total[p][128:, 128:].astype(bf16)


def block_state(a, b):
    t, c = a.shape
    heads = c // HEAD_DIM
    return pl.pallas_call(
        outer_kernel,
        in_specs=[ANY, ANY],
        out_specs=VMEM,
        out_shape=jax.ShapeDtypeStruct((heads, 128, 128), bf16),
        scratch_shapes=[
            pltpu.VMEM((t, c), bf16),
            pltpu.VMEM((t, c), bf16),
            pltpu.SemaphoreType.DMA((2 * t // ROWS,)),
        ],
        compiler_params=params(8),
        cost_estimate=cost(2 * t * c * 256, 2 * t * c * 2),
        name="block_state",
    )(a, b)


def masked(x, upper=False):
    row = lax.broadcasted_iota(jnp.int32, x.shape, 0)
    col = lax.broadcasted_iota(jnp.int32, x.shape, 1)
    return jnp.where((row <= col) if upper else (row >= col), x, 0.0).astype(bf16)


def local_kernel(head, q_ref, k_ref, v_ref, o_ref):
    t = q_ref.shape[0]
    cols = slice(head * HEAD_DIM, (head + 1) * HEAD_DIM)
    for r in range(0, t, ROWS):
        q = q_ref[r : r + ROWS, cols]
        w = masked(nt(q, k_ref[r : r + ROWS, cols]))
        o = nn(w, v_ref[r : r + ROWS, cols])
        if r:
            w = nt(q, k_ref[:r, cols]).astype(bf16)
            o = o + nn(w, v_ref[:r, cols])
        o_ref[r : r + ROWS, :] = o


def local_attn(q, k, v, head):
    t = q.shape[0]
    return pl.pallas_call(
        functools.partial(local_kernel, head),
        in_specs=[VMEM] * 3,
        out_specs=VMEM,
        out_shape=jax.ShapeDtypeStruct((t, HEAD_DIM), f32),
        compiler_params=params(8),
        cost_estimate=cost(2 * 2 * t * t * HEAD_DIM * 5 // 8, t * HEAD_DIM * 10),
        name="local_attn",
    )(q, k, v)


def column(row):
    return jnp.broadcast_to(row, (128, row.shape[1])).T


def attn_kernel(*refs):
    n = len(refs) - 6
    o_refs = refs[:n]
    q_ref, p_ref, y_ref, g_ref, attn_ref, stat_ref = refs[n:]
    t, c = q_ref.shape
    w = o_refs[0].shape[1]
    for i in range(t // ROWS):
        rows = chunk(i)
        squares = dots = 0.0
        for at in range(0, c, HEAD_DIM):
            cols = slice(at, at + HEAD_DIM)
            own = o_refs[at // w][rows, at % w : at % w + HEAD_DIM]
            attn = own + nn(q_ref[rows, cols], p_ref[at // HEAD_DIM])
            attn_ref[rows, cols] = attn
            squares = squares + attn * attn
            dots = dots + y_ref[rows, cols].astype(f32) * g_ref[:, cols] * attn
        stat_ref[0:1, rows] = jnp.sum(squares.T, axis=0, keepdims=True)
        stat_ref[1:2, rows] = jnp.sum(dots.T, axis=0, keepdims=True)


def attn_stats(locals_, q, prefix, y, gain):
    t, c = q.shape
    return pl.pallas_call(
        attn_kernel,
        in_specs=[VMEM] * (len(locals_) + 4),
        out_specs=(VMEM, VMEM),
        out_shape=(jax.ShapeDtypeStruct((t, c), f32), jax.ShapeDtypeStruct((2, t), f32)),
        compiler_params=params(8),
        cost_estimate=cost(2 * t * c * 128, t * c * 12),
        name="attn_stats",
    )(*locals_, q, prefix, y, gain)


def grad_kernel(attn_ref, y_ref, q_ref, s0, s1, s2, s3, g_ref, mixed_hbm, d_ref, term_ref, m_ref, sems):
    t, c = q_ref.shape
    stat = (s0[...] + s1[...]) + (s2[...] + s3[...])
    inv_row = lax.rsqrt(stat[0:1, :] / WIDTH + epsilon)
    scale_row = inv_row * inv_row * stat[1:2, :] / WIDTH
    total = [None] * (c // 256)
    copies = []
    for i in range(t // ROWS):
        rows = chunk(i)
        inv = column(inv_row[:, rows])
        scale = column(scale_row[:, rows])
        for at in range(0, c, HEAD_DIM):
            cols = slice(at, at + HEAD_DIM)
            attn = attn_ref[rows, cols]
            gain = g_ref[:, cols]
            m_ref[rows, cols] = (attn * inv * gain).astype(bf16)
            up = y_ref[rows, cols].astype(f32) * gain
            d_ref[rows, cols] = (inv * (up - attn * scale)).astype(bf16)
        copies.append(
            pltpu.make_async_copy(
                m_ref.at[pl.ds(i * ROWS, ROWS)], mixed_hbm.at[pl.ds(i * ROWS, ROWS)], sems.at[i]
            )
        )
        copies[-1].start()
        for p in range(c // 256):
            cols = slice(p * 256, p * 256 + 256)
            x = tn(q_ref[rows, cols], d_ref[rows, cols])
            total[p] = x if i == 0 else total[p] + x
    for p in range(c // 256):
        term_ref[2 * p] = total[p][:128, :128].astype(bf16)
        term_ref[2 * p + 1] = total[p][128:, 128:].astype(bf16)
    for copy in copies:
        copy.wait()


def grads_of_norm(attn, y, q, stats, gain):
    t, c = q.shape
    heads = c // HEAD_DIM
    return pl.pallas_call(
        grad_kernel,
        in_specs=[VMEM] * 8,
        out_specs=(ANY, VMEM, VMEM),
        out_shape=(
            jax.ShapeDtypeStruct((t, c), bf16),
            jax.ShapeDtypeStruct((t, c), bf16),
            jax.ShapeDtypeStruct((heads, 128, 128), bf16),
        ),
        scratch_shapes=[pltpu.VMEM((t, c), bf16), pltpu.SemaphoreType.DMA((t // ROWS,))],
        compiler_params=params(8),
        cost_estimate=cost(2 * t * c * 256, t * c * 12),
        name="grads_of_norm",
    )(attn, y, q, *stats, gain)


def back_kernel(head, q_ref, k_ref, v_ref, d_ref, p_ref, *refs):
    dq_hbm, dk_ref, dv_ref, dq_ref, sems = refs[-5:]
    t = q_ref.shape[0]
    cols = slice(head * HEAD_DIM, (head + 1) * HEAD_DIM)
    copies = []
    for i in range(t // ROWS):
        r, e = i * ROWS, (i + 1) * ROWS
        here = slice(r, e)
        q, k, v, d = q_ref[here, cols], k_ref[here, cols], v_ref[here, cols], d_ref[here, cols]
        dq = nt(d, p_ref[head]) + nn(masked(nt(d, v)), k)
        if r:
            dq = dq + nn(nt(d, v_ref[:r, cols]).astype(bf16), k_ref[:r, cols])
        dq_ref[here, :] = dq.astype(bf16)
        there = pl.ds(r, ROWS)
        copies.append(
            pltpu.make_async_copy(
                dq_ref.at[there], dq_hbm.at[there, pl.ds(head * HEAD_DIM, HEAD_DIM)], sems.at[i]
            )
        )
        copies[-1].start()
        dk = nn(masked(nt(v, d), True), q)
        dv = nn(masked(nt(k, q), True), d)
        if e < t:
            dk = dk + nn(nt(v, d_ref[e:, cols]).astype(bf16), q_ref[e:, cols])
            dv = dv + nn(nt(k, q_ref[e:, cols]).astype(bf16), d_ref[e:, cols])
        dk_ref[here, :] = dk
        dv_ref[here, :] = dv
    for copy in copies:
        copy.wait()


def local_back(q, k, v, d, prefix, dq, head):
    t, c = q.shape
    held = [] if dq is None else [dq]
    return pl.pallas_call(
        functools.partial(back_kernel, head),
        in_specs=[VMEM] * 5 + [ANY] * len(held),
        out_specs=(ANY, VMEM, VMEM),
        input_output_aliases={5: 0} if held else {},
        out_shape=(
            jax.ShapeDtypeStruct((t, c), bf16),
            jax.ShapeDtypeStruct((t, HEAD_DIM), f32),
            jax.ShapeDtypeStruct((t, HEAD_DIM), f32),
        ),
        scratch_shapes=[
            pltpu.VMEM((t, HEAD_DIM), bf16),
            pltpu.SemaphoreType.DMA((t // ROWS,)),
        ],
        compiler_params=params(8),
        cost_estimate=cost(6 * 2 * t * t * HEAD_DIM * 5 // 8, t * HEAD_DIM * 18),
        name="local_back",
    )(q, k, v, d, prefix, *held)


def final_kernel(*refs):
    n = (len(refs) - 8) // 2
    dk_refs, dv_refs = refs[:n], refs[n : 2 * n]
    k_ref, v_ref, s_ref, ok_hbm, ov_hbm, ok_ref, ov_ref, sems = refs[2 * n :]
    t, c = k_ref.shape
    w = dk_refs[0].shape[1]
    copies = []
    for i in range(t // ROWS):
        rows = chunk(i)
        for at in range(0, c, HEAD_DIM):
            cols = slice(at, at + HEAD_DIM)
            h = at // HEAD_DIM
            part = slice(at % w, at % w + HEAD_DIM)
            ok_ref[rows, cols] = (dk_refs[at // w][rows, part] + nt(v_ref[rows, cols], s_ref[h])).astype(bf16)
            ov_ref[rows, cols] = (dv_refs[at // w][rows, part] + nn(k_ref[rows, cols], s_ref[h])).astype(bf16)
        for ref, hbm in ((ok_ref, ok_hbm), (ov_ref, ov_hbm)):
            there = pl.ds(i * ROWS, ROWS)
            copies.append(pltpu.make_async_copy(ref.at[there], hbm.at[there], sems.at[len(copies)]))
            copies[-1].start()
    for copy in copies:
        copy.wait()


def finish(dks, dvs, k, v, suffix):
    t, c = k.shape
    return pl.pallas_call(
        final_kernel,
        in_specs=[VMEM] * (2 * len(dks) + 3),
        out_specs=(ANY, ANY),
        out_shape=(jax.ShapeDtypeStruct((t, c), bf16),) * 2,
        scratch_shapes=[
            pltpu.VMEM((t, c), bf16),
            pltpu.VMEM((t, c), bf16),
            pltpu.SemaphoreType.DMA((2 * t // ROWS,)),
        ],
        compiler_params=params(8),
        cost_estimate=cost(4 * t * c * 128, t * c * 16),
        name="finish",
    )(*dks, *dvs, k, v, suffix)


NZ, NX = 8, 4


def step_pairs(reverse, dz=0, dx=0, swap=False):
    pairs = []
    for i in range(NZ * NX * 2):
        z, x, c = i // 8, (i // 2) % 4, i % 2
        j = ((z + dz) % NZ * NX + (x + dx) % NX) * 2 + (1 - c if swap else c)
        pairs.append((63 - i, 63 - j) if reverse else (i, j))
    return pairs


def places(reverse):
    index = lax.axis_index("seq")
    index = 63 - index if reverse else index
    z, x, c = index >> 3, (index >> 1) & 3, index & 1
    low, high = (z + 7) & 7, (z + 1) & 7
    up, down = (z + 3) & 7, (z + 5) & 7
    return (
        c == 0,
        tuple(x >= k for k in (1, 2, 3)),
        z >= 1,
        z == 7,
        (low < up, z < up, high < up),
        (low < down, z < down),
    )


def exclusive_sum(own, reverse, masks):
    def send(a, **step):
        return lax.ppermute(a, "seq", step_pairs(reverse, **step))

    first, west, south, north, up, down = masks
    n = own.shape[0] // 2
    mine = jnp.where(first, own[:n], own[n:])
    other = jnp.where(first, own[n:], own[:n])
    got = send(other, swap=True)
    chip = (mine.astype(f32) + got.astype(f32)).astype(bf16)
    row = chip.astype(f32)
    before = jnp.zeros_like(row)
    for k in (1, 3, 2):
        r = send(chip, dx=k).astype(f32)
        row = row + r
        before = before + jnp.where(west[k - 1], r, 0.0)
    plane = row.astype(bf16)
    below = send(plane, dz=1).astype(f32)
    above = send(plane, dz=-1).astype(f32)
    near = jnp.where(south, below, 0.0) + jnp.where(north, above, 0.0)

    def lacking(flags):
        return sum(jnp.where(m, p, 0.0) for m, p in zip(flags, (below, row, above))).astype(bf16)

    far = send(lacking(up), dz=3).astype(f32)
    far = far + send(lacking(down), dz=-3).astype(f32)
    e0 = before + near + far
    e1 = e0 + jnp.where(first, mine, got).astype(f32)
    e0, e1 = e0.astype(bf16), e1.astype(bf16)
    keep = jnp.where(first, e0, e1)
    back = send(jnp.where(first, e1, e0), swap=True)
    return jnp.where(first, jnp.concatenate([keep, back]), jnp.concatenate([back, keep]))


def head_parts(a):
    return [a] + [
        lax.ppermute(a, "head", [(i, (i + k) % 4) for i in range(4)]) for k in (1, 3, 2)
    ]


PARTS = 4


def shards(q, k, v, y, gain):
    gain = gain[None, :]
    first, last = places(False), places(True)
    first, last, k, v = lax.optimization_barrier((first, last, k, v))
    in_hbm = [pltpu.with_memory_space_constraint(a, pltpu.HBM) for a in (k, v)]
    prefix = exclusive_sum(block_state(*in_hbm), False, first)
    locals_ = []
    for i in range(PARTS):
        locals_.append(local_attn(q, k, v, i))
    attn, stats = attn_stats(locals_, q, prefix, y, gain)
    mixed, d, term = grads_of_norm(attn, y, q, head_parts(stats), gain)
    suffix = exclusive_sum(term, True, last)
    dq, dks, dvs = None, [], []
    for i in range(PARTS):
        dq, dk, dv = local_back(q, k, v, d, prefix, dq, i)
        dks.append(dk)
        dvs.append(dv)
    dk, dv = finish(dks, dvs, k, v, suffix)
    return mixed, dq, dk, dv


def solution(mesh):
    wide = P("seq", "head")
    return jax.shard_map(
        shards,
        mesh=mesh,
        in_specs=(wide, wide, wide, wide, P("head")),
        out_specs=(wide, wide, wide, wide),
        check_vma=False,
    )
```

time: 87.4 us -> 83.5 us (0.955)
  Pallas kernels: 29.4 us -> 25.1 us
    pallas_call x12, Pallas kernels: 29.4 us -> 25.1 us  [the longest x4 14.5 us: local_back(): pl.pallas_call(functools.partial(back_kernel, head), in_specs=[VMEM] * 5...]
where the time goes in v3:
time: 83.5 us; the launch traced here: 83.4 us
  starting transfers between devices  38.7 us (46%)
  Pallas kernels  25.1 us (30%)
  waiting for transfers between devices  17.6 us (21%)
  between operations  1.15 us (1%)
    ppermute x18, starting transfers between devices, send(): return lax.ppermute(a, 'seq', step_pairs(reverse, **step))  34.1 us
    ppermute x18, waiting for transfers between devices, send(): return lax.ppermute(a, 'seq', step_pairs(reverse, **step))  14.6 us
    pallas_call x4, Pallas kernels, local_back(): pl.pallas_call(functools.partial(back_kernel, head), in_specs=[VMEM] * 5...  14.5 us
    ppermute x3, starting transfers between devices, head_parts(): lax.ppermute(a, 'head', [(i, (i + k) % 4) for i in range(4)])  4.64 us
    pallas_call x4, Pallas kernels, local_attn(): pl.pallas_call(functools.partial(local_kernel, head), in_specs=[VMEM] * 3...  4.22 us
    ppermute x3, waiting for transfers between devices, head_parts(): lax.ppermute(a, 'head', [(i, (i + k) % 4) for i in range(4)])  3.03 us
    pallas_call x1, Pallas kernels, block_state(): pl.pallas_call(outer_kernel, in_specs=[ANY, ANY], out_specs=VMEM, out_sha...  2.07 us
    pallas_call x1, Pallas kernels, grads_of_norm(): pl.pallas_call(grad_kernel, in_specs=[VMEM] * 8, out_specs=(ANY, VMEM, VM...  1.72 us
  transfers between devices with their start and end apart: 21, of which 11 were waited for; matrix products, arithmetic and copies ran while one was open for 0% of the time, Pallas kernels for 22%

profile of v3, /device:TPU:1, one launch (start us, length us, event | category | flops | bytes accessed | tf_op | source)
XLA Modules:
  0.0 83.4 jit_solution(18265982217746421766)
XLA Ops:
  0.7 2.1 %block_state.1 = bf16[4,128,128]{2,1,0:T(8,128)(2,1)S(1)} custom-call(bf16[1024,512]{1,0:T(8,128)(2,1)} %refs_8_, bf16[1024,512]{1,0:T(8,128)(2,1)} %refs_9_), custom_call_target="tpu_custom_call" | custom-call | flops 268435456 | bytes 2097152 | tf_op jit(solution)/shard_map/block_state/pallas_call | solution.py:74
  2.8 3.3 %collective-permute-start = (bf16[2,128,128]{2,1,0:T(8,128)(2,1)S(1)}, bf16[2,128,128]{2,1,0:T(8,128)(2,1)S(1)}, u32[]{:S(2)}, u32[]{:S(2)}) collective-permute-start(bf16[2,128,128]{2,1,0:T(8,128)(2,1)S(1)} %broadcast_select_fusion.6), channel_id=1, source_target_pairs={{0,4},{4,0},{8,12},{12,8},{16,20},{20,16},{24,28},{28,24},{32,36},... | collective-permute-start | bytes 196616 | tf_op jit(solution)/shard_map/ppermute | solution.py:338
  6.1 0.9 %collective-permute-done = bf16[2,128,128]{2,1,0:T(8,128)(2,1)S(1)} collective-permute-done((bf16[2,128,128]{2,1,0:T(8,128)(2,1)S(1)}, bf16[2,128,128]{2,1,0:T(8,128)(2,1)S(1)}, u32[]{:S(2)}, u32[]{:S(2)}) %collective-permute-start) | collective-permute-done | bytes 65568 | tf_op jit(solution)/shard_map/ppermute | solution.py:338
  7.0 1.1 %collective-permute-start.3 = (bf16[2,128,128]{2,1,0:T(8,128)(2,1)S(1)}, bf16[2,128,128]{2,1,0:T(8,128)(2,1)S(1)}, u32[]{:S(2)}, u32[]{:S(2)}) collective-permute-start(bf16[2,128,128]{2,1,0:T(8,128)(2,1)S(1)} %add_convert_fusion.3), channel_id=1, source_target_pairs={{0,16},{4,20},{8,24},{12,28},{16,0},{20,4},{24,8},{28,12},{32,48},... | collective-permute-start | bytes 196616 | tf_op jit(solution)/shard_map/ppermute | solution.py:338
  8.2 0.9 %collective-permute-start.2 = (bf16[2,128,128]{2,1,0:T(8,128)(2,1)S(1)}, bf16[2,128,128]{2,1,0:T(8,128)(2,1)S(1)}, u32[]{:S(2)}, u32[]{:S(2)}) collective-permute-start(bf16[2,128,128]{2,1,0:T(8,128)(2,1)S(1)} %add_convert_fusion.3), channel_id=1, source_target_pairs={{0,24},{4,28},{8,0},{12,4},{16,8},{20,12},{24,16},{28,20},{32,56},... | collective-permute-start | bytes 196616 | tf_op jit(solution)/shard_map/ppermute | solution.py:338
  9.0 0.6 collective-permute-start.1
  9.6 2.1 %collective-permute-done.3 = bf16[2,128,128]{2,1,0:T(8,128)(2,1)S(1)} collective-permute-done((bf16[2,128,128]{2,1,0:T(8,128)(2,1)S(1)}, bf16[2,128,128]{2,1,0:T(8,128)(2,1)S(1)}, u32[]{:S(2)}, u32[]{:S(2)}) %collective-permute-start.3) | collective-permute-done | bytes 65568 | tf_op jit(solution)/shard_map/ppermute | solution.py:338
  11.8 0.2 collective-permute-done.2
  11.9 1.4 %collective-permute-done.1 = bf16[2,128,128]{2,1,0:T(8,128)(2,1)S(1)} collective-permute-done((bf16[2,128,128]{2,1,0:T(8,128)(2,1)S(1)}, bf16[2,128,128]{2,1,0:T(8,128)(2,1)S(1)}, u32[]{:S(2)}, u32[]{:S(2)}) %collective-permute-start.1) | collective-permute-done | bytes 65568 | tf_op jit(solution)/shard_map/ppermute | solution.py:338
  13.4 5.7 %collective-permute-start.5 = (bf16[2,128,128]{2,1,0:T(8,128)(2,1)S(1)}, bf16[2,128,128]{2,1,0:T(8,128)(2,1)S(1)}, u32[]{:S(2)}, u32[]{:S(2)}) collective-permute-start(bf16[2,128,128]{2,1,0:T(8,128)(2,1)S(1)} %fusion.20), channel_id=1, source_target_pairs={{0,224},{4,228},{8,232},{12,236},{16,240},{20,244},{24,248},{28,25... | collective-permute-start | bytes 196616 | tf_op jit(solution)/shard_map/ppermute | solution.py:338
  19.1 1.3 %collective-permute-done.5 = bf16[2,128,128]{2,1,0:T(8,128)(2,1)S(1)} collective-permute-done((bf16[2,128,128]{2,1,0:T(8,128)(2,1)S(1)}, bf16[2,128,128]{2,1,0:T(8,128)(2,1)S(1)}, u32[]{:S(2)}, u32[]{:S(2)}) %collective-permute-start.5) | collective-permute-done | bytes 65568 | tf_op jit(solution)/shard_map/ppermute | solution.py:338
  20.4 3.0 %collective-permute-done.4 = bf16[2,128,128]{2,1,0:T(8,128)(2,1)S(1)} collective-permute-done((bf16[2,128,128]{2,1,0:T(8,128)(2,1)S(1)}, bf16[2,128,128]{2,1,0:T(8,128)(2,1)S(1)}, u32[]{:S(2)}, u32[]{:S(2)}) %collective-permute-start.4) | collective-permute-done | bytes 65568 | tf_op jit(solution)/shard_map/ppermute | solution.py:338
  23.4 0.1 fusion.6
  23.5 0.1 collective-permute-start.6
  23.6 4.5 %collective-permute-start.7 = (bf16[2,128,128]{2,1,0:T(8,128)(2,1)S(1)}, bf16[2,128,128]{2,1,0:T(8,128)(2,1)S(1)}, u32[]{:S(2)}, u32[]{:S(2)}) collective-permute-start(bf16[2,128,128]{2,1,0:T(8,128)(2,1)S(1)} %get-tuple-element.97), channel_id=1, source_target_pairs={{0,160},{4,164},{8,168},{12,172},{16,176},{20,180},{24,184},{28,18... | collective-permute-start | bytes 196616 | tf_op jit(solution)/shard_map/ppermute | solution.py:338
  28.0 1.1 %local_attn.7.refs_3_ = f32[1024,128]{1,0:T(8,128)S(1)} custom-call(bf16[1024,512]{1,0:T(8,128)(2,1)S(1)} %copy-done.2, bf16[1024,512]{1,0:T(8,128)(2,1)S(1)} %copy-done, bf16[1024,512]{1,0:T(8,128)(2,1)S(1)} %copy-done.1), custom_call_target="tpu_custom_call" | custom-call | flops 335544320 | bytes 1310720 | tf_op jit(solution)/shard_map/local_attn/pallas_call | solution.py:111
  29.1 0.8 collective-permute-done.6
  29.9 0.1 broadcast_select_fusion.5
  30.1 4.9 %collective-permute-start.8 = (bf16[2,128,128]{2,1,0:T(8,128)(2,1)S(1)}, bf16[2,128,128]{2,1,0:T(8,128)(2,1)S(1)}, u32[]{:S(2)}, u32[]{:S(2)}) collective-permute-start(bf16[2,128,128]{2,1,0:T(8,128)(2,1)S(1)} %broadcast_select_fusion.4), channel_id=1, source_target_pairs={{0,4},{4,0},{8,12},{12,8},{16,20},{20,16},{24,28},{28,24},{32,36},... | collective-permute-start | bytes 196616 | tf_op jit(solution)/shard_map/ppermute | solution.py:338
  35.0 1.1 %local_attn.6.refs_2_ = f32[1024,128]{1,0:T(8,128)S(1)} custom-call(bf16[1024,512]{1,0:T(8,128)(2,1)S(1)} %copy-done.2, bf16[1024,512]{1,0:T(8,128)(2,1)S(1)} %copy-done, bf16[1024,512]{1,0:T(8,128)(2,1)S(1)} %copy-done.1), custom_call_target="tpu_custom_call" | custom-call | flops 335544320 | bytes 1310720 | tf_op jit(solution)/shard_map/local_attn/pallas_call | solution.py:111
  36.0 1.1 %local_attn.5.refs_1_ = f32[1024,128]{1,0:T(8,128)S(1)} custom-call(bf16[1024,512]{1,0:T(8,128)(2,1)S(1)} %copy-done.2, bf16[1024,512]{1,0:T(8,128)(2,1)S(1)} %copy-done, bf16[1024,512]{1,0:T(8,128)(2,1)S(1)} %copy-done.1), custom_call_target="tpu_custom_call" | custom-call | flops 335544320 | bytes 1310720 | tf_op jit(solution)/shard_map/local_attn/pallas_call | solution.py:111
  37.1 1.1 %local_attn.4.refs_0_ = f32[1024,128]{1,0:T(8,128)S(1)} custom-call(bf16[1024,512]{1,0:T(8,128)(2,1)S(1)} %copy-done.2, bf16[1024,512]{1,0:T(8,128)(2,1)S(1)} %copy-done, bf16[1024,512]{1,0:T(8,128)(2,1)S(1)} %copy-done.1), custom_call_target="tpu_custom_call" | custom-call | flops 335544320 | bytes 1310720 | tf_op jit(solution)/shard_map/local_attn/pallas_call | solution.py:111
  38.2 0.1 copy-done.3
  38.3 0.9 %attn_stats.1 = (f32[1024,512]{1,0:T(8,128)S(1)}, f32[2,1024]{1,0:T(2,128)S(1)}) custom-call(f32[1024,128]{1,0:T(8,128)S(1)} %local_attn.4.refs_0_, f32[1024,128]{1,0:T(8,128)S(1)} %local_attn.5.refs_1_, f32[1024,128]{1,0:T(8,128)S(1)} %local_attn.6.refs_2_, f32[1024,128]{1,0:T(8,128)S(1)} %local_attn.7.refs_3_, bf16[1024,512]{1,0:T(8,128)(2,1)S(1)} %copy-done.2, ...), custom_call_target="tpu_custom_call" | custom-call | flops 134217728 | bytes 6291456 | tf_op jit(solution)/shard_map/attn_stats/pallas_call | solution.py:148
  39.2 3.2 %collective-permute-start.11 = (f32[2,1024]{1,0:T(2,128)S(1)}, f32[2,1024]{1,0:T(2,128)S(1)}, u32[]{:S(2)}, u32[]{:S(2)}) collective-permute-start(f32[2,1024]{1,0:T(2,128)S(1)} %get-tuple-element.61.s0), channel_id=1, source_target_pairs={{0,2},{1,3},{2,0},{3,1},{4,6},{5,7},{6,4},{7,5},{8,10},{9,11},{10,... | collective-permute-start | bytes 24584 | tf_op jit(solution)/shard_map/ppermute | solution.py:372
  42.3 0.8 collective-permute-start.10
  43.1 0.7 collective-permute-start.9
  43.8 1.0 %collective-permute-done.10.s2 = f32[2,1024]{1,0:T(2,128)S(1)} collective-permute-done((f32[2,1024]{1,0:T(2,128)S(1)}, f32[2,1024]{1,0:T(2,128)S(1)}, u32[]{:S(2)}, u32[]{:S(2)}) %collective-permute-start.10) | collective-permute-done | bytes 8224 | tf_op jit(solution)/shard_map/ppermute | solution.py:372
  44.9 2.0 %collective-permute-done.9.s1 = f32[2,1024]{1,0:T(2,128)S(1)} collective-permute-done((f32[2,1024]{1,0:T(2,128)S(1)}, f32[2,1024]{1,0:T(2,128)S(1)}, u32[]{:S(2)}, u32[]{:S(2)}) %collective-permute-start.9) | collective-permute-done | bytes 8224 | tf_op jit(solution)/shard_map/ppermute | solution.py:372
  46.8 1.7 %grads_of_norm.1 = (bf16[1024,512]{1,0:T(8,128)(2,1)}, bf16[1024,512]{1,0:T(8,128)(2,1)S(1)}, bf16[4,128,128]{2,1,0:T(8,128)(2,1)S(1)}) custom-call(f32[1024,512]{1,0:T(8,128)S(1)} %get-tuple-element.60.attn_ref, bf16[1024,512]{1,0:T(8,128)(2,1)S(1)} %copy-done.3, bf16[1024,512]{1,0:T(8,128)(2,1)S(1)} %copy-done.2, f32[2,1024]{1,0:T(2,128)S(1)} %get-tuple-element.61.s0, ...), custom_call_target="tpu_custom_call" | custom-call | flops 268435456 | bytes 6291456 | tf_op jit(solution)/shard_map/grads_of_norm/pallas_call | solution.py:197
  48.6 1.8 %collective-permute-start.12 = (bf16[2,128,128]{2,1,0:T(8,128)(2,1)S(1)}, bf16[2,128,128]{2,1,0:T(8,128)(2,1)S(1)}, u32[]{:S(2)}, u32[]{:S(2)}) collective-permute-start(bf16[2,128,128]{2,1,0:T(8,128)(2,1)S(1)} %broadcast_select_fusion.2), channel_id=1, source_target_pairs={{252,248},{248,252},{244,240},{240,244},{236,232},{232,236},{228,2... | collective-permute-start | bytes 196616 | tf_op jit(solution)/shard_map/ppermute | solution.py:338
  50.4 0.9 %collective-permute-done.12 = bf16[2,128,128]{2,1,0:T(8,128)(2,1)S(1)} collective-permute-done((bf16[2,128,128]{2,1,0:T(8,128)(2,1)S(1)}, bf16[2,128,128]{2,1,0:T(8,128)(2,1)S(1)}, u32[]{:S(2)}, u32[]{:S(2)}) %collective-permute-start.12) | collective-permute-done | bytes 65568 | tf_op jit(solution)/shard_map/ppermute | solution.py:338
  51.3 0.8 collective-permute-start.15
  52.1 0.4 collective-permute-start.14
  52.5 2.3 %collective-permute-start.13 = (bf16[2,128,128]{2,1,0:T(8,128)(2,1)S(1)}, bf16[2,128,128]{2,1,0:T(8,128)(2,1)S(1)}, u32[]{:S(2)}, u32[]{:S(2)}) collective-permute-start(bf16[2,128,128]{2,1,0:T(8,128)(2,1)S(1)} %add_convert_fusion.1), channel_id=1, source_target_pairs={{252,244},{248,240},{244,236},{240,232},{236,228},{232,224},{228,2... | collective-permute-start | bytes 196616 | tf_op jit(solution)/shard_map/ppermute | solution.py:338
  54.8 3.6 %local_back.4 = (bf16[1024,512]{1,0:T(8,128)(2,1)}, f32[1024,128]{1,0:T(8,128)S(1)}, f32[1024,128]{1,0:T(8,128)S(1)}) custom-call(bf16[1024,512]{1,0:T(8,128)(2,1)S(1)} %copy-done.2, bf16[1024,512]{1,0:T(8,128)(2,1)S(1)} %copy-done, bf16[1024,512]{1,0:T(8,128)(2,1)S(1)} %copy-done.1, bf16[1024,512]{1,0:T(8,128)(2,1)S(1)} %get-tuple-element.63.d_ref, ...), custom_call_target="tpu_custom_call" | custom-call | flops 1006632960 | bytes 2359296 | tf_op jit(solution)/shard_map/local_back/pallas_call | solution.py:247
  58.5 1.7 %collective-permute-start.17 = (bf16[2,128,128]{2,1,0:T(8,128)(2,1)S(1)}, bf16[2,128,128]{2,1,0:T(8,128)(2,1)S(1)}, u32[]{:S(2)}, u32[]{:S(2)}) collective-permute-start(bf16[2,128,128]{2,1,0:T(8,128)(2,1)S(1)} %fusion.21), channel_id=1, source_target_pairs={{252,28},{248,24},{244,20},{240,16},{236,12},{232,8},{228,4},{224,... | collective-permute-start | bytes 196616 | tf_op jit(solution)/shard_map/ppermute | solution.py:338
  60.2 1.0 %collective-permute-start.16 = (bf16[2,128,128]{2,1,0:T(8,128)(2,1)S(1)}, bf16[2,128,128]{2,1,0:T(8,128)(2,1)S(1)}, u32[]{:S(2)}, u32[]{:S(2)}) collective-permute-start(bf16[2,128,128]{2,1,0:T(8,128)(2,1)S(1)} %fusion.21), channel_id=1, source_target_pairs={{252,220},{248,216},{244,212},{240,208},{236,204},{232,200},{228,1... | collective-permute-start | bytes 196616 | tf_op jit(solution)/shard_map/ppermute | solution.py:338
  61.3 3.6 %local_back.5 = (bf16[1024,512]{1,0:T(8,128)(2,1)}, f32[1024,128]{1,0:T(8,128)S(1)}, f32[1024,128]{1,0:T(8,128)S(1)}) custom-call(bf16[1024,512]{1,0:T(8,128)(2,1)S(1)} %copy-done.2, bf16[1024,512]{1,0:T(8,128)(2,1)S(1)} %copy-done, bf16[1024,512]{1,0:T(8,128)(2,1)S(1)} %copy-done.1, ...), custom_call_target="tpu_custom_call", output_to_operand_aliasing={{0}: (5, {})} | custom-call | flops 1006632960 | bytes 2359296 | tf_op jit(solution)/shard_map/local_back/pallas_call | solution.py:247
  64.9 0.1 fusion.13
  65.0 3.3 %collective-permute-start.18 = (bf16[2,128,128]{2,1,0:T(8,128)(2,1)S(1)}, bf16[2,128,128]{2,1,0:T(8,128)(2,1)S(1)}, u32[]{:S(2)}, u32[]{:S(2)}) collective-permute-start(bf16[2,128,128]{2,1,0:T(8,128)(2,1)S(1)} %get-tuple-element.94), channel_id=1, source_target_pairs={{252,156},{248,152},{244,148},{240,144},{236,140},{232,136},{228,1... | collective-permute-start | bytes 196616 | tf_op jit(solution)/shard_map/ppermute | solution.py:338
  68.3 0.0 collective-permute-start.19
  68.4 3.6 %local_back.6 = (bf16[1024,512]{1,0:T(8,128)(2,1)}, f32[1024,128]{1,0:T(8,128)S(1)}, f32[1024,128]{1,0:T(8,128)S(1)}) custom-call(bf16[1024,512]{1,0:T(8,128)(2,1)S(1)} %copy-done.2, bf16[1024,512]{1,0:T(8,128)(2,1)S(1)} %copy-done, bf16[1024,512]{1,0:T(8,128)(2,1)S(1)} %copy-done.1, ...), custom_call_target="tpu_custom_call", output_to_operand_aliasing={{0}: (5, {})} | custom-call | flops 1006632960 | bytes 2359296 | tf_op jit(solution)/shard_map/local_back/pallas_call | solution.py:247
  72.0 3.9 %collective-permute-done.19 = bf16[2,128,128]{2,1,0:T(8,128)(2,1)S(1)} collective-permute-done((bf16[2,128,128]{2,1,0:T(8,128)(2,1)S(1)}, bf16[2,128,128]{2,1,0:T(8,128)(2,1)S(1)}, u32[]{:S(2)}, u32[]{:S(2)}) %collective-permute-start.19) | collective-permute-done | bytes 65568 | tf_op jit(solution)/shard_map/ppermute | solution.py:338
  75.9 0.1 broadcast_select_fusion.1
  76.1 1.8 %collective-permute-start.20 = (bf16[2,128,128]{2,1,0:T(8,128)(2,1)S(1)}, bf16[2,128,128]{2,1,0:T(8,128)(2,1)S(1)}, u32[]{:S(2)}, u32[]{:S(2)}) collective-permute-start(bf16[2,128,128]{2,1,0:T(8,128)(2,1)S(1)} %broadcast_select_fusion), channel_id=1, source_target_pairs={{252,248},{248,252},{244,240},{240,244},{236,232},{232,236},{228,2... | collective-permute-start | bytes 196616 | tf_op jit(solution)/shard_map/ppermute | solution.py:338
  77.9 3.6 %local_back.7 = (bf16[1024,512]{1,0:T(8,128)(2,1)}, f32[1024,128]{1,0:T(8,128)S(1)}, f32[1024,128]{1,0:T(8,128)S(1)}) custom-call(bf16[1024,512]{1,0:T(8,128)(2,1)S(1)} %copy-done.2, bf16[1024,512]{1,0:T(8,128)(2,1)S(1)} %copy-done, bf16[1024,512]{1,0:T(8,128)(2,1)S(1)} %copy-done.1, ...), custom_call_target="tpu_custom_call", output_to_operand_aliasing={{0}: (5, {})} | custom-call | flops 1006632960 | bytes 2359296 | tf_op jit(solution)/shard_map/local_back/pallas_call | solution.py:247
  81.6 1.7 %finish.1 = (bf16[1024,512]{1,0:T(8,128)(2,1)}, bf16[1024,512]{1,0:T(8,128)(2,1)}) custom-call(f32[1024,128]{1,0:T(8,128)S(1)} %get-tuple-element.68.refs_0_, f32[1024,128]{1,0:T(8,128)S(1)} %get-tuple-element.69.refs_1_, f32[1024,128]{1,0:T(8,128)S(1)} %get-tuple-element.70.refs_2_, f32[1024,128]{1,0:T(8,128)S(1)} %get-tuple-element.71.refs_3_, ...), custom_call_target="tpu_custom_call" | custom-call | flops 268435456 | bytes 8388608 | tf_op jit(solution)/shard_map/finish/pallas_call | solution.py:292
  (30 shorter events, 0.3 us)
Async XLA Ops:
  0.6 27.4 %copy-start.1 = (bf16[1024,512]{1,0:T(8,128)(2,1)S(1)}, bf16[1024,512]{1,0:T(8,128)(2,1)}, u32[]{:S(2)}) copy-start(bf16[1024,512]{1,0:T(8,128)(2,1)} %refs_9_) | copy-start | bytes 3145732
  0.6 27.4 %copy-start = (bf16[1024,512]{1,0:T(8,128)(2,1)S(1)}, bf16[1024,512]{1,0:T(8,128)(2,1)}, u32[]{:S(2)}) copy-start(bf16[1024,512]{1,0:T(8,128)(2,1)} %refs_8_) | copy-start | bytes 3145732
  0.7 27.4 %copy-start.2 = (bf16[1024,512]{1,0:T(8,128)(2,1)S(1)}, bf16[1024,512]{1,0:T(8,128)(2,1)}, u32[]{:S(2)}) copy-start(bf16[1024,512]{1,0:T(8,128)(2,1)} %q_ref.17) | copy-start | bytes 3145732
  2.8 4.2 %collective-permute-start = (bf16[2,128,128]{2,1,0:T(8,128)(2,1)S(1)}, bf16[2,128,128]{2,1,0:T(8,128)(2,1)S(1)}, u32[]{:S(2)}, u32[]{:S(2)}) collective-permute-start(bf16[2,128,128]{2,1,0:T(8,128)(2,1)S(1)} %broadcast_select_fusion.6), channel_id=1, source_target_pairs={{0,4},{4,0},{8,12},{12,8},{16,20},{20,16},{24,28},{28,24},{32,36},... | collective-permute-start | bytes 196616 | tf_op jit(solution)/shard_map/ppermute | solution.py:338
  7.0 4.7 %collective-permute-start.3 = (bf16[2,128,128]{2,1,0:T(8,128)(2,1)S(1)}, bf16[2,128,128]{2,1,0:T(8,128)(2,1)S(1)}, u32[]{:S(2)}, u32[]{:S(2)}) collective-permute-start(bf16[2,128,128]{2,1,0:T(8,128)(2,1)S(1)} %add_convert_fusion.3), channel_id=1, source_target_pairs={{0,16},{4,20},{8,24},{12,28},{16,0},{20,4},{24,8},{28,12},{32,48},... | collective-permute-start | bytes 196616 | tf_op jit(solution)/shard_map/ppermute | solution.py:338
  8.2 3.8 %collective-permute-start.2 = (bf16[2,128,128]{2,1,0:T(8,128)(2,1)S(1)}, bf16[2,128,128]{2,1,0:T(8,128)(2,1)S(1)}, u32[]{:S(2)}, u32[]{:S(2)}) collective-permute-start(bf16[2,128,128]{2,1,0:T(8,128)(2,1)S(1)} %add_convert_fusion.3), channel_id=1, source_target_pairs={{0,24},{4,28},{8,0},{12,4},{16,8},{20,12},{24,16},{28,20},{32,56},... | collective-permute-start | bytes 196616 | tf_op jit(solution)/shard_map/ppermute | solution.py:338
  9.0 4.3 %collective-permute-start.1 = (bf16[2,128,128]{2,1,0:T(8,128)(2,1)S(1)}, bf16[2,128,128]{2,1,0:T(8,128)(2,1)S(1)}, u32[]{:S(2)}, u32[]{:S(2)}) collective-permute-start(bf16[2,128,128]{2,1,0:T(8,128)(2,1)S(1)} %add_convert_fusion.3), channel_id=1, source_target_pairs={{0,8},{4,12},{8,16},{12,20},{16,24},{20,28},{24,0},{28,4},{32,40},... | collective-permute-start | bytes 196616 | tf_op jit(solution)/shard_map/ppermute | solution.py:338
  13.4 7.0 %collective-permute-start.5 = (bf16[2,128,128]{2,1,0:T(8,128)(2,1)S(1)}, bf16[2,128,128]{2,1,0:T(8,128)(2,1)S(1)}, u32[]{:S(2)}, u32[]{:S(2)}) collective-permute-start(bf16[2,128,128]{2,1,0:T(8,128)(2,1)S(1)} %fusion.20), channel_id=1, source_target_pairs={{0,224},{4,228},{8,232},{12,236},{16,240},{20,244},{24,248},{28,25... | collective-permute-start | bytes 196616 | tf_op jit(solution)/shard_map/ppermute | solution.py:338
  19.1 4.3 %collective-permute-start.4 = (bf16[2,128,128]{2,1,0:T(8,128)(2,1)S(1)}, bf16[2,128,128]{2,1,0:T(8,128)(2,1)S(1)}, u32[]{:S(2)}, u32[]{:S(2)}) collective-permute-start(bf16[2,128,128]{2,1,0:T(8,128)(2,1)S(1)} %fusion.20), channel_id=1, source_target_pairs={{0,32},{4,36},{8,40},{12,44},{16,48},{20,52},{24,56},{28,60},{32,6... | collective-permute-start | bytes 196616 | tf_op jit(solution)/shard_map/ppermute | solution.py:338
  23.5 6.4 %collective-permute-start.6 = (bf16[2,128,128]{2,1,0:T(8,128)(2,1)S(1)}, bf16[2,128,128]{2,1,0:T(8,128)(2,1)S(1)}, u32[]{:S(2)}, u32[]{:S(2)}) collective-permute-start(bf16[2,128,128]{2,1,0:T(8,128)(2,1)S(1)} %get-tuple-element.96), channel_id=1, source_target_pairs={{0,96},{4,100},{8,104},{12,108},{16,112},{20,116},{24,120},{28,124... | collective-permute-start | bytes 196616 | tf_op jit(solution)/shard_map/ppermute | solution.py:338
  23.6 6.3 %collective-permute-start.7 = (bf16[2,128,128]{2,1,0:T(8,128)(2,1)S(1)}, bf16[2,128,128]{2,1,0:T(8,128)(2,1)S(1)}, u32[]{:S(2)}, u32[]{:S(2)}) collective-permute-start(bf16[2,128,128]{2,1,0:T(8,128)(2,1)S(1)} %get-tuple-element.97), channel_id=1, source_target_pairs={{0,160},{4,164},{8,168},{12,172},{16,176},{20,180},{24,184},{28,18... | collective-permute-start | bytes 196616 | tf_op jit(solution)/shard_map/ppermute | solution.py:338
  30.1 8.1 %collective-permute-start.8 = (bf16[2,128,128]{2,1,0:T(8,128)(2,1)S(1)}, bf16[2,128,128]{2,1,0:T(8,128)(2,1)S(1)}, u32[]{:S(2)}, u32[]{:S(2)}) collective-permute-start(bf16[2,128,128]{2,1,0:T(8,128)(2,1)S(1)} %broadcast_select_fusion.4), channel_id=1, source_target_pairs={{0,4},{4,0},{8,12},{12,8},{16,20},{20,16},{24,28},{28,24},{32,36},... | collective-permute-start | bytes 196616 | tf_op jit(solution)/shard_map/ppermute | solution.py:338
  37.1 1.2 %copy-start.3 = (bf16[1024,512]{1,0:T(8,128)(2,1)S(1)}, bf16[1024,512]{1,0:T(8,128)(2,1)}, u32[]{:S(2)}) copy-start(bf16[1024,512]{1,0:T(8,128)(2,1)} %y_ref.1) | copy-start | bytes 3145732
  37.1 1.2 %copy-start.4 = (f32[512]{0:T(512)S(1)}, f32[512]{0:T(512)}, u32[]{:S(2)}) copy-start(f32[512]{0:T(512)} %param.9) | copy-start | bytes 6148
  39.2 4.6 %collective-permute-start.11 = (f32[2,1024]{1,0:T(2,128)S(1)}, f32[2,1024]{1,0:T(2,128)S(1)}, u32[]{:S(2)}, u32[]{:S(2)}) collective-permute-start(f32[2,1024]{1,0:T(2,128)S(1)} %get-tuple-element.61.s0), channel_id=1, source_target_pairs={{0,2},{1,3},{2,0},{3,1},{4,6},{5,7},{6,4},{7,5},{8,10},{9,11},{10,... | collective-permute-start | bytes 24584 | tf_op jit(solution)/shard_map/ppermute | solution.py:372
  42.3 2.5 %collective-permute-start.10 = (f32[2,1024]{1,0:T(2,128)S(1)}, f32[2,1024]{1,0:T(2,128)S(1)}, u32[]{:S(2)}, u32[]{:S(2)}) collective-permute-start(f32[2,1024]{1,0:T(2,128)S(1)} %get-tuple-element.61.s0), channel_id=1, source_target_pairs={{0,3},{1,0},{2,1},{3,2},{4,7},{5,4},{6,5},{7,6},{8,11},{9,8},{10,9... | collective-permute-start | bytes 24584 | tf_op jit(solution)/shard_map/ppermute | solution.py:372
  43.1 3.7 %collective-permute-start.9 = (f32[2,1024]{1,0:T(2,128)S(1)}, f32[2,1024]{1,0:T(2,128)S(1)}, u32[]{:S(2)}, u32[]{:S(2)}) collective-permute-start(f32[2,1024]{1,0:T(2,128)S(1)} %get-tuple-element.61.s0), channel_id=1, source_target_pairs={{0,1},{1,2},{2,3},{3,0},{4,5},{5,6},{6,7},{7,4},{8,9},{9,10},{10,1... | collective-permute-start | bytes 24584 | tf_op jit(solution)/shard_map/ppermute | solution.py:372
  48.6 2.7 %collective-permute-start.12 = (bf16[2,128,128]{2,1,0:T(8,128)(2,1)S(1)}, bf16[2,128,128]{2,1,0:T(8,128)(2,1)S(1)}, u32[]{:S(2)}, u32[]{:S(2)}) collective-permute-start(bf16[2,128,128]{2,1,0:T(8,128)(2,1)S(1)} %broadcast_select_fusion.2), channel_id=1, source_target_pairs={{252,248},{248,252},{244,240},{240,244},{236,232},{232,236},{228,2... | collective-permute-start | bytes 196616 | tf_op jit(solution)/shard_map/ppermute | solution.py:338
  51.3 7.1 %collective-permute-start.15 = (bf16[2,128,128]{2,1,0:T(8,128)(2,1)S(1)}, bf16[2,128,128]{2,1,0:T(8,128)(2,1)S(1)}, u32[]{:S(2)}, u32[]{:S(2)}) collective-permute-start(bf16[2,128,128]{2,1,0:T(8,128)(2,1)S(1)} %add_convert_fusion.1), channel_id=1, source_target_pairs={{252,236},{248,232},{244,228},{240,224},{236,252},{232,248},{228,2... | collective-permute-start | bytes 196616 | tf_op jit(solution)/shard_map/ppermute | solution.py:338
  52.1 6.3 %collective-permute-start.14 = (bf16[2,128,128]{2,1,0:T(8,128)(2,1)S(1)}, bf16[2,128,128]{2,1,0:T(8,128)(2,1)S(1)}, u32[]{:S(2)}, u32[]{:S(2)}) collective-permute-start(bf16[2,128,128]{2,1,0:T(8,128)(2,1)S(1)} %add_convert_fusion.1), channel_id=1, source_target_pairs={{252,228},{248,224},{244,252},{240,248},{236,244},{232,240},{228,2... | collective-permute-start | bytes 196616 | tf_op jit(solution)/shard_map/ppermute | solution.py:338
  52.5 5.9 %collective-permute-start.13 = (bf16[2,128,128]{2,1,0:T(8,128)(2,1)S(1)}, bf16[2,128,128]{2,1,0:T(8,128)(2,1)S(1)}, u32[]{:S(2)}, u32[]{:S(2)}) collective-permute-start(bf16[2,128,128]{2,1,0:T(8,128)(2,1)S(1)} %add_convert_fusion.1), channel_id=1, source_target_pairs={{252,244},{248,240},{244,236},{240,232},{236,228},{232,224},{228,2... | collective-permute-start | bytes 196616 | tf_op jit(solution)/shard_map/ppermute | solution.py:338
  58.5 6.4 %collective-permute-start.17 = (bf16[2,128,128]{2,1,0:T(8,128)(2,1)S(1)}, bf16[2,128,128]{2,1,0:T(8,128)(2,1)S(1)}, u32[]{:S(2)}, u32[]{:S(2)}) collective-permute-start(bf16[2,128,128]{2,1,0:T(8,128)(2,1)S(1)} %fusion.21), channel_id=1, source_target_pairs={{252,28},{248,24},{244,20},{240,16},{236,12},{232,8},{228,4},{224,... | collective-permute-start | bytes 196616 | tf_op jit(solution)/shard_map/ppermute | solution.py:338
  60.2 4.7 %collective-permute-start.16 = (bf16[2,128,128]{2,1,0:T(8,128)(2,1)S(1)}, bf16[2,128,128]{2,1,0:T(8,128)(2,1)S(1)}, u32[]{:S(2)}, u32[]{:S(2)}) collective-permute-start(bf16[2,128,128]{2,1,0:T(8,128)(2,1)S(1)} %fusion.21), channel_id=1, source_target_pairs={{252,220},{248,216},{244,212},{240,208},{236,204},{232,200},{228,1... | collective-permute-start | bytes 196616 | tf_op jit(solution)/shard_map/ppermute | solution.py:338
  65.0 7.0 %collective-permute-start.18 = (bf16[2,128,128]{2,1,0:T(8,128)(2,1)S(1)}, bf16[2,128,128]{2,1,0:T(8,128)(2,1)S(1)}, u32[]{:S(2)}, u32[]{:S(2)}) collective-permute-start(bf16[2,128,128]{2,1,0:T(8,128)(2,1)S(1)} %get-tuple-element.94), channel_id=1, source_target_pairs={{252,156},{248,152},{244,148},{240,144},{236,140},{232,136},{228,1... | collective-permute-start | bytes 196616 | tf_op jit(solution)/shard_map/ppermute | solution.py:338
  68.3 7.6 %collective-permute-start.19 = (bf16[2,128,128]{2,1,0:T(8,128)(2,1)S(1)}, bf16[2,128,128]{2,1,0:T(8,128)(2,1)S(1)}, u32[]{:S(2)}, u32[]{:S(2)}) collective-permute-start(bf16[2,128,128]{2,1,0:T(8,128)(2,1)S(1)} %get-tuple-element.95), channel_id=1, source_target_pairs={{252,92},{248,88},{244,84},{240,80},{236,76},{232,72},{228,68},{22... | collective-permute-start | bytes 196616 | tf_op jit(solution)/shard_map/ppermute | solution.py:338
  76.1 5.4 %collective-permute-start.20 = (bf16[2,128,128]{2,1,0:T(8,128)(2,1)S(1)}, bf16[2,128,128]{2,1,0:T(8,128)(2,1)S(1)}, u32[]{:S(2)}, u32[]{:S(2)}) collective-permute-start(bf16[2,128,128]{2,1,0:T(8,128)(2,1)S(1)} %broadcast_select_fusion), channel_id=1, source_target_pairs={{252,248},{248,252},{244,240},{240,244},{236,232},{232,236},{228,2... | collective-permute-start | bytes 196616 | tf_op jit(solution)/shard_map/ppermute | solution.py:338

commit v4 on v3

--- a/solution.py
+++ b/solution.py
@@ -117,6 +117,30 @@
         cost_estimate=cost(2 * 2 * t * t * HEAD_DIM * 5 // 8, t * HEAD_DIM * 10),
         name="local_attn",
     )(q, k, v)
+
+
+def turned_kernel(head, q_ref, k_ref, w_ref):
+    t = q_ref.shape[0]
+    cols = slice(head * HEAD_DIM, (head + 1) * HEAD_DIM)
+    for r in range(0, t, ROWS):
+        e = r + ROWS
+        k = k_ref[r:e, cols]
+        w_ref[r:e, r:e] = masked(nt(k, q_ref[r:e, cols]), True)
+        if e < t:
+            w_ref[r:e, e:] = nt(k, q_ref[e:, cols]).astype(bf16)
+
+
+def turned_weights(q, k, head):
+    t = q.shape[0]
+    return pl.pallas_call(
+        functools.partial(turned_kernel, head),
+        in_specs=[VMEM] * 2,
+        out_specs=VMEM,
+        out_shape=jax.ShapeDtypeStruct((t, t), bf16),
+        compiler_params=params(8),
+        cost_estimate=cost(2 * t * t * HEAD_DIM * 5 // 8, t * t),
+        name="turned_weights",
+    )(q, k)
 
 
 def column(row):
@@ -210,58 +234,84 @@
     )(attn, y, q, *stats, gain)
 
 
-def back_kernel(head, q_ref, k_ref, v_ref, d_ref, p_ref, *refs):
-    dq_hbm, dk_ref, dv_ref, dq_ref, sems = refs[-5:]
-    t = q_ref.shape[0]
+def query_kernel(head, k_ref, v_ref, d_ref, p_ref, dq_ref):
+    t = k_ref.shape[0]
     cols = slice(head * HEAD_DIM, (head + 1) * HEAD_DIM)
-    copies = []
-    for i in range(t // ROWS):
-        r, e = i * ROWS, (i + 1) * ROWS
-        here = slice(r, e)
-        q, k, v, d = q_ref[here, cols], k_ref[here, cols], v_ref[here, cols], d_ref[here, cols]
-        dq = nt(d, p_ref[head]) + nn(masked(nt(d, v)), k)
+    for r in range(0, t, ROWS):
+        here = slice(r, r + ROWS)
+        d = d_ref[here, cols]
+        dq = nt(d, p_ref[head]) + nn(masked(nt(d, v_ref[here, cols])), k_ref[here, cols])
         if r:
             dq = dq + nn(nt(d, v_ref[:r, cols]).astype(bf16), k_ref[:r, cols])
         dq_ref[here, :] = dq.astype(bf16)
-        there = pl.ds(r, ROWS)
-        copies.append(
-            pltpu.make_async_copy(
-                dq_ref.at[there], dq_hbm.at[there, pl.ds(head * HEAD_DIM, HEAD_DIM)], sems.at[i]
-            )
-        )
-        copies[-1].start()
-        dk = nn(masked(nt(v, d), True), q)
-        dv = nn(masked(nt(k, q), True), d)
+
+
+def grad_query(k, v, d, prefix, head):
+    t = k.shape[0]
+    return pl.pallas_call(
+        functools.partial(query_kernel, head),
+        in_specs=[VMEM] * 4,
+        out_specs=VMEM,
+        out_shape=jax.ShapeDtypeStruct((t, HEAD_DIM), bf16),
+        compiler_params=params(8),
+        cost_estimate=cost(2 * 2 * t * t * HEAD_DIM * 5 // 8, t * HEAD_DIM * 10),
+        name="grad_query",
+    )(k, v, d, prefix)
+
+
+def back_kernel(head, q_ref, v_ref, d_ref, w_ref, dk_ref, dv_ref):
+    t = q_ref.shape[0]
+    cols = slice(head * HEAD_DIM, (head + 1) * HEAD_DIM)
+    for r in range(0, t, ROWS):
+        e = r + ROWS
+        here = slice(r, e)
+        v = v_ref[here, cols]
+        dk = nn(masked(nt(v, d_ref[here, cols]), True), q_ref[here, cols])
         if e < t:
             dk = dk + nn(nt(v, d_ref[e:, cols]).astype(bf16), q_ref[e:, cols])
-            dv = dv + nn(nt(k, q_ref[e:, cols]).astype(bf16), d_ref[e:, cols])
         dk_ref[here, :] = dk
-        dv_ref[here, :] = dv
+        dv_ref[here, :] = nn(w_ref[here, r:], d_ref[r:, cols])
+
+
+def local_back(q, v, d, turned, head):
+    t = q.shape[0]
+    return pl.pallas_call(
+        functools.partial(back_kernel, head),
+        in_specs=[VMEM] * 4,
+        out_specs=(VMEM, VMEM),
+        out_shape=(jax.ShapeDtypeStruct((t, HEAD_DIM), f32),) * 2,
+        compiler_params=params(8),
+        cost_estimate=cost(3 * 2 * t * t * HEAD_DIM * 5 // 8, t * HEAD_DIM * 14),
+        name="local_back",
+    )(q, v, d, turned)
+
+
+def write_kernel(*refs):
+    n = len(refs) - 2
+    parts, out, sems = refs[:n], refs[n], refs[n + 1]
+    copies = [
+        pltpu.make_async_copy(part, out.at[:, pl.ds(i * HEAD_DIM, HEAD_DIM)], sems.at[i])
+        for i, part in enumerate(parts)
+    ]
+    for copy in copies:
+        copy.start()
     for copy in copies:
         copy.wait()
 
 
-def local_back(q, k, v, d, prefix, dq, head):
-    t, c = q.shape
-    held = [] if dq is None else [dq]
-    return pl.pallas_call(
-        functools.partial(back_kernel, head),
-        in_specs=[VMEM] * 5 + [ANY] * len(held),
-        out_specs=(ANY, VMEM, VMEM),
-        input_output_aliases={5: 0} if held else {},
-        out_shape=(
-            jax.ShapeDtypeStruct((t, c), bf16),
-            jax.ShapeDtypeStruct((t, HEAD_DIM), f32),
-            jax.ShapeDtypeStruct((t, HEAD_DIM), f32),
-        ),
-        scratch_shapes=[
-            pltpu.VMEM((t, HEAD_DIM), bf16),
-            pltpu.SemaphoreType.DMA((t // ROWS,)),
-        ],
-        compiler_params=params(8),
-        cost_estimate=cost(6 * 2 * t * t * HEAD_DIM * 5 // 8, t * HEAD_DIM * 18),
-        name="local_back",
-    )(q, k, v, d, prefix, *held)
+def side_by_side(parts):
+    t = parts[0].shape[0]
+    n = len(parts)
+    return pl.pallas_call(
+        write_kernel,
+        in_specs=[VMEM] * n,
+        out_specs=ANY,
+        out_shape=jax.ShapeDtypeStruct((t, n * HEAD_DIM), bf16),
+        scratch_shapes=[pltpu.SemaphoreType.DMA((n,))],
+        compiler_params=params(8),
+        cost_estimate=cost(0, 4 * t * n * HEAD_DIM),
+        name="side_by_side",
+    )(*parts)
 
 
 def final_kernel(*refs):
@@ -382,17 +432,20 @@
     first, last, k, v = lax.optimization_barrier((first, last, k, v))
     in_hbm = [pltpu.with_memory_space_constraint(a, pltpu.HBM) for a in (k, v)]
     prefix = exclusive_sum(block_state(*in_hbm), False, first)
-    locals_ = []
+    locals_, turned = [], []
     for i in range(PARTS):
         locals_.append(local_attn(q, k, v, i))
+        turned.append(turned_weights(q, k, i))
     attn, stats = attn_stats(locals_, q, prefix, y, gain)
     mixed, d, term = grads_of_norm(attn, y, q, head_parts(stats), gain)
     suffix = exclusive_sum(term, True, last)
-    dq, dks, dvs = None, [], []
+    dqs, dks, dvs = [], [], []
     for i in range(PARTS):
-        dq, dk, dv = local_back(q, k, v, d, prefix, dq, i)
+        dqs.append(grad_query(k, v, d, prefix, i))
+        dk, dv = local_back(q, v, d, turned[i], i)
         dks.append(dk)
         dvs.append(dv)
+    dq = side_by_side(dqs)
     dk, dv = finish(dks, dvs, k, v, suffix)
     return mixed, dq, dk, dv
 

time: 83.5 us -> 82 us (0.982)
  starting transfers between devices: 38.7 us -> 37.4 us
    pallas_call x4 -> x13, Pallas kernels: 14.5 us -> 14.1 us  [the longest x4 5.72 us: local_back(): pl.pallas_call(functools.partial(back_kernel, head), in_specs=[VMEM] * 4,...]
  transfers between devices with their start and end apart: 21 -> 21, of which waited for: 11 -> 12; matrix products, arithmetic and copies ran while one was open for 0% -> 0% of each run, Pallas kernels for 22% -> 22%
where the time goes in v4:
time: 82 us; the launch traced here: 81.9 us
  starting transfers between devices  37.4 us (46%)
  Pallas kernels  24.6 us (30%)
  waiting for transfers between devices  17.9 us (22%)
  between operations  1.19 us (1%)
    ppermute x18, starting transfers between devices, send(): return lax.ppermute(a, 'seq', step_pairs(reverse, **step))  33.3 us
    ppermute x18, waiting for transfers between devices, send(): return lax.ppermute(a, 'seq', step_pairs(reverse, **step))  14.9 us
    pallas_call x4, Pallas kernels, local_back(): pl.pallas_call(functools.partial(back_kernel, head), in_specs=[VMEM] * 4,...  5.72 us
    pallas_call x4, Pallas kernels, grad_query(): pl.pallas_call(functools.partial(query_kernel, head), in_specs=[VMEM] * 4...  5.36 us
    pallas_call x4, Pallas kernels, local_attn(): pl.pallas_call(functools.partial(local_kernel, head), in_specs=[VMEM] * 3...  4.22 us
    ppermute x3, starting transfers between devices, head_parts(): lax.ppermute(a, 'head', [(i, (i + k) % 4) for i in range(4)])  4.02 us
    ppermute x3, waiting for transfers between devices, head_parts(): lax.ppermute(a, 'head', [(i, (i + k) % 4) for i in range(4)])  3.05 us
    pallas_call x1, Pallas kernels, block_state(): pl.pallas_call(outer_kernel, in_specs=[ANY, ANY], out_specs=VMEM, out_sha...  2.07 us
  transfers between devices with their start and end apart: 21, of which 12 were waited for; matrix products, arithmetic and copies ran while one was open for 0% of the time, Pallas kernels for 22%

profile of v4, /device:TPU:1, one launch (start us, length us, event | category | flops | bytes accessed | tf_op | source)
XLA Modules:
  0.0 81.9 jit_solution(9659931295564189672)
XLA Ops:
  0.7 2.1 %block_state.1 = bf16[4,128,128]{2,1,0:T(8,128)(2,1)S(1)} custom-call(bf16[1024,512]{1,0:T(8,128)(2,1)} %refs_8_, bf16[1024,512]{1,0:T(8,128)(2,1)} %refs_9_), custom_call_target="tpu_custom_call" | custom-call | flops 268435456 | bytes 2097152 | tf_op jit(solution)/shard_map/block_state/pallas_call | solution.py:74
  2.8 3.3 %collective-permute-start = (bf16[2,128,128]{2,1,0:T(8,128)(2,1)S(1)}, bf16[2,128,128]{2,1,0:T(8,128)(2,1)S(1)}, u32[]{:S(2)}, u32[]{:S(2)}) collective-permute-start(bf16[2,128,128]{2,1,0:T(8,128)(2,1)S(1)} %broadcast_select_fusion.6), channel_id=1, source_target_pairs={{0,4},{4,0},{8,12},{12,8},{16,20},{20,16},{24,28},{28,24},{32,36},... | collective-permute-start | bytes 196616 | tf_op jit(solution)/shard_map/ppermute | solution.py:388
  6.1 0.9 %collective-permute-done = bf16[2,128,128]{2,1,0:T(8,128)(2,1)S(1)} collective-permute-done((bf16[2,128,128]{2,1,0:T(8,128)(2,1)S(1)}, bf16[2,128,128]{2,1,0:T(8,128)(2,1)S(1)}, u32[]{:S(2)}, u32[]{:S(2)}) %collective-permute-start) | collective-permute-done | bytes 65568 | tf_op jit(solution)/shard_map/ppermute | solution.py:388
  7.1 2.7 %collective-permute-start.2 = (bf16[2,128,128]{2,1,0:T(8,128)(2,1)S(1)}, bf16[2,128,128]{2,1,0:T(8,128)(2,1)S(1)}, u32[]{:S(2)}, u32[]{:S(2)}) collective-permute-start(bf16[2,128,128]{2,1,0:T(8,128)(2,1)S(1)} %add_convert_fusion.3), channel_id=1, source_target_pairs={{0,24},{4,28},{8,0},{12,4},{16,8},{20,12},{24,16},{28,20},{32,56},... | collective-permute-start | bytes 196616 | tf_op jit(solution)/shard_map/ppermute | solution.py:388
  9.8 1.6 %collective-permute-done.1 = bf16[2,128,128]{2,1,0:T(8,128)(2,1)S(1)} collective-permute-done((bf16[2,128,128]{2,1,0:T(8,128)(2,1)S(1)}, bf16[2,128,128]{2,1,0:T(8,128)(2,1)S(1)}, u32[]{:S(2)}, u32[]{:S(2)}) %collective-permute-start.1) | collective-permute-done | bytes 65568 | tf_op jit(solution)/shard_map/ppermute | solution.py:388
  11.5 0.4 collective-permute-done.2
  11.9 2.5 %collective-permute-done.3 = bf16[2,128,128]{2,1,0:T(8,128)(2,1)S(1)} collective-permute-done((bf16[2,128,128]{2,1,0:T(8,128)(2,1)S(1)}, bf16[2,128,128]{2,1,0:T(8,128)(2,1)S(1)}, u32[]{:S(2)}, u32[]{:S(2)}) %collective-permute-start.3) | collective-permute-done | bytes 65568 | tf_op jit(solution)/shard_map/ppermute | solution.py:388
  14.6 3.9 %collective-permute-start.5 = (bf16[2,128,128]{2,1,0:T(8,128)(2,1)S(1)}, bf16[2,128,128]{2,1,0:T(8,128)(2,1)S(1)}, u32[]{:S(2)}, u32[]{:S(2)}) collective-permute-start(bf16[2,128,128]{2,1,0:T(8,128)(2,1)S(1)} %fusion.20), channel_id=1, source_target_pairs={{0,224},{4,228},{8,232},{12,236},{16,240},{20,244},{24,248},{28,25... | collective-permute-start | bytes 196616 | tf_op jit(solution)/shard_map/ppermute | solution.py:388
  18.5 1.6 %collective-permute-done.4 = bf16[2,128,128]{2,1,0:T(8,128)(2,1)S(1)} collective-permute-done((bf16[2,128,128]{2,1,0:T(8,128)(2,1)S(1)}, bf16[2,128,128]{2,1,0:T(8,128)(2,1)S(1)}, u32[]{:S(2)}, u32[]{:S(2)}) %collective-permute-start.4) | collective-permute-done | bytes 65568 | tf_op jit(solution)/shard_map/ppermute | solution.py:388
  20.2 4.4 %collective-permute-start.6 = (bf16[2,128,128]{2,1,0:T(8,128)(2,1)S(1)}, bf16[2,128,128]{2,1,0:T(8,128)(2,1)S(1)}, u32[]{:S(2)}, u32[]{:S(2)}) collective-permute-start(bf16[2,128,128]{2,1,0:T(8,128)(2,1)S(1)} %get-tuple-element.88), channel_id=1, source_target_pairs={{0,96},{4,100},{8,104},{12,108},{16,112},{20,116},{24,120},{28,124... | collective-permute-start | bytes 196616 | tf_op jit(solution)/shard_map/ppermute | solution.py:388
  24.7 1.1 %local_attn.5.refs_1_ = f32[1024,128]{1,0:T(8,128)S(1)} custom-call(bf16[1024,512]{1,0:T(8,128)(2,1)S(1)} %copy-done.2, bf16[1024,512]{1,0:T(8,128)(2,1)S(1)} %copy-done, bf16[1024,512]{1,0:T(8,128)(2,1)S(1)} %copy-done.1), custom_call_target="tpu_custom_call" | custom-call | flops 335544320 | bytes 1310720 | tf_op jit(solution)/shard_map/local_attn/pallas_call | solution.py:111
  25.8 0.7 collective-permute-done.6
  26.5 3.3 %collective-permute-done.7 = bf16[2,128,128]{2,1,0:T(8,128)(2,1)S(1)} collective-permute-done((bf16[2,128,128]{2,1,0:T(8,128)(2,1)S(1)}, bf16[2,128,128]{2,1,0:T(8,128)(2,1)S(1)}, u32[]{:S(2)}, u32[]{:S(2)}) %collective-permute-start.7) | collective-permute-done | bytes 65568 | tf_op jit(solution)/shard_map/ppermute | solution.py:388
  29.9 4.7 %collective-permute-start.8 = (bf16[2,128,128]{2,1,0:T(8,128)(2,1)S(1)}, bf16[2,128,128]{2,1,0:T(8,128)(2,1)S(1)}, u32[]{:S(2)}, u32[]{:S(2)}) collective-permute-start(bf16[2,128,128]{2,1,0:T(8,128)(2,1)S(1)} %broadcast_select_fusion.4), channel_id=1, source_target_pairs={{0,4},{4,0},{8,12},{12,8},{16,20},{20,16},{24,28},{28,24},{32,36},... | collective-permute-start | bytes 196616 | tf_op jit(solution)/shard_map/ppermute | solution.py:388
  34.6 1.1 %local_attn.6.refs_2_ = f32[1024,128]{1,0:T(8,128)S(1)} custom-call(bf16[1024,512]{1,0:T(8,128)(2,1)S(1)} %copy-done.2, bf16[1024,512]{1,0:T(8,128)(2,1)S(1)} %copy-done, bf16[1024,512]{1,0:T(8,128)(2,1)S(1)} %copy-done.1), custom_call_target="tpu_custom_call" | custom-call | flops 335544320 | bytes 1310720 | tf_op jit(solution)/shard_map/local_attn/pallas_call | solution.py:111
  35.7 1.1 %local_attn.7.refs_3_ = f32[1024,128]{1,0:T(8,128)S(1)} custom-call(bf16[1024,512]{1,0:T(8,128)(2,1)S(1)} %copy-done.2, bf16[1024,512]{1,0:T(8,128)(2,1)S(1)} %copy-done, bf16[1024,512]{1,0:T(8,128)(2,1)S(1)} %copy-done.1), custom_call_target="tpu_custom_call" | custom-call | flops 335544320 | bytes 1310720 | tf_op jit(solution)/shard_map/local_attn/pallas_call | solution.py:111
  36.8 1.1 %local_attn.4.refs_0_ = f32[1024,128]{1,0:T(8,128)S(1)} custom-call(bf16[1024,512]{1,0:T(8,128)(2,1)S(1)} %copy-done.2, bf16[1024,512]{1,0:T(8,128)(2,1)S(1)} %copy-done, bf16[1024,512]{1,0:T(8,128)(2,1)S(1)} %copy-done.1), custom_call_target="tpu_custom_call" | custom-call | flops 335544320 | bytes 1310720 | tf_op jit(solution)/shard_map/local_attn/pallas_call | solution.py:111
  38.0 0.8 %attn_stats.1 = (f32[1024,512]{1,0:T(8,128)S(1)}, f32[2,1024]{1,0:T(2,128)S(1)}) custom-call(f32[1024,128]{1,0:T(8,128)S(1)} %local_attn.4.refs_0_, f32[1024,128]{1,0:T(8,128)S(1)} %local_attn.5.refs_1_, f32[1024,128]{1,0:T(8,128)S(1)} %local_attn.6.refs_2_, f32[1024,128]{1,0:T(8,128)S(1)} %local_attn.7.refs_3_, bf16[1024,512]{1,0:T(8,128)(2,1)S(1)} %copy-done.2, ...), custom_call_target="tpu_custom_call" | custom-call | flops 134217728 | bytes 6291456 | tf_op jit(solution)/shard_map/attn_stats/pallas_call | solution.py:172
  38.8 3.0 %collective-permute-start.10 = (f32[2,1024]{1,0:T(2,128)S(1)}, f32[2,1024]{1,0:T(2,128)S(1)}, u32[]{:S(2)}, u32[]{:S(2)}) collective-permute-start(f32[2,1024]{1,0:T(2,128)S(1)} %get-tuple-element.57.s0), channel_id=1, source_target_pairs={{0,3},{1,0},{2,1},{3,2},{4,7},{5,4},{6,5},{7,6},{8,11},{9,8},{10,9... | collective-permute-start | bytes 24584 | tf_op jit(solution)/shard_map/ppermute | solution.py:422
  41.8 0.4 collective-permute-start.11
  42.2 0.7 collective-permute-start.9
  42.8 3.0 %collective-permute-done.11.s3 = f32[2,1024]{1,0:T(2,128)S(1)} collective-permute-done((f32[2,1024]{1,0:T(2,128)S(1)}, f32[2,1024]{1,0:T(2,128)S(1)}, u32[]{:S(2)}, u32[]{:S(2)}) %collective-permute-start.11) | collective-permute-done | bytes 8224 | tf_op jit(solution)/shard_map/ppermute | solution.py:422
  45.9 1.7 %grads_of_norm.1 = (bf16[1024,512]{1,0:T(8,128)(2,1)}, bf16[1024,512]{1,0:T(8,128)(2,1)S(1)}, bf16[4,128,128]{2,1,0:T(8,128)(2,1)S(1)}) custom-call(f32[1024,512]{1,0:T(8,128)S(1)} %get-tuple-element.56.attn_ref, bf16[1024,512]{1,0:T(8,128)(2,1)S(1)} %copy-done.3, bf16[1024,512]{1,0:T(8,128)(2,1)S(1)} %copy-done.2, f32[2,1024]{1,0:T(2,128)S(1)} %get-tuple-element.57.s0, ...), custom_call_target="tpu_custom_call" | custom-call | flops 268435456 | bytes 6291456 | tf_op jit(solution)/shard_map/grads_of_norm/pallas_call | solution.py:221
  47.6 1.8 %collective-permute-start.12 = (bf16[2,128,128]{2,1,0:T(8,128)(2,1)S(1)}, bf16[2,128,128]{2,1,0:T(8,128)(2,1)S(1)}, u32[]{:S(2)}, u32[]{:S(2)}) collective-permute-start(bf16[2,128,128]{2,1,0:T(8,128)(2,1)S(1)} %broadcast_select_fusion.2), channel_id=1, source_target_pairs={{252,248},{248,252},{244,240},{240,244},{236,232},{232,236},{228,2... | collective-permute-start | bytes 196616 | tf_op jit(solution)/shard_map/ppermute | solution.py:388
  49.4 0.5 turned_weights.4.w_ref
  49.9 0.5 turned_weights.5.w_ref
  50.4 0.5 turned_weights.6.w_ref
  50.9 0.5 turned_weights.7.w_ref
  51.5 1.3 %collective-permute-start.13 = (bf16[2,128,128]{2,1,0:T(8,128)(2,1)S(1)}, bf16[2,128,128]{2,1,0:T(8,128)(2,1)S(1)}, u32[]{:S(2)}, u32[]{:S(2)}) collective-permute-start(bf16[2,128,128]{2,1,0:T(8,128)(2,1)S(1)} %add_convert_fusion.1), channel_id=1, source_target_pairs={{252,244},{248,240},{244,236},{240,232},{236,228},{232,224},{228,2... | collective-permute-start | bytes 196616 | tf_op jit(solution)/shard_map/ppermute | solution.py:388
  53.0 1.5 %collective-permute-start.15 = (bf16[2,128,128]{2,1,0:T(8,128)(2,1)S(1)}, bf16[2,128,128]{2,1,0:T(8,128)(2,1)S(1)}, u32[]{:S(2)}, u32[]{:S(2)}) collective-permute-start(bf16[2,128,128]{2,1,0:T(8,128)(2,1)S(1)} %add_convert_fusion.1), channel_id=1, source_target_pairs={{252,236},{248,232},{244,228},{240,224},{236,252},{232,248},{228,2... | collective-permute-start | bytes 196616 | tf_op jit(solution)/shard_map/ppermute | solution.py:388
  54.5 1.3 %grad_query.7.refs_3_ = bf16[1024,128]{1,0:T(8,128)(2,1)S(1)} custom-call(bf16[1024,512]{1,0:T(8,128)(2,1)S(1)} %copy-done, bf16[1024,512]{1,0:T(8,128)(2,1)S(1)} %copy-done.1, bf16[1024,512]{1,0:T(8,128)(2,1)S(1)} %get-tuple-element.59.d_ref, bf16[4,128,128]{2,1,0:T(8,128)(2,1)S(1)} %maximum_select_fusion.refs_5_.p_ref), custom_call_target="tpu_custom_call" | custom-call | flops 335544320 | bytes 1310720 | tf_op jit(solution)/shard_map/grad_query/pallas_call | solution.py:251
  55.9 1.4 %local_back.4 = (f32[1024,128]{1,0:T(8,128)S(1)}, f32[1024,128]{1,0:T(8,128)S(1)}) custom-call(bf16[1024,512]{1,0:T(8,128)(2,1)S(1)} %copy-done.2, bf16[1024,512]{1,0:T(8,128)(2,1)S(1)} %copy-done.1, bf16[1024,512]{1,0:T(8,128)(2,1)S(1)} %get-tuple-element.59.d_ref, bf16[1024,1024]{1,0:T(8,128)(2,1)S(1)} %turned_weights.4.w_ref), custom_call_target="tpu_custom_call" | custom-call | flops 503316480 | bytes 1835008 | tf_op jit(solution)/shard_map/local_back/pallas_call | solution.py:278
  57.3 0.9 %collective-permute-done.14 = bf16[2,128,128]{2,1,0:T(8,128)(2,1)S(1)} collective-permute-done((bf16[2,128,128]{2,1,0:T(8,128)(2,1)S(1)}, bf16[2,128,128]{2,1,0:T(8,128)(2,1)S(1)}, u32[]{:S(2)}, u32[]{:S(2)}) %collective-permute-start.14) | collective-permute-done | bytes 65568 | tf_op jit(solution)/shard_map/ppermute | solution.py:388
  58.3 1.2 %collective-permute-start.16 = (bf16[2,128,128]{2,1,0:T(8,128)(2,1)S(1)}, bf16[2,128,128]{2,1,0:T(8,128)(2,1)S(1)}, u32[]{:S(2)}, u32[]{:S(2)}) collective-permute-start(bf16[2,128,128]{2,1,0:T(8,128)(2,1)S(1)} %fusion.21), channel_id=1, source_target_pairs={{252,220},{248,216},{244,212},{240,208},{236,204},{232,200},{228,1... | collective-permute-start | bytes 196616 | tf_op jit(solution)/shard_map/ppermute | solution.py:388
  59.5 0.3 collective-permute-start.17
  59.8 1.3 %grad_query.6.refs_2_ = bf16[1024,128]{1,0:T(8,128)(2,1)S(1)} custom-call(bf16[1024,512]{1,0:T(8,128)(2,1)S(1)} %copy-done, bf16[1024,512]{1,0:T(8,128)(2,1)S(1)} %copy-done.1, bf16[1024,512]{1,0:T(8,128)(2,1)S(1)} %get-tuple-element.59.d_ref, bf16[4,128,128]{2,1,0:T(8,128)(2,1)S(1)} %maximum_select_fusion.refs_5_.p_ref), custom_call_target="tpu_custom_call" | custom-call | flops 335544320 | bytes 1310720 | tf_op jit(solution)/shard_map/grad_query/pallas_call | solution.py:251
  61.2 1.4 %local_back.5 = (f32[1024,128]{1,0:T(8,128)S(1)}, f32[1024,128]{1,0:T(8,128)S(1)}) custom-call(bf16[1024,512]{1,0:T(8,128)(2,1)S(1)} %copy-done.2, bf16[1024,512]{1,0:T(8,128)(2,1)S(1)} %copy-done.1, bf16[1024,512]{1,0:T(8,128)(2,1)S(1)} %get-tuple-element.59.d_ref, bf16[1024,1024]{1,0:T(8,128)(2,1)S(1)} %turned_weights.5.w_ref), custom_call_target="tpu_custom_call" | custom-call | flops 503316480 | bytes 1835008 | tf_op jit(solution)/shard_map/local_back/pallas_call | solution.py:278
  62.6 1.2 %collective-permute-done.17 = bf16[2,128,128]{2,1,0:T(8,128)(2,1)S(1)} collective-permute-done((bf16[2,128,128]{2,1,0:T(8,128)(2,1)S(1)}, bf16[2,128,128]{2,1,0:T(8,128)(2,1)S(1)}, u32[]{:S(2)}, u32[]{:S(2)}) %collective-permute-start.17) | collective-permute-done | bytes 65568 | tf_op jit(solution)/shard_map/ppermute | solution.py:388
  63.9 1.7 %collective-permute-start.18 = (bf16[2,128,128]{2,1,0:T(8,128)(2,1)S(1)}, bf16[2,128,128]{2,1,0:T(8,128)(2,1)S(1)}, u32[]{:S(2)}, u32[]{:S(2)}) collective-permute-start(bf16[2,128,128]{2,1,0:T(8,128)(2,1)S(1)} %get-tuple-element.86), channel_id=1, source_target_pairs={{252,156},{248,152},{244,148},{240,144},{236,140},{232,136},{228,1... | collective-permute-start | bytes 196616 | tf_op jit(solution)/shard_map/ppermute | solution.py:388
  65.7 1.6 %collective-permute-start.19 = (bf16[2,128,128]{2,1,0:T(8,128)(2,1)S(1)}, bf16[2,128,128]{2,1,0:T(8,128)(2,1)S(1)}, u32[]{:S(2)}, u32[]{:S(2)}) collective-permute-start(bf16[2,128,128]{2,1,0:T(8,128)(2,1)S(1)} %get-tuple-element.87), channel_id=1, source_target_pairs={{252,92},{248,88},{244,84},{240,80},{236,76},{232,72},{228,68},{22... | collective-permute-start | bytes 196616 | tf_op jit(solution)/shard_map/ppermute | solution.py:388
  67.3 1.3 %grad_query.5.refs_1_ = bf16[1024,128]{1,0:T(8,128)(2,1)S(1)} custom-call(bf16[1024,512]{1,0:T(8,128)(2,1)S(1)} %copy-done, bf16[1024,512]{1,0:T(8,128)(2,1)S(1)} %copy-done.1, bf16[1024,512]{1,0:T(8,128)(2,1)S(1)} %get-tuple-element.59.d_ref, bf16[4,128,128]{2,1,0:T(8,128)(2,1)S(1)} %maximum_select_fusion.refs_5_.p_ref), custom_call_target="tpu_custom_call" | custom-call | flops 335544320 | bytes 1310720 | tf_op jit(solution)/shard_map/grad_query/pallas_call | solution.py:251
  68.6 1.4 %local_back.6 = (f32[1024,128]{1,0:T(8,128)S(1)}, f32[1024,128]{1,0:T(8,128)S(1)}) custom-call(bf16[1024,512]{1,0:T(8,128)(2,1)S(1)} %copy-done.2, bf16[1024,512]{1,0:T(8,128)(2,1)S(1)} %copy-done.1, bf16[1024,512]{1,0:T(8,128)(2,1)S(1)} %get-tuple-element.59.d_ref, bf16[1024,1024]{1,0:T(8,128)(2,1)S(1)} %turned_weights.6.w_ref), custom_call_target="tpu_custom_call" | custom-call | flops 503316480 | bytes 1835008 | tf_op jit(solution)/shard_map/local_back/pallas_call | solution.py:278
  70.1 1.7 %collective-permute-done.19 = bf16[2,128,128]{2,1,0:T(8,128)(2,1)S(1)} collective-permute-done((bf16[2,128,128]{2,1,0:T(8,128)(2,1)S(1)}, bf16[2,128,128]{2,1,0:T(8,128)(2,1)S(1)}, u32[]{:S(2)}, u32[]{:S(2)}) %collective-permute-start.19) | collective-permute-done | bytes 65568 | tf_op jit(solution)/shard_map/ppermute | solution.py:388
  72.0 4.3 %collective-permute-start.20 = (bf16[2,128,128]{2,1,0:T(8,128)(2,1)S(1)}, bf16[2,128,128]{2,1,0:T(8,128)(2,1)S(1)}, u32[]{:S(2)}, u32[]{:S(2)}) collective-permute-start(bf16[2,128,128]{2,1,0:T(8,128)(2,1)S(1)} %broadcast_select_fusion), channel_id=1, source_target_pairs={{252,248},{248,252},{244,240},{240,244},{236,232},{232,236},{228,2... | collective-permute-start | bytes 196616 | tf_op jit(solution)/shard_map/ppermute | solution.py:388
  76.2 1.3 %grad_query.4.refs_0_ = bf16[1024,128]{1,0:T(8,128)(2,1)S(1)} custom-call(bf16[1024,512]{1,0:T(8,128)(2,1)S(1)} %copy-done, bf16[1024,512]{1,0:T(8,128)(2,1)S(1)} %copy-done.1, bf16[1024,512]{1,0:T(8,128)(2,1)S(1)} %get-tuple-element.59.d_ref, bf16[4,128,128]{2,1,0:T(8,128)(2,1)S(1)} %maximum_select_fusion.refs_5_.p_ref), custom_call_target="tpu_custom_call" | custom-call | flops 335544320 | bytes 1310720 | tf_op jit(solution)/shard_map/grad_query/pallas_call | solution.py:251
  77.6 1.0 %side_by_side.1 = bf16[1024,512]{1,0:T(8,128)(2,1)} custom-call(bf16[1024,128]{1,0:T(8,128)(2,1)S(1)} %grad_query.4.refs_0_, bf16[1024,128]{1,0:T(8,128)(2,1)S(1)} %grad_query.5.refs_1_, bf16[1024,128]{1,0:T(8,128)(2,1)S(1)} %grad_query.6.refs_2_, bf16[1024,128]{1,0:T(8,128)(2,1)S(1)} %grad_query.7.refs_3_), custom_call_target="tpu_custom_call" | custom-call | bytes 2097152 | tf_op jit(solution)/shard_map/side_by_side/pallas_call | solution.py:305
  78.6 1.4 %local_back.7 = (f32[1024,128]{1,0:T(8,128)S(1)}, f32[1024,128]{1,0:T(8,128)S(1)}) custom-call(bf16[1024,512]{1,0:T(8,128)(2,1)S(1)} %copy-done.2, bf16[1024,512]{1,0:T(8,128)(2,1)S(1)} %copy-done.1, bf16[1024,512]{1,0:T(8,128)(2,1)S(1)} %get-tuple-element.59.d_ref, bf16[1024,1024]{1,0:T(8,128)(2,1)S(1)} %turned_weights.7.w_ref), custom_call_target="tpu_custom_call" | custom-call | flops 503316480 | bytes 1835008 | tf_op jit(solution)/shard_map/local_back/pallas_call | solution.py:278
  80.0 1.7 %finish.1 = (bf16[1024,512]{1,0:T(8,128)(2,1)}, bf16[1024,512]{1,0:T(8,128)(2,1)}) custom-call(f32[1024,128]{1,0:T(8,128)S(1)} %get-tuple-element.60.refs_0_, f32[1024,128]{1,0:T(8,128)S(1)} %get-tuple-element.61.refs_1_, f32[1024,128]{1,0:T(8,128)S(1)} %get-tuple-element.62.refs_2_, f32[1024,128]{1,0:T(8,128)S(1)} %get-tuple-element.63.refs_3_, ...), custom_call_target="tpu_custom_call" | custom-call | flops 268435456 | bytes 8388608 | tf_op jit(solution)/shard_map/finish/pallas_call | solution.py:342
  (39 shorter events, 1.5 us)
Async XLA Ops:
  0.6 24.1 %copy-start = (bf16[1024,512]{1,0:T(8,128)(2,1)S(1)}, bf16[1024,512]{1,0:T(8,128)(2,1)}, u32[]{:S(2)}) copy-start(bf16[1024,512]{1,0:T(8,128)(2,1)} %refs_8_) | copy-start | bytes 3145732
  0.6 24.1 %copy-start.1 = (bf16[1024,512]{1,0:T(8,128)(2,1)S(1)}, bf16[1024,512]{1,0:T(8,128)(2,1)}, u32[]{:S(2)}) copy-start(bf16[1024,512]{1,0:T(8,128)(2,1)} %refs_9_) | copy-start | bytes 3145732
  0.7 24.1 %copy-start.2 = (bf16[1024,512]{1,0:T(8,128)(2,1)S(1)}, bf16[1024,512]{1,0:T(8,128)(2,1)}, u32[]{:S(2)}) copy-start(bf16[1024,512]{1,0:T(8,128)(2,1)} %q_ref.25) | copy-start | bytes 3145732
  2.8 4.2 %collective-permute-start = (bf16[2,128,128]{2,1,0:T(8,128)(2,1)S(1)}, bf16[2,128,128]{2,1,0:T(8,128)(2,1)S(1)}, u32[]{:S(2)}, u32[]{:S(2)}) collective-permute-start(bf16[2,128,128]{2,1,0:T(8,128)(2,1)S(1)} %broadcast_select_fusion.6), channel_id=1, source_target_pairs={{0,4},{4,0},{8,12},{12,8},{16,20},{20,16},{24,28},{28,24},{32,36},... | collective-permute-start | bytes 196616 | tf_op jit(solution)/shard_map/ppermute | solution.py:388
  7.0 4.4 %collective-permute-start.1 = (bf16[2,128,128]{2,1,0:T(8,128)(2,1)S(1)}, bf16[2,128,128]{2,1,0:T(8,128)(2,1)S(1)}, u32[]{:S(2)}, u32[]{:S(2)}) collective-permute-start(bf16[2,128,128]{2,1,0:T(8,128)(2,1)S(1)} %add_convert_fusion.3), channel_id=1, source_target_pairs={{0,8},{4,12},{8,16},{12,20},{16,24},{20,28},{24,0},{28,4},{32,40},... | collective-permute-start | bytes 196616 | tf_op jit(solution)/shard_map/ppermute | solution.py:388
  7.1 4.7 %collective-permute-start.2 = (bf16[2,128,128]{2,1,0:T(8,128)(2,1)S(1)}, bf16[2,128,128]{2,1,0:T(8,128)(2,1)S(1)}, u32[]{:S(2)}, u32[]{:S(2)}) collective-permute-start(bf16[2,128,128]{2,1,0:T(8,128)(2,1)S(1)} %add_convert_fusion.3), channel_id=1, source_target_pairs={{0,24},{4,28},{8,0},{12,4},{16,8},{20,12},{24,16},{28,20},{32,56},... | collective-permute-start | bytes 196616 | tf_op jit(solution)/shard_map/ppermute | solution.py:388
  9.8 4.6 %collective-permute-start.3 = (bf16[2,128,128]{2,1,0:T(8,128)(2,1)S(1)}, bf16[2,128,128]{2,1,0:T(8,128)(2,1)S(1)}, u32[]{:S(2)}, u32[]{:S(2)}) collective-permute-start(bf16[2,128,128]{2,1,0:T(8,128)(2,1)S(1)} %add_convert_fusion.3), channel_id=1, source_target_pairs={{0,16},{4,20},{8,24},{12,28},{16,0},{20,4},{24,8},{28,12},{32,48},... | collective-permute-start | bytes 196616 | tf_op jit(solution)/shard_map/ppermute | solution.py:388
  14.5 5.6 %collective-permute-start.4 = (bf16[2,128,128]{2,1,0:T(8,128)(2,1)S(1)}, bf16[2,128,128]{2,1,0:T(8,128)(2,1)S(1)}, u32[]{:S(2)}, u32[]{:S(2)}) collective-permute-start(bf16[2,128,128]{2,1,0:T(8,128)(2,1)S(1)} %fusion.20), channel_id=1, source_target_pairs={{0,32},{4,36},{8,40},{12,44},{16,48},{20,52},{24,56},{28,60},{32,6... | collective-permute-start | bytes 196616 | tf_op jit(solution)/shard_map/ppermute | solution.py:388
  14.6 5.5 %collective-permute-start.5 = (bf16[2,128,128]{2,1,0:T(8,128)(2,1)S(1)}, bf16[2,128,128]{2,1,0:T(8,128)(2,1)S(1)}, u32[]{:S(2)}, u32[]{:S(2)}) collective-permute-start(bf16[2,128,128]{2,1,0:T(8,128)(2,1)S(1)} %fusion.20), channel_id=1, source_target_pairs={{0,224},{4,228},{8,232},{12,236},{16,240},{20,244},{24,248},{28,25... | collective-permute-start | bytes 196616 | tf_op jit(solution)/shard_map/ppermute | solution.py:388
  20.2 6.3 %collective-permute-start.6 = (bf16[2,128,128]{2,1,0:T(8,128)(2,1)S(1)}, bf16[2,128,128]{2,1,0:T(8,128)(2,1)S(1)}, u32[]{:S(2)}, u32[]{:S(2)}) collective-permute-start(bf16[2,128,128]{2,1,0:T(8,128)(2,1)S(1)} %get-tuple-element.88), channel_id=1, source_target_pairs={{0,96},{4,100},{8,104},{12,108},{16,112},{20,116},{24,120},{28,124... | collective-permute-start | bytes 196616 | tf_op jit(solution)/shard_map/ppermute | solution.py:388
  24.5 5.2 %collective-permute-start.7 = (bf16[2,128,128]{2,1,0:T(8,128)(2,1)S(1)}, bf16[2,128,128]{2,1,0:T(8,128)(2,1)S(1)}, u32[]{:S(2)}, u32[]{:S(2)}) collective-permute-start(bf16[2,128,128]{2,1,0:T(8,128)(2,1)S(1)} %get-tuple-element.89), channel_id=1, source_target_pairs={{0,160},{4,164},{8,168},{12,172},{16,176},{20,180},{24,184},{28,18... | collective-permute-start | bytes 196616 | tf_op jit(solution)/shard_map/ppermute | solution.py:388
  29.9 7.9 %collective-permute-start.8 = (bf16[2,128,128]{2,1,0:T(8,128)(2,1)S(1)}, bf16[2,128,128]{2,1,0:T(8,128)(2,1)S(1)}, u32[]{:S(2)}, u32[]{:S(2)}) collective-permute-start(bf16[2,128,128]{2,1,0:T(8,128)(2,1)S(1)} %broadcast_select_fusion.4), channel_id=1, source_target_pairs={{0,4},{4,0},{8,12},{12,8},{16,20},{20,16},{24,28},{28,24},{32,36},... | collective-permute-start | bytes 196616 | tf_op jit(solution)/shard_map/ppermute | solution.py:388
  36.7 1.2 %copy-start.3 = (bf16[1024,512]{1,0:T(8,128)(2,1)S(1)}, bf16[1024,512]{1,0:T(8,128)(2,1)}, u32[]{:S(2)}) copy-start(bf16[1024,512]{1,0:T(8,128)(2,1)} %y_ref.1) | copy-start | bytes 3145732
  36.8 1.2 %copy-start.4 = (f32[512]{0:T(512)S(1)}, f32[512]{0:T(512)}, u32[]{:S(2)}) copy-start(f32[512]{0:T(512)} %param.9) | copy-start | bytes 6148
  38.8 4.0 %collective-permute-start.10 = (f32[2,1024]{1,0:T(2,128)S(1)}, f32[2,1024]{1,0:T(2,128)S(1)}, u32[]{:S(2)}, u32[]{:S(2)}) collective-permute-start(f32[2,1024]{1,0:T(2,128)S(1)} %get-tuple-element.57.s0), channel_id=1, source_target_pairs={{0,3},{1,0},{2,1},{3,2},{4,7},{5,4},{6,5},{7,6},{8,11},{9,8},{10,9... | collective-permute-start | bytes 24584 | tf_op jit(solution)/shard_map/ppermute | solution.py:422
  41.8 4.0 %collective-permute-start.11 = (f32[2,1024]{1,0:T(2,128)S(1)}, f32[2,1024]{1,0:T(2,128)S(1)}, u32[]{:S(2)}, u32[]{:S(2)}) collective-permute-start(f32[2,1024]{1,0:T(2,128)S(1)} %get-tuple-element.57.s0), channel_id=1, source_target_pairs={{0,2},{1,3},{2,0},{3,1},{4,6},{5,7},{6,4},{7,5},{8,10},{9,11},{10,... | collective-permute-start | bytes 24584 | tf_op jit(solution)/shard_map/ppermute | solution.py:422
  42.2 3.7 %collective-permute-start.9 = (f32[2,1024]{1,0:T(2,128)S(1)}, f32[2,1024]{1,0:T(2,128)S(1)}, u32[]{:S(2)}, u32[]{:S(2)}) collective-permute-start(f32[2,1024]{1,0:T(2,128)S(1)} %get-tuple-element.57.s0), channel_id=1, source_target_pairs={{0,1},{1,2},{2,3},{3,0},{4,5},{5,6},{6,7},{7,4},{8,9},{9,10},{10,1... | collective-permute-start | bytes 24584 | tf_op jit(solution)/shard_map/ppermute | solution.py:422
  47.6 3.8 %collective-permute-start.12 = (bf16[2,128,128]{2,1,0:T(8,128)(2,1)S(1)}, bf16[2,128,128]{2,1,0:T(8,128)(2,1)S(1)}, u32[]{:S(2)}, u32[]{:S(2)}) collective-permute-start(bf16[2,128,128]{2,1,0:T(8,128)(2,1)S(1)} %broadcast_select_fusion.2), channel_id=1, source_target_pairs={{252,248},{248,252},{244,240},{240,244},{236,232},{232,236},{228,2... | collective-permute-start | bytes 196616 | tf_op jit(solution)/shard_map/ppermute | solution.py:388
  51.5 5.9 %collective-permute-start.13 = (bf16[2,128,128]{2,1,0:T(8,128)(2,1)S(1)}, bf16[2,128,128]{2,1,0:T(8,128)(2,1)S(1)}, u32[]{:S(2)}, u32[]{:S(2)}) collective-permute-start(bf16[2,128,128]{2,1,0:T(8,128)(2,1)S(1)} %add_convert_fusion.1), channel_id=1, source_target_pairs={{252,244},{248,240},{244,236},{240,232},{236,228},{232,224},{228,2... | collective-permute-start | bytes 196616 | tf_op jit(solution)/shard_map/ppermute | solution.py:388
  52.8 5.4 %collective-permute-start.14 = (bf16[2,128,128]{2,1,0:T(8,128)(2,1)S(1)}, bf16[2,128,128]{2,1,0:T(8,128)(2,1)S(1)}, u32[]{:S(2)}, u32[]{:S(2)}) collective-permute-start(bf16[2,128,128]{2,1,0:T(8,128)(2,1)S(1)} %add_convert_fusion.1), channel_id=1, source_target_pairs={{252,228},{248,224},{244,252},{240,248},{236,244},{232,240},{228,2... | collective-permute-start | bytes 196616 | tf_op jit(solution)/shard_map/ppermute | solution.py:388
  53.0 5.2 %collective-permute-start.15 = (bf16[2,128,128]{2,1,0:T(8,128)(2,1)S(1)}, bf16[2,128,128]{2,1,0:T(8,128)(2,1)S(1)}, u32[]{:S(2)}, u32[]{:S(2)}) collective-permute-start(bf16[2,128,128]{2,1,0:T(8,128)(2,1)S(1)} %add_convert_fusion.1), channel_id=1, source_target_pairs={{252,236},{248,232},{244,228},{240,224},{236,252},{232,248},{228,2... | collective-permute-start | bytes 196616 | tf_op jit(solution)/shard_map/ppermute | solution.py:388
  58.3 4.3 %collective-permute-start.16 = (bf16[2,128,128]{2,1,0:T(8,128)(2,1)S(1)}, bf16[2,128,128]{2,1,0:T(8,128)(2,1)S(1)}, u32[]{:S(2)}, u32[]{:S(2)}) collective-permute-start(bf16[2,128,128]{2,1,0:T(8,128)(2,1)S(1)} %fusion.21), channel_id=1, source_target_pairs={{252,220},{248,216},{244,212},{240,208},{236,204},{232,200},{228,1... | collective-permute-start | bytes 196616 | tf_op jit(solution)/shard_map/ppermute | solution.py:388
  59.5 4.3 %collective-permute-start.17 = (bf16[2,128,128]{2,1,0:T(8,128)(2,1)S(1)}, bf16[2,128,128]{2,1,0:T(8,128)(2,1)S(1)}, u32[]{:S(2)}, u32[]{:S(2)}) collective-permute-start(bf16[2,128,128]{2,1,0:T(8,128)(2,1)S(1)} %fusion.21), channel_id=1, source_target_pairs={{252,28},{248,24},{244,20},{240,16},{236,12},{232,8},{228,4},{224,... | collective-permute-start | bytes 196616 | tf_op jit(solution)/shard_map/ppermute | solution.py:388
  63.9 6.1 %collective-permute-start.18 = (bf16[2,128,128]{2,1,0:T(8,128)(2,1)S(1)}, bf16[2,128,128]{2,1,0:T(8,128)(2,1)S(1)}, u32[]{:S(2)}, u32[]{:S(2)}) collective-permute-start(bf16[2,128,128]{2,1,0:T(8,128)(2,1)S(1)} %get-tuple-element.86), channel_id=1, source_target_pairs={{252,156},{248,152},{244,148},{240,144},{236,140},{232,136},{228,1... | collective-permute-start | bytes 196616 | tf_op jit(solution)/shard_map/ppermute | solution.py:388
  65.7 6.1 %collective-permute-start.19 = (bf16[2,128,128]{2,1,0:T(8,128)(2,1)S(1)}, bf16[2,128,128]{2,1,0:T(8,128)(2,1)S(1)}, u32[]{:S(2)}, u32[]{:S(2)}) collective-permute-start(bf16[2,128,128]{2,1,0:T(8,128)(2,1)S(1)} %get-tuple-element.87), channel_id=1, source_target_pairs={{252,92},{248,88},{244,84},{240,80},{236,76},{232,72},{228,68},{22... | collective-permute-start | bytes 196616 | tf_op jit(solution)/shard_map/ppermute | solution.py:388
  72.0 8.1 %collective-permute-start.20 = (bf16[2,128,128]{2,1,0:T(8,128)(2,1)S(1)}, bf16[2,128,128]{2,1,0:T(8,128)(2,1)S(1)}, u32[]{:S(2)}, u32[]{:S(2)}) collective-permute-start(bf16[2,128,128]{2,1,0:T(8,128)(2,1)S(1)} %broadcast_select_fusion), channel_id=1, source_target_pairs={{252,248},{248,252},{244,240},{240,244},{236,232},{232,236},{228,2... | collective-permute-start | bytes 196616 | tf_op jit(solution)/shard_map/ppermute | solution.py:388
